TPU v7x, 512 devices: a whole 4x4x16 slice. The times are simulated.
512 devices in a mesh: row: 16 (over x_hi, y, core), col: 32 (over z, x_lo).
Axes of the slice: x: 4 (x_hi: 2, x_lo: 2; x = x_hi * 2 + x_lo), y: 4, z: 16, core: 2. Of those that a mesh axis runs over, the one named last changes fastest.
Arguments:
- orbitals: bfloat16 [16384, 2048], P(('row', 'col')), may hold values from -0.125 to 0.125
- coulomb: bfloat16 [16384, 16384], P('row', 'col'), may hold values from -6 to 6
- applied: bfloat16 [16384, 256], P(('row', 'col')), may hold values from -6 to 6
Outputs:
- projectors: float32 [16384, 256], P(('row', 'col'))
All inputs are finite; a program needn't handle non-finite values.
Results may differ from a plain program's by a relative error of at most 0.0029.
Values may be sent and summed in bfloat16 or wider, within the bound.
No kernel may reach another device: no remote copies, remote signals or barrier semaphores. Data moves between devices by JAX's collectives and lax.ppermute only.
A program may use at most 64 MiB of HBM per device.

v0:
```python
import jax
import jax.numpy as jnp
from jax import lax
from jax.sharding import PartitionSpec as P

NMU = 16384


def per_device(orbitals, coulomb, applied):
    point_block = lax.all_gather(orbitals, "col", axis=0, tiled=True)
    paired_orbitals, paired_applied = (
        lax.all_gather(orbitals, "row", axis=0, tiled=True),
        lax.all_gather(applied, "row", axis=0, tiled=True),
    )
    density = jnp.einsum(
        "ik,jk->ij", point_block, paired_orbitals, preferred_element_type=jnp.float32
    )
    kernel = (coulomb.astype(jnp.float32) * density).astype(jnp.bfloat16)
    images = lax.psum_scatter(
        jnp.dot(kernel, paired_applied, preferred_element_type=jnp.float32),
        "col",
        scatter_dimension=0,
        tiled=True,
    )
    local_gram = jnp.einsum("ia,ib->ab", images, images, precision=lax.Precision.HIGHEST)
    gram_sum = lax.psum(local_gram, ("row", "col"))
    gram_matrix = jnp.eye(gram_sum.shape[0], dtype=jnp.float32) + gram_sum / NMU
    factor = jnp.linalg.cholesky(gram_matrix)
    projectors = lax.linalg.triangular_solve(
        factor, images, left_side=False, lower=True, transpose_a=True
    )
    return projectors


def solution(mesh):
    return jax.shard_map(
        per_device,
        mesh=mesh,
        in_specs=(P(("row", "col"), None), P("row", "col"), P(("row", "col"), None)),
        out_specs=P(("row", "col"), None),
        check_vma=False,
    )
```

profile of v0, /device:TPU:1, one launch (start us, length us, event | category | flops | bytes accessed | tf_op | source)
XLA Modules:
  0.0 898.1 jit_solution(3592845915459076260)
XLA Ops:
  6.5 0.7 all-gather.5.cloned.1.call-update
  7.3 0.0 all-gather.3.cloned.1.call-start
  7.3 0.7 all-gather.3.cloned.1.call-update
  8.0 0.0 reduce-scatter.2.cloned.1.call-start
  8.1 26.7 %all_gather.11 = bf16[512,256]{1,0:T(8,128)(2,1)S(1)} all-gather(bf16[32,256]{1,0:T(8,128)(2,1)} %param.5), channel_id=1, replica_groups=mesh['row'=16,'col'=32] {'row'}, dimensions={0}, use_global_device_ids=true | all-gather | bytes 278528 | tf_op jit(solution)/shard_map/all_gather | solution.py:13
  34.7 44.5 %all-gather.5.cloned.1.call-done = bf16[512,2048]{1,0:T(8,128)(2,1)} async-done(((bf16[32,2048]{1,0:T(8,128)(2,1)}), bf16[512,2048]{1,0:T(8,128)(2,1)}) %all-gather.5.cloned.1.call-update) | async-done | bytes 2097168 | tf_op jit(solution)/shard_map/all_gather | solution.py:12
  79.3 120.5 %all-gather.3.cloned.1.call-done = bf16[1024,2048]{1,0:T(8,128)(2,1)} async-done(((bf16[32,2048]{1,0:T(8,128)(2,1)}), bf16[1024,2048]{1,0:T(8,128)(2,1)}) %all-gather.3.cloned.1.call-update) | async-done | bytes 4194320 | tf_op jit(solution)/shard_map/all_gather | solution.py:10
  199.8 6.8 fusion
  206.6 0.2 all-reduce.3.cloned.1.call-start
  206.8 130.1 %reduce-scatter.2.cloned.1.call-done = f32[32,256]{1,0:T(8,128)} async-done(((f32[1024,256]{1,0:T(8,128)}), f32[32,256]{1,0:T(8,128)}) %reduce-scatter.2.cloned.1.call-update) | async-done | bytes 32784 | tf_op jit(solution)/shard_map/reduce_scatter | solution.py:19
  337.0 1.9 fusion.10
  338.9 489.5 %all-reduce.3.cloned.1.call-done = f32[256,256]{0,1:T(8,128)} async-done(((f32[256,256]{0,1:T(8,128)}), f32[256,256]{0,1:T(8,128)}) %all-reduce.3.cloned.1.call-update) | async-done | bytes 262160 | tf_op jit(solution)/shard_map/psum | solution.py:26
  828.4 1.0 multiply_add_fusion
  829.4 0.1 copy.5
  829.6 1.0 fusion.1
  830.6 11.7 %cholesky.50 = f32[128,128]{1,0:T(8,128)S(1)} custom-call(f32[128,128]{1,0:T(8,128)S(1)} %cholesky.118), custom_call_target="Cholesky" | custom-call | tf_op jit(solution)/shard_map/jit(cholesky)/cholesky | solution.py:28
  842.3 9.8 %custom-call.14 = f32[1,128,128]{1,2,0:T(8,128)S(1)} custom-call(f32[1,128,128]{2,1,0:T(8,128)S(1)} %get-tuple-element.26), custom_call_target="InvertDiagBlocksLowerTriangular" | custom-call | tf_op jit(solution)/shard_map/jit(cholesky)/cholesky | solution.py:28
  852.2 0.2 constant_dynamic-update-slice_fusion.1
  852.4 0.3 convolution_subtract_fusion
  852.7 11.7 %cholesky.105 = f32[128,128]{1,0:T(8,128)S(1)} custom-call(f32[128,128]{1,0:T(8,128)S(1)} %convolution_subtract_fusion), custom_call_target="Cholesky" | custom-call | tf_op jit(solution)/shard_map/jit(cholesky)/cholesky | solution.py:28
  864.4 0.7 compare_reduce_fusion
  866.4 0.1 triangular_solve.61
  866.5 4.2 while.1
  866.7 0.6 fusion.21
  867.3 1.4 bitcast_dynamic-update-slice_fusion.2
  868.7 0.6 fusion.21
  869.3 1.4 bitcast_dynamic-update-slice_fusion.2
  870.7 19.7 %custom-call.15 = f32[2,128,128]{1,2,0:T(8,128)S(1)} custom-call(f32[2,128,128]{2,1,0:T(8,128)S(1)} %get-tuple-element.12), custom_call_target="InvertDiagBlocksLowerTriangular" | custom-call | tf_op jit(solution)/shard_map/triangular_solve | solution.py:29
  890.4 0.2 fusion.4
  890.5 0.2 convolution_subtract_fusion.1
  890.7 0.2 fusion.2
  890.9 0.6 pad_maximum_fusion
  (14 shorter events, 0.2 us)
Async XLA Ops:
  6.5 72.7 %all-gather.5.cloned.1.call-start = ((), (), s32[]{:S(2)}) async-start(), calls=%async_computation.2 | async-start | bytes 2228224 | tf_op jit(solution)/shard_map/all_gather | solution.py:12
  7.3 192.5 %all-gather.3.cloned.1.call-start = ((), (), s32[]{:S(2)}) async-start(), calls=%async_computation.1 | async-start | bytes 4325376 | tf_op jit(solution)/shard_map/all_gather | solution.py:10
  8.0 328.9 %reduce-scatter.2.cloned.1.call-start = ((), (), s32[]{:S(2)}) async-start(), calls=%async_computation.3 | async-start | bytes 1081344 | tf_op jit(solution)/shard_map/reduce_scatter | solution.py:19
  206.6 621.8 %all-reduce.3.cloned.1.call-start = ((), (), s32[]{:S(2)}) async-start(), calls=%async_computation.4 | async-start | bytes 524288 | tf_op jit(solution)/shard_map/psum | solution.py:26
  829.4 60.9 %copy-start = (f32[32,256]{1,0:T(8,128)S(1)}, f32[32,256]{1,0:T(8,128)}, u32[]{:S(2)}) copy-start(f32[32,256]{1,0:T(8,128)} %reduce-scatter.2.cloned.1.call-done) | copy-start | bytes 98308
Sparse Core Ops, SparseCore 0:
  10.7 68.5 all-gather.4
  81.3 118.3 all-gather.2
  206.7 130.1 reduce-scatter.1
  342.2 486.1 all-reduce.2
where the time goes:
time: 899 us; the launch traced here: 898 us
  waiting for transfers between devices  786 us (87%)
  other arithmetic  56.3 us (6%)
  blocking collectives  26.7 us (3%)
  between operations  14.5 us (2%)
  matrix products  9.77 us (1%)
    psum x1, waiting for transfers between devices, per_device(): gram_sum = lax.psum(local_gram, ('row', 'col'))  489 us
    reduce_scatter x1, waiting for transfers between devices, per_device(): lax.psum_scatter(jnp.dot(kernel, paired_applied, preferred_element_type=j...  130 us
    all_gather x1, waiting for transfers between devices, per_device(): point_block = lax.all_gather(orbitals, 'col', axis=0, tiled=True)  121 us
    all_gather x1, waiting for transfers between devices, per_device(): lax.all_gather(orbitals, 'row', axis=0, tiled=True)  44.5 us
    another operation x6, other arithmetic, per_device(): factor = jnp.linalg.cholesky(gram_matrix)  34 us
    all_gather x1, blocking collectives, per_device(): lax.all_gather(applied, 'row', axis=0, tiled=True)  26.7 us
    another operation x4, other arithmetic, per_device(): lax.linalg.triangular_solve(factor, images, left_side=False, lower=True,...  20.3 us
  transfers between devices with their start and end apart: 4, of which 4 were waited for; matrix products, arithmetic and copies ran while one was open for 0% of the time, Pallas kernels for 0%

commit v1 on v0

--- a/solution.py
+++ b/solution.py
@@ -4,6 +4,22 @@
 from jax.sharding import PartitionSpec as P
 
 NMU = 16384
+BOTH = ("row", "col")
+
+
+def reduce_rows(partial):
+    n = lax.axis_size("col")
+    chunks = partial.astype(jnp.bfloat16).reshape(n, -1, partial.shape[1])
+    moved = lax.all_to_all(chunks, "col", 0, 0, tiled=True)
+    return jnp.sum(moved.astype(jnp.float32), axis=0)
+
+
+def sum_everywhere(x):
+    n = lax.axis_size("row") * lax.axis_size("col")
+    chunks = x.reshape(n, 1, -1)
+    share = jnp.sum(lax.all_to_all(chunks, BOTH, 0, 0, tiled=True), axis=0)
+    copies = jnp.broadcast_to(share[None], chunks.shape)
+    return lax.all_to_all(copies, BOTH, 0, 0, tiled=True).reshape(x.shape)
 
 
 def per_device(orbitals, coulomb, applied):
@@ -16,14 +32,11 @@
         "ik,jk->ij", point_block, paired_orbitals, preferred_element_type=jnp.float32
     )
     kernel = (coulomb.astype(jnp.float32) * density).astype(jnp.bfloat16)
-    images = lax.psum_scatter(
-        jnp.dot(kernel, paired_applied, preferred_element_type=jnp.float32),
-        "col",
-        scatter_dimension=0,
-        tiled=True,
+    images = reduce_rows(
+        jnp.dot(kernel, paired_applied, preferred_element_type=jnp.float32)
     )
     local_gram = jnp.einsum("ia,ib->ab", images, images, precision=lax.Precision.HIGHEST)
-    gram_sum = lax.psum(local_gram, ("row", "col"))
+    gram_sum = sum_everywhere(local_gram)
     gram_matrix = jnp.eye(gram_sum.shape[0], dtype=jnp.float32) + gram_sum / NMU
     factor = jnp.linalg.cholesky(gram_matrix)
     projectors = lax.linalg.triangular_solve(

time: 899 us -> 397 us (0.44)
  waiting for transfers between devices: 786 us -> 191 us
  blocking collectives: 26.7 us -> 113 us
  starting transfers between devices: 0.3 us -> 9.65 us
    psum x1 -> x0, waiting for transfers between devices: 489 us -> none  [per_device(): gram_sum = lax.psum(local_gram, ('row', 'col'))]
    reduce_scatter x1 -> x0, waiting for transfers between devices: 130 us -> none  [per_device(): lax.psum_scatter(jnp.dot(kernel, paired_applied, preferred_element_type=j...]
    all_to_all x0 -> x2, blocking collectives: none -> 86.4 us  [the longest x1 55.4 us: sum_everywhere(): share = jnp.sum(lax.all_to_all(chunks, BOTH, 0, 0, tiled=True), axis=0)]
    all_to_all x0 -> x1, waiting for transfers between devices: none -> 24.2 us  [sum_everywhere(): return lax.all_to_all(copies, BOTH, 0, 0, tiled=True).reshape(x.shape)]
    all_to_all x0 -> x1, starting transfers between devices: none -> 9.6 us  [sum_everywhere(): return lax.all_to_all(copies, BOTH, 0, 0, tiled=True).reshape(x.shape)]
  transfers between devices with their start and end apart: 4 -> 3, of which waited for: 4 -> 3; matrix products, arithmetic and copies ran while one was open for 0% -> 0% of each run, Pallas kernels for 0% -> 0%
where the time goes in v1:
time: 397 us
  waiting for transfers between devices  191 us (48%)
  blocking collectives  113 us (28%)
  other arithmetic  56 us (14%)
  between operations  14.8 us (4%)
  starting transfers between devices  9.65 us (2%)
  matrix products  7.25 us (2%)
  local copies, waits for them, and re-layouts  5.3 us (1%)
    all_gather x1, waiting for transfers between devices, per_device(): point_block = lax.all_gather(orbitals, 'col', axis=0, tiled=True)  121 us
    all_to_all x1, blocking collectives, sum_everywhere(): share = jnp.sum(lax.all_to_all(chunks, BOTH, 0, 0, tiled=True), axis=0)  55.4 us
    all_gather x1, waiting for transfers between devices, per_device(): lax.all_gather(orbitals, 'row', axis=0, tiled=True)  44.6 us
    another operation x6, other arithmetic, per_device(): factor = jnp.linalg.cholesky(gram_matrix)  34 us
    all_to_all x1, blocking collectives, reduce_rows(): moved = lax.all_to_all(chunks, 'col', 0, 0, tiled=True)  31 us
    all_gather x1, blocking collectives, per_device(): lax.all_gather(applied, 'row', axis=0, tiled=True)  26.7 us
    all_to_all x1, waiting for transfers between devices, sum_everywhere(): return lax.all_to_all(copies, BOTH, 0, 0, tiled=True).reshape(x.shape)  24.2 us
    another operation x4, other arithmetic, per_device(): lax.linalg.triangular_solve(factor, images, left_side=False, lower=True,...  20.6 us
  transfers between devices with their start and end apart: 3, of which 3 were waited for; matrix products, arithmetic and copies ran while one was open for 0% of the time, Pallas kernels for 0%

profile of v1, /device:TPU:1, one launch (start us, length us, event | category | flops | bytes accessed | tf_op | source)
XLA Modules:
  0.0 396.8 jit_solution(14576205465308880732)
XLA Ops:
  6.5 0.7 all-gather.5.cloned.1.call-update
  7.3 0.7 all-gather.3.cloned.1.call-update
  8.0 26.7 %all_gather.11 = bf16[512,256]{1,0:T(8,128)(2,1)S(1)} all-gather(bf16[32,256]{1,0:T(8,128)(2,1)} %param.5), channel_id=1, replica_groups=mesh['row'=16,'col'=32] {'row'}, dimensions={0}, use_global_device_ids=true | all-gather | bytes 278528 | tf_op jit(solution)/shard_map/all_gather | solution.py:29
  34.7 44.6 %all-gather.5.cloned.1.call-done = bf16[512,2048]{1,0:T(8,128)(2,1)} async-done(((bf16[32,2048]{1,0:T(8,128)(2,1)}), bf16[512,2048]{1,0:T(8,128)(2,1)}) %all-gather.5.cloned.1.call-update) | async-done | bytes 2097168 | tf_op jit(solution)/shard_map/all_gather | solution.py:28
  79.3 120.5 %all-gather.3.cloned.1.call-done = bf16[1024,2048]{1,0:T(8,128)(2,1)} async-done(((bf16[32,2048]{1,0:T(8,128)(2,1)}), bf16[1024,2048]{1,0:T(8,128)(2,1)}) %all-gather.3.cloned.1.call-update) | async-done | bytes 4194320 | tf_op jit(solution)/shard_map/all_gather | solution.py:26
  199.8 5.8 %convolution_convert_fusion = bf16[1024,256]{1,0:T(8,128)(2,1)S(1)} fusion(bf16[512,256]{1,0:T(8,128)(2,1)S(1)} %all_gather.11, bf16[1024,512]{1,0:T(8,128)(2,1)} %param.4, bf16[1024,2048]{1,0:T(8,128)(2,1)} %all-gather.3.cloned.1.call-done, bf16[512,2048]{1,0:T(8,128)(2,1)} %all-gather.5.cloned.1.call-done), kind=kOutput, calls=%fused_computation.3 | convolution fusion | flops 2417754112 | bytes 8126464 | tf_op jit(solution)/shard_map/dot_general | solution.py:36
  205.6 31.0 %all_to_all.15 = bf16[32,32,256]{2,1,0:T(8,128)(2,1)S(1)} all-to-all(bf16[32,32,256]{2,1,0:T(8,128)(2,1)S(1)} %bitcast.39), channel_id=1, replica_groups=mesh['row'=16,'col'=32] {'col'}, dimensions={0} | all-to-all | bytes 1048576 | tf_op jit(solution)/shard_map/all_to_all | solution.py:13
  236.7 0.4 fusion.9
  237.1 55.4 %all_to_all.16 = f32[512,1,128]{2,1,0:T(1,128)S(1)} all-to-all(f32[512,1,128]{2,1,0:T(1,128)S(1)} %bitcast.38), channel_id=1, replica_groups=mesh['row'=16,'col'=32] {'row','col'}, dimensions={0} | all-to-all | bytes 524288 | tf_op jit(solution)/shard_map/all_to_all | solution.py:20
  292.5 0.6 reduce_sum.19
  293.1 0.8 broadcast_in_dim.3
  293.9 9.6 %all-to-all-start.2 = ((f32[512,1,128]{2,1,0:T(1,128)}), f32[512,1,128]{2,1,0:T(1,128)S(1)}, u32[]{:S(2)}, u32[]{:S(2)}) async-start(f32[512,1,128]{2,1,0:T(1,128)} %broadcast_in_dim.3), calls=%async_computation.2 | async-start | bytes 524288 | tf_op jit(solution)/shard_map/all_to_all | solution.py:22
  303.5 24.2 %all-to-all-done.2 = f32[512,1,128]{2,1,0:T(1,128)S(1)} async-done(((f32[512,1,128]{2,1,0:T(1,128)}), f32[512,1,128]{2,1,0:T(1,128)S(1)}, u32[]{:S(2)}, u32[]{:S(2)}) %all-to-all-start.2) | async-done | bytes 262176 | tf_op jit(solution)/shard_map/all_to_all | solution.py:22
  327.7 0.7 multiply_reduce_fusion
  328.5 0.1 copy.8
  328.7 0.1 copy.9
  328.9 11.7 %cholesky.50 = f32[128,128]{1,0:T(8,128)S(1)} custom-call(f32[128,128]{1,0:T(8,128)S(1)} %cholesky.118), custom_call_target="Cholesky" | custom-call | tf_op jit(solution)/shard_map/jit(cholesky)/cholesky | solution.py:41
  340.7 9.8 %custom-call.14 = f32[1,128,128]{1,2,0:T(8,128)S(1)} custom-call(f32[1,128,128]{2,1,0:T(8,128)S(1)} %get-tuple-element.26), custom_call_target="InvertDiagBlocksLowerTriangular" | custom-call | tf_op jit(solution)/shard_map/jit(cholesky)/cholesky | solution.py:41
  350.5 0.2 constant_dynamic-update-slice_fusion.1
  350.7 0.3 convolution_subtract_fusion
  351.0 11.7 %cholesky.105 = f32[128,128]{1,0:T(8,128)S(1)} custom-call(f32[128,128]{1,0:T(8,128)S(1)} %convolution_subtract_fusion), custom_call_target="Cholesky" | custom-call | tf_op jit(solution)/shard_map/jit(cholesky)/cholesky | solution.py:41
  362.7 0.7 compare_reduce_fusion
  364.8 4.1 %while.1 = (s32[]{:T(128)}, f32[256,256]{1,0:T(8,128)S(1)}, s32[2,2]{1,0:T(2,128)S(1)}, f32[2,128,128]{2,1,0:T(8,128)S(1)}, s32[]{:T(128)}) while((s32[]{:T(128)}, f32[256,256]{1,0:T(8,128)S(1)}, s32[2,2]{1,0:T(2,128)S(1)}, f32[2,128,128]{2,1,0:T(8,128)S(1)}, s32[]{:T(128)}) %tuple.23), condition=%wide.while_cond, body=%wide.while_body.sunk | while | flops 2 | bytes 131181 | solution.py:42
  364.8 0.7 fusion.20
  365.5 1.3 bitcast_dynamic-update-slice_fusion.2
  366.9 0.7 fusion.20
  367.5 1.3 bitcast_dynamic-update-slice_fusion.2
  368.9 19.9 %custom-call.15 = f32[2,128,128]{1,2,0:T(8,128)S(1)} custom-call(f32[2,128,128]{2,1,0:T(8,128)S(1)} %get-tuple-element.12), custom_call_target="InvertDiagBlocksLowerTriangular" | custom-call | tf_op jit(solution)/shard_map/triangular_solve | solution.py:42
  388.8 0.2 fusion.3
  388.9 0.2 convolution_subtract_fusion.1
  389.1 0.2 fusion.1
  389.3 0.6 pad_maximum_fusion
  (17 shorter events, 0.5 us)
Async XLA Ops:
  6.5 72.7 %all-gather.5.cloned.1.call-start = ((), (), s32[]{:S(2)}) async-start(), calls=%async_computation.4 | async-start | bytes 2228224 | tf_op jit(solution)/shard_map/all_gather | solution.py:28
  7.3 192.5 %all-gather.3.cloned.1.call-start = ((), (), s32[]{:S(2)}) async-start(), calls=%async_computation.3 | async-start | bytes 4325376 | tf_op jit(solution)/shard_map/all_gather | solution.py:26
  293.9 33.8 %all-to-all-start.2 = ((f32[512,1,128]{2,1,0:T(1,128)}), f32[512,1,128]{2,1,0:T(1,128)S(1)}, u32[]{:S(2)}, u32[]{:S(2)}) async-start(f32[512,1,128]{2,1,0:T(1,128)} %broadcast_in_dim.3), calls=%async_computation.2 | async-start | bytes 524288 | tf_op jit(solution)/shard_map/all_to_all | solution.py:22
Sparse Core Ops, SparseCore 0:
  10.7 68.5 all-gather.4
  81.3 118.3 all-gather.2

commit v2 on v1

v2 whole, which is shorter than its diff:
```python
import jax
import jax.numpy as jnp
from jax import lax
from jax.sharding import Mesh
from jax.sharding import PartitionSpec as P

NMU = 16384
ROW = ("x_hi", "y", "core")
COL = ("z", "x_lo")
PLANE = ("x_hi", "y", "core", "x_lo")
AXES = ROW + COL
SIZES = (2, 4, 2, 16, 2)


def exchange(chunks, axes):
    return lax.all_to_all(chunks, axes, 0, 0, tiled=True)


def spread(x, axes):
    copies = jnp.broadcast_to(x[None], (lax.axis_size(axes),) + x.shape)
    return exchange(copies, axes)


def gather_col(orbitals):
    n = lax.axis_size("z")
    z = lax.axis_index("z")
    pair = spread(orbitals, "x_lo").reshape(-1, orbitals.shape[1])
    rows = pair.shape[0]
    block = jnp.zeros((n * rows, pair.shape[1]), pair.dtype)
    block = lax.dynamic_update_slice(block, pair, (z * rows, 0))
    up = [(i, (i + 1) % n) for i in range(n)]
    down = [(i, (i - 1) % n) for i in range(n)]
    ahead, behind = pair, pair
    for step in range(1, n // 2 + 1):
        ahead = lax.ppermute(ahead, "z", up)
        if step < n // 2:
            behind = lax.ppermute(behind, "z", down)
            block = lax.dynamic_update_slice(block, behind, (((z + step) & (n - 1)) * rows, 0))
        block = lax.dynamic_update_slice(block, ahead, (((z - step) & (n - 1)) * rows, 0))
    return block


def reduce_rows(partial):
    chunks = partial.astype(jnp.bfloat16).reshape(lax.axis_size(COL), -1, partial.shape[1])
    return jnp.sum(exchange(chunks, COL).astype(jnp.float32), axis=0)


def sum_everywhere(x):
    n = lax.axis_size(PLANE)
    share = jnp.sum(exchange(x.reshape(n, -1, x.shape[1]), PLANE), axis=0)
    share = jnp.sum(spread(share, "z"), axis=0)
    return spread(share, PLANE).reshape(x.shape)


def per_device(orbitals, coulomb, applied):
    width = orbitals.shape[1]
    paired = spread(jnp.concatenate([orbitals, applied], axis=1), ROW)
    paired = paired.reshape(-1, paired.shape[-1])
    paired_orbitals, paired_applied = paired[:, :width], paired[:, width:]
    point_block = gather_col(orbitals)
    density = jnp.einsum(
        "ik,jk->ij", point_block, paired_orbitals, preferred_element_type=jnp.float32
    )
    kernel = (coulomb.astype(jnp.float32) * density).astype(jnp.bfloat16)
    images = reduce_rows(
        jnp.dot(kernel, paired_applied, preferred_element_type=jnp.float32)
    )
    local_gram = jnp.einsum("ia,ib->ab", images, images, precision=lax.Precision.HIGHEST)
    gram_sum = sum_everywhere(local_gram)
    gram_matrix = jnp.eye(gram_sum.shape[0], dtype=jnp.float32) + gram_sum / NMU
    factor = jnp.linalg.cholesky(gram_matrix)
    projectors = lax.linalg.triangular_solve(
        factor, images, left_side=False, lower=True, transpose_a=True
    )
    return projectors


def solution(mesh):
    fine = Mesh(mesh.devices.reshape(SIZES), AXES)
    return jax.shard_map(
        per_device,
        mesh=fine,
        in_specs=(P(AXES, None), P(ROW, COL), P(AXES, None)),
        out_specs=P(AXES, None),
        check_vma=False,
    )
```

time: 397 us -> 259 us (0.65)
  waiting for transfers between devices: 191 us -> 22.7 us
  starting transfers between devices: 9.65 us -> 73.6 us
  blocking collectives: 113 us -> 76.2 us
  local copies, waits for them, and re-layouts: 5.3 us -> 21.5 us
  between operations: 14.8 us -> 1.54 us
    all_gather x2 -> x0, waiting for transfers between devices: 165 us -> none  [the longest x1 121 us: per_device(): point_block = lax.all_gather(orbitals, 'col', axis=0, tiled=True)]
    ppermute x0 -> x15, starting transfers between devices: none -> 57.5 us  [the longest x7 42.2 us: gather_col(): behind = lax.ppermute(behind, 'z', down)]
    all_gather x1 -> x0, blocking collectives: 26.7 us -> none  [per_device(): lax.all_gather(applied, 'row', axis=0, tiled=True)]
    all_to_all x1 -> x2, waiting for transfers between devices: 24.2 us -> 8.72 us  [exchange(): return lax.all_to_all(chunks, axes, 0, 0, tiled=True)]
    ppermute x0 -> x15, waiting for transfers between devices: none -> 13.9 us  [the longest x8 10.2 us: gather_col(): ahead = lax.ppermute(ahead, 'z', up)]
    dynamic_update_slice x0 -> x16, local copies, waits for them, and re-layouts: none -> 11.5 us  [the longest x8 5.75 us: gather_col(): lax.dynamic_update_slice(block, ahead, ((z - step & n - 1) * rows, 0))]
    all_to_all x2 -> x4, blocking collectives: 86.4 us -> 76.2 us  [exchange(): return lax.all_to_all(chunks, axes, 0, 0, tiled=True)]
    all_to_all x1 -> x2, starting transfers between devices: 9.6 us -> 16.1 us  [exchange(): return lax.all_to_all(chunks, axes, 0, 0, tiled=True)]
  transfers between devices with their start and end apart: 3 -> 17, of which waited for: 3 -> 6; matrix products, arithmetic and copies ran while one was open for 0% -> 6% of each run, Pallas kernels for 0% -> 0%
where the time goes in v2:
time: 259 us; the launch traced here: 258 us
  blocking collectives  76.2 us (29%)
  starting transfers between devices  73.6 us (28%)
  other arithmetic  55.7 us (22%)
  waiting for transfers between devices  22.7 us (9%)
  local copies, waits for them, and re-layouts  21.5 us (8%)
  matrix products  6.6 us (3%)
    all_to_all x4, blocking collectives, exchange(): return lax.all_to_all(chunks, axes, 0, 0, tiled=True)  76.2 us
    ppermute x7, starting transfers between devices, gather_col(): behind = lax.ppermute(behind, 'z', down)  42.2 us
    another operation x6, other arithmetic, per_device(): factor = jnp.linalg.cholesky(gram_matrix)  34 us
    another operation x4, other arithmetic, per_device(): lax.linalg.triangular_solve(factor, images, left_side=False, lower=True,...  20.6 us
    all_to_all x2, starting transfers between devices, exchange(): return lax.all_to_all(chunks, axes, 0, 0, tiled=True)  16.1 us
    ppermute x8, starting transfers between devices, gather_col(): ahead = lax.ppermute(ahead, 'z', up)  15.3 us
    ppermute x8, waiting for transfers between devices, gather_col(): ahead = lax.ppermute(ahead, 'z', up)  10.2 us
    all_to_all x2, waiting for transfers between devices, exchange(): return lax.all_to_all(chunks, axes, 0, 0, tiled=True)  8.72 us
  transfers between devices with their start and end apart: 17, of which 6 were waited for; matrix products, arithmetic and copies ran while one was open for 6% of the time, Pallas kernels for 0%

profile of v2, /device:TPU:1, one launch (start us, length us, event | category | flops | bytes accessed | tf_op | source)
XLA Modules:
  0.0 257.8 jit_solution(12818353619073291026)
XLA Ops:
  0.9 7.1 %all_to_all.30 = bf16[2,32,2048]{2,1,0:T(8,128)(2,1)S(1)} all-to-all(bf16[2,32,2048]{2,1,0:T(8,128)(2,1)S(1)} %broadcast_in_dim.12), channel_id=1, replica_groups=mesh['x_hi'=2,'y'=4,'core'=2,'z'=16,'x_lo'=2] {'x_lo'}, dimensions={0} | all-to-all | bytes 524288 | tf_op jit(solution)/shard_map/all_to_all | solution.py:16
  8.0 11.6 %collective-permute-start = (bf16[64,2048]{1,0:T(8,128)(2,1)S(1)}, bf16[64,2048]{1,0:T(8,128)(2,1)S(1)}, u32[]{:S(2)}, u32[]{:S(2)}) collective-permute-start(bf16[64,2048]{1,0:T(8,128)(2,1)S(1)} %bitcast.45), channel_id=1, source_target_pairs={{0,30},{2,0},{4,2},{6,4},{8,6},{10,8},{12,10},{14,12},{16,14},{18,... | collective-permute-start | bytes 786440 | tf_op jit(solution)/shard_map/ppermute | solution.py:37
  19.7 1.9 collective-permute-start.1
  24.2 8.9 %all-to-all-start.1 = ((bf16[16,32,2304]{2,1,0:T(8,128)(2,1)}), bf16[16,32,2304]{2,1,0:T(8,128)(2,1)S(1)}, u32[]{:S(2)}, u32[]{:S(2)}) async-start(bf16[16,32,2304]{2,1,0:T(8,128)(2,1)} %broadcast_in_dim.13), calls=%async_computation.1 | async-start | bytes 4718592 | tf_op jit(solution)/shard_map/all_to_all | solution.py:16
  33.1 2.5 broadcast_in_dim.11
  36.3 4.8 %collective-permute-start.2 = (bf16[64,2048]{1,0:T(8,128)(2,1)S(1)}, bf16[64,2048]{1,0:T(8,128)(2,1)S(1)}, u32[]{:S(2)}, u32[]{:S(2)}) collective-permute-start(bf16[64,2048]{1,0:T(8,128)(2,1)S(1)} %collective-permute-done), channel_id=1, source_target_pairs={{0,30},{2,0},{4,2},{6,4},{8,6},{10,8},{12,10},{14,12},{16,14},{18,... | collective-permute-start | bytes 786440 | tf_op jit(solution)/shard_map/ppermute | solution.py:37
  41.2 1.9 collective-permute-start.3
  44.5 2.1 collective-permute-done.2
  46.6 5.3 %collective-permute-start.4 = (bf16[64,2048]{1,0:T(8,128)(2,1)S(1)}, bf16[64,2048]{1,0:T(8,128)(2,1)S(1)}, u32[]{:S(2)}, u32[]{:S(2)}) collective-permute-start(bf16[64,2048]{1,0:T(8,128)(2,1)S(1)} %collective-permute-done.2), channel_id=1, source_target_pairs={{0,30},{2,0},{4,2},{6,4},{8,6},{10,8},{12,10},{14,12},{16,14},{18,... | collective-permute-start | bytes 786440 | tf_op jit(solution)/shard_map/ppermute | solution.py:37
  51.9 1.9 collective-permute-start.5
  56.5 5.3 %collective-permute-start.6 = (bf16[64,2048]{1,0:T(8,128)(2,1)S(1)}, bf16[64,2048]{1,0:T(8,128)(2,1)S(1)}, u32[]{:S(2)}, u32[]{:S(2)}) collective-permute-start(bf16[64,2048]{1,0:T(8,128)(2,1)S(1)} %collective-permute-done.4), channel_id=1, source_target_pairs={{0,30},{2,0},{4,2},{6,4},{8,6},{10,8},{12,10},{14,12},{16,14},{18,... | collective-permute-start | bytes 786440 | tf_op jit(solution)/shard_map/ppermute | solution.py:37
  61.9 1.9 collective-permute-start.7
  65.6 5.3 %collective-permute-start.8 = (bf16[64,2048]{1,0:T(8,128)(2,1)S(1)}, bf16[64,2048]{1,0:T(8,128)(2,1)S(1)}, u32[]{:S(2)}, u32[]{:S(2)}) collective-permute-start(bf16[64,2048]{1,0:T(8,128)(2,1)S(1)} %collective-permute-done.6), channel_id=1, source_target_pairs={{0,30},{2,0},{4,2},{6,4},{8,6},{10,8},{12,10},{14,12},{16,14},{18,... | collective-permute-start | bytes 786440 | tf_op jit(solution)/shard_map/ppermute | solution.py:37
  70.9 1.9 collective-permute-start.9
  74.3 4.9 %collective-permute-start.10 = (bf16[64,2048]{1,0:T(8,128)(2,1)S(1)}, bf16[64,2048]{1,0:T(8,128)(2,1)S(1)}, u32[]{:S(2)}, u32[]{:S(2)}) collective-permute-start(bf16[64,2048]{1,0:T(8,128)(2,1)S(1)} %collective-permute-done.8), channel_id=1, source_target_pairs={{0,30},{2,0},{4,2},{6,4},{8,6},{10,8},{12,10},{14,12},{16,14},{18,... | collective-permute-start | bytes 786440 | tf_op jit(solution)/shard_map/ppermute | solution.py:37
  79.3 1.9 collective-permute-start.11
  82.7 4.9 %collective-permute-start.12 = (bf16[64,2048]{1,0:T(8,128)(2,1)S(1)}, bf16[64,2048]{1,0:T(8,128)(2,1)S(1)}, u32[]{:S(2)}, u32[]{:S(2)}) collective-permute-start(bf16[64,2048]{1,0:T(8,128)(2,1)S(1)} %collective-permute-done.10), channel_id=1, source_target_pairs={{0,30},{2,0},{4,2},{6,4},{8,6},{10,8},{12,10},{14,12},{16,14},{18,... | collective-permute-start | bytes 786440 | tf_op jit(solution)/shard_map/ppermute | solution.py:37
  87.6 1.9 collective-permute-start.13
  90.9 5.0 %collective-permute-done.13 = bf16[64,2048]{1,0:T(8,128)(2,1)S(1)} collective-permute-done((bf16[64,2048]{1,0:T(8,128)(2,1)S(1)}, bf16[64,2048]{1,0:T(8,128)(2,1)S(1)}, u32[]{:S(2)}, u32[]{:S(2)}) %collective-permute-start.13) | collective-permute-done | bytes 262176 | tf_op jit(solution)/shard_map/ppermute | solution.py:35
  95.9 1.9 collective-permute-start.14
  99.3 5.2 %collective-permute-done.14 = bf16[64,2048]{1,0:T(8,128)(2,1)S(1)} collective-permute-done((bf16[64,2048]{1,0:T(8,128)(2,1)S(1)}, bf16[64,2048]{1,0:T(8,128)(2,1)S(1)}, u32[]{:S(2)}, u32[]{:S(2)}) %collective-permute-start.14) | collective-permute-done | bytes 262176 | tf_op jit(solution)/shard_map/ppermute | solution.py:35
  105.2 5.2 %convolution_convert_fusion = bf16[1024,256]{1,0:T(8,128)(2,1)S(1)} fusion(bf16[1024,512]{1,0:T(8,128)(2,1)} %param.4, bf16[1024,2048]{1,0:T(8,128)(2,1)} %constant_dynamic-update-slice_fusion.1, bf16[512,2304]{1,0:T(8,128)(2,1)S(1)} %bitcast.44), kind=kOutput, calls=%fused_computation.5 | convolution fusion | flops 2417754112 | bytes 8126464 | tf_op jit(solution)/shard_map/dot_general | solution.py:66
  110.5 29.3 %all_to_all.31 = bf16[32,32,256]{2,1,0:T(8,128)(2,1)S(1)} all-to-all(bf16[32,32,256]{2,1,0:T(8,128)(2,1)S(1)} %bitcast.48), channel_id=1, replica_groups=mesh['x_hi'=2,'y'=4,'core'=2,'z'=16,'x_lo'=2] {'z','x_lo'}, dimensions={0} | all-to-all | bytes 1048576 | tf_op jit(solution)/shard_map/all_to_all | solution.py:16
  140.3 25.2 %all_to_all.32 = f32[32,8,256]{2,1,0:T(8,128)S(1)} all-to-all(f32[32,8,256]{2,1,0:T(8,128)S(1)} %fusion.8), channel_id=1, replica_groups=mesh['x_hi'=2,'y'=4,'core'=2,'z'=16,'x_lo'=2] {'x_hi','y','core','x_lo'}, dimensions={0} | all-to-all | bytes 524288 | tf_op jit(solution)/shard_map/all_to_all | solution.py:16
  165.6 14.5 %all_to_all.33 = f32[16,8,256]{2,1,0:T(8,128)S(1)} all-to-all(f32[16,8,256]{2,1,0:T(8,128)S(1)} %broadcast_in_dim.14), channel_id=1, replica_groups=mesh['x_hi'=2,'y'=4,'core'=2,'z'=16,'x_lo'=2] {'z'}, dimensions={0} | all-to-all | bytes 262144 | tf_op jit(solution)/shard_map/all_to_all | solution.py:16
  180.9 7.2 %all-to-all-start.5 = ((f32[32,8,256]{2,1,0:T(8,128)}), f32[32,8,256]{2,1,0:T(8,128)S(1)}, u32[]{:S(2)}, u32[]{:S(2)}) async-start(f32[32,8,256]{2,1,0:T(8,128)} %broadcast_in_dim.15), calls=%async_computation.5 | async-start | bytes 524288 | tf_op jit(solution)/shard_map/all_to_all | solution.py:16
  188.1 8.7 %all-to-all-done.5 = f32[32,8,256]{2,1,0:T(8,128)S(1)} async-done(((f32[32,8,256]{2,1,0:T(8,128)}), f32[32,8,256]{2,1,0:T(8,128)S(1)}, u32[]{:S(2)}, u32[]{:S(2)}) %all-to-all-start.5) | async-done | bytes 262176 | tf_op jit(solution)/shard_map/all_to_all | solution.py:16
  197.2 11.7 %cholesky.50 = f32[128,128]{1,0:T(8,128)S(1)} custom-call(f32[128,128]{1,0:T(8,128)S(1)} %cholesky.118), custom_call_target="Cholesky" | custom-call | tf_op jit(solution)/shard_map/jit(cholesky)/cholesky | solution.py:71
  208.9 9.8 %custom-call.14 = f32[1,128,128]{1,2,0:T(8,128)S(1)} custom-call(f32[1,128,128]{2,1,0:T(8,128)S(1)} %get-tuple-element.26), custom_call_target="InvertDiagBlocksLowerTriangular" | custom-call | tf_op jit(solution)/shard_map/jit(cholesky)/cholesky | solution.py:71
  219.2 11.7 %cholesky.105 = f32[128,128]{1,0:T(8,128)S(1)} custom-call(f32[128,128]{1,0:T(8,128)S(1)} %convolution_subtract_fusion), custom_call_target="Cholesky" | custom-call | tf_op jit(solution)/shard_map/jit(cholesky)/cholesky | solution.py:71
  232.9 3.8 %while.1 = (s32[]{:T(128)}, f32[256,256]{1,0:T(8,128)S(1)}, s32[2,2]{1,0:T(2,128)S(1)}, f32[2,128,128]{2,1,0:T(8,128)S(1)}, s32[]{:T(128)}) while((s32[]{:T(128)}, f32[256,256]{1,0:T(8,128)S(1)}, s32[2,2]{1,0:T(2,128)S(1)}, f32[2,128,128]{2,1,0:T(8,128)S(1)}, s32[]{:T(128)}) %tuple.23), condition=%wide.while_cond, body=%wide.while_body.sunk | while | flops 2 | bytes 131181 | solution.py:72
  236.7 19.9 %custom-call.15 = f32[2,128,128]{1,2,0:T(8,128)S(1)} custom-call(f32[2,128,128]{2,1,0:T(8,128)S(1)} %get-tuple-element.12), custom_call_target="InvertDiagBlocksLowerTriangular" | custom-call | tf_op jit(solution)/shard_map/triangular_solve | solution.py:72
  (65 shorter events, 24.6 us)
Async XLA Ops:
  8.0 28.2 %collective-permute-start = (bf16[64,2048]{1,0:T(8,128)(2,1)S(1)}, bf16[64,2048]{1,0:T(8,128)(2,1)S(1)}, u32[]{:S(2)}, u32[]{:S(2)}) collective-permute-start(bf16[64,2048]{1,0:T(8,128)(2,1)S(1)} %bitcast.45), channel_id=1, source_target_pairs={{0,30},{2,0},{4,2},{6,4},{8,6},{10,8},{12,10},{14,12},{16,14},{18,... | collective-permute-start | bytes 786440 | tf_op jit(solution)/shard_map/ppermute | solution.py:37
  19.7 21.5 %collective-permute-start.1 = (bf16[64,2048]{1,0:T(8,128)(2,1)S(1)}, bf16[64,2048]{1,0:T(8,128)(2,1)S(1)}, u32[]{:S(2)}, u32[]{:S(2)}) collective-permute-start(bf16[64,2048]{1,0:T(8,128)(2,1)S(1)} %bitcast.46), channel_id=1, source_target_pairs={{0,2},{2,4},{4,6},{6,8},{8,10},{10,12},{12,14},{14,16},{16,18},{18... | collective-permute-start | bytes 786440 | tf_op jit(solution)/shard_map/ppermute | solution.py:35
  24.2 81.0 %all-to-all-start.1 = ((bf16[16,32,2304]{2,1,0:T(8,128)(2,1)}), bf16[16,32,2304]{2,1,0:T(8,128)(2,1)S(1)}, u32[]{:S(2)}, u32[]{:S(2)}) async-start(bf16[16,32,2304]{2,1,0:T(8,128)(2,1)} %broadcast_in_dim.13), calls=%async_computation.1 | async-start | bytes 4718592 | tf_op jit(solution)/shard_map/all_to_all | solution.py:16
  36.3 10.3 %collective-permute-start.2 = (bf16[64,2048]{1,0:T(8,128)(2,1)S(1)}, bf16[64,2048]{1,0:T(8,128)(2,1)S(1)}, u32[]{:S(2)}, u32[]{:S(2)}) collective-permute-start(bf16[64,2048]{1,0:T(8,128)(2,1)S(1)} %collective-permute-done), channel_id=1, source_target_pairs={{0,30},{2,0},{4,2},{6,4},{8,6},{10,8},{12,10},{14,12},{16,14},{18,... | collective-permute-start | bytes 786440 | tf_op jit(solution)/shard_map/ppermute | solution.py:37
  41.2 10.8 %collective-permute-start.3 = (bf16[64,2048]{1,0:T(8,128)(2,1)S(1)}, bf16[64,2048]{1,0:T(8,128)(2,1)S(1)}, u32[]{:S(2)}, u32[]{:S(2)}) collective-permute-start(bf16[64,2048]{1,0:T(8,128)(2,1)S(1)} %collective-permute-done.1), channel_id=1, source_target_pairs={{0,2},{2,4},{4,6},{6,8},{8,10},{10,12},{12,14},{14,16},{16,18},{18... | collective-permute-start | bytes 786440 | tf_op jit(solution)/shard_map/ppermute | solution.py:35
  46.6 9.9 %collective-permute-start.4 = (bf16[64,2048]{1,0:T(8,128)(2,1)S(1)}, bf16[64,2048]{1,0:T(8,128)(2,1)S(1)}, u32[]{:S(2)}, u32[]{:S(2)}) collective-permute-start(bf16[64,2048]{1,0:T(8,128)(2,1)S(1)} %collective-permute-done.2), channel_id=1, source_target_pairs={{0,30},{2,0},{4,2},{6,4},{8,6},{10,8},{12,10},{14,12},{16,14},{18,... | collective-permute-start | bytes 786440 | tf_op jit(solution)/shard_map/ppermute | solution.py:37
  51.9 9.9 %collective-permute-start.5 = (bf16[64,2048]{1,0:T(8,128)(2,1)S(1)}, bf16[64,2048]{1,0:T(8,128)(2,1)S(1)}, u32[]{:S(2)}, u32[]{:S(2)}) collective-permute-start(bf16[64,2048]{1,0:T(8,128)(2,1)S(1)} %collective-permute-done.3), channel_id=1, source_target_pairs={{0,2},{2,4},{4,6},{6,8},{8,10},{10,12},{12,14},{14,16},{16,18},{18... | collective-permute-start | bytes 786440 | tf_op jit(solution)/shard_map/ppermute | solution.py:35
  56.5 9.1 %collective-permute-start.6 = (bf16[64,2048]{1,0:T(8,128)(2,1)S(1)}, bf16[64,2048]{1,0:T(8,128)(2,1)S(1)}, u32[]{:S(2)}, u32[]{:S(2)}) collective-permute-start(bf16[64,2048]{1,0:T(8,128)(2,1)S(1)} %collective-permute-done.4), channel_id=1, source_target_pairs={{0,30},{2,0},{4,2},{6,4},{8,6},{10,8},{12,10},{14,12},{16,14},{18,... | collective-permute-start | bytes 786440 | tf_op jit(solution)/shard_map/ppermute | solution.py:37
  61.9 9.1 %collective-permute-start.7 = (bf16[64,2048]{1,0:T(8,128)(2,1)S(1)}, bf16[64,2048]{1,0:T(8,128)(2,1)S(1)}, u32[]{:S(2)}, u32[]{:S(2)}) collective-permute-start(bf16[64,2048]{1,0:T(8,128)(2,1)S(1)} %collective-permute-done.5), channel_id=1, source_target_pairs={{0,2},{2,4},{4,6},{6,8},{8,10},{10,12},{12,14},{14,16},{16,18},{18... | collective-permute-start | bytes 786440 | tf_op jit(solution)/shard_map/ppermute | solution.py:35
  65.6 8.7 %collective-permute-start.8 = (bf16[64,2048]{1,0:T(8,128)(2,1)S(1)}, bf16[64,2048]{1,0:T(8,128)(2,1)S(1)}, u32[]{:S(2)}, u32[]{:S(2)}) collective-permute-start(bf16[64,2048]{1,0:T(8,128)(2,1)S(1)} %collective-permute-done.6), channel_id=1, source_target_pairs={{0,30},{2,0},{4,2},{6,4},{8,6},{10,8},{12,10},{14,12},{16,14},{18,... | collective-permute-start | bytes 786440 | tf_op jit(solution)/shard_map/ppermute | solution.py:37
  70.9 8.3 %collective-permute-start.9 = (bf16[64,2048]{1,0:T(8,128)(2,1)S(1)}, bf16[64,2048]{1,0:T(8,128)(2,1)S(1)}, u32[]{:S(2)}, u32[]{:S(2)}) collective-permute-start(bf16[64,2048]{1,0:T(8,128)(2,1)S(1)} %collective-permute-done.7), channel_id=1, source_target_pairs={{0,2},{2,4},{4,6},{6,8},{8,10},{10,12},{12,14},{14,16},{16,18},{18... | collective-permute-start | bytes 786440 | tf_op jit(solution)/shard_map/ppermute | solution.py:35
  74.3 8.4 %collective-permute-start.10 = (bf16[64,2048]{1,0:T(8,128)(2,1)S(1)}, bf16[64,2048]{1,0:T(8,128)(2,1)S(1)}, u32[]{:S(2)}, u32[]{:S(2)}) collective-permute-start(bf16[64,2048]{1,0:T(8,128)(2,1)S(1)} %collective-permute-done.8), channel_id=1, source_target_pairs={{0,30},{2,0},{4,2},{6,4},{8,6},{10,8},{12,10},{14,12},{16,14},{18,... | collective-permute-start | bytes 786440 | tf_op jit(solution)/shard_map/ppermute | solution.py:37
  79.3 8.3 %collective-permute-start.11 = (bf16[64,2048]{1,0:T(8,128)(2,1)S(1)}, bf16[64,2048]{1,0:T(8,128)(2,1)S(1)}, u32[]{:S(2)}, u32[]{:S(2)}) collective-permute-start(bf16[64,2048]{1,0:T(8,128)(2,1)S(1)} %collective-permute-done.9), channel_id=1, source_target_pairs={{0,2},{2,4},{4,6},{6,8},{8,10},{10,12},{12,14},{14,16},{16,18},{18... | collective-permute-start | bytes 786440 | tf_op jit(solution)/shard_map/ppermute | solution.py:35
  82.7 15.1 %collective-permute-start.12 = (bf16[64,2048]{1,0:T(8,128)(2,1)S(1)}, bf16[64,2048]{1,0:T(8,128)(2,1)S(1)}, u32[]{:S(2)}, u32[]{:S(2)}) collective-permute-start(bf16[64,2048]{1,0:T(8,128)(2,1)S(1)} %collective-permute-done.10), channel_id=1, source_target_pairs={{0,30},{2,0},{4,2},{6,4},{8,6},{10,8},{12,10},{14,12},{16,14},{18,... | collective-permute-start | bytes 786440 | tf_op jit(solution)/shard_map/ppermute | solution.py:37
  87.6 8.3 %collective-permute-start.13 = (bf16[64,2048]{1,0:T(8,128)(2,1)S(1)}, bf16[64,2048]{1,0:T(8,128)(2,1)S(1)}, u32[]{:S(2)}, u32[]{:S(2)}) collective-permute-start(bf16[64,2048]{1,0:T(8,128)(2,1)S(1)} %collective-permute-done.11), channel_id=1, source_target_pairs={{0,2},{2,4},{4,6},{6,8},{8,10},{10,12},{12,14},{14,16},{16,18},{18... | collective-permute-start | bytes 786440 | tf_op jit(solution)/shard_map/ppermute | solution.py:35
  95.9 8.6 %collective-permute-start.14 = (bf16[64,2048]{1,0:T(8,128)(2,1)S(1)}, bf16[64,2048]{1,0:T(8,128)(2,1)S(1)}, u32[]{:S(2)}, u32[]{:S(2)}) collective-permute-start(bf16[64,2048]{1,0:T(8,128)(2,1)S(1)} %collective-permute-done.13), channel_id=1, source_target_pairs={{0,2},{2,4},{4,6},{6,8},{8,10},{10,12},{12,14},{14,16},{16,18},{18... | collective-permute-start | bytes 786440 | tf_op jit(solution)/shard_map/ppermute | solution.py:35
  180.9 15.9 %all-to-all-start.5 = ((f32[32,8,256]{2,1,0:T(8,128)}), f32[32,8,256]{2,1,0:T(8,128)S(1)}, u32[]{:S(2)}, u32[]{:S(2)}) async-start(f32[32,8,256]{2,1,0:T(8,128)} %broadcast_in_dim.15), calls=%async_computation.5 | async-start | bytes 524288 | tf_op jit(solution)/shard_map/all_to_all | solution.py:16

commit v3 on v2

--- a/solution.py
+++ b/solution.py
@@ -1,6 +1,10 @@
+import functools
+
 import jax
 import jax.numpy as jnp
 from jax import lax
+from jax.experimental import pallas as pl
+from jax.experimental.pallas import tpu as pltpu
 from jax.sharding import Mesh
 from jax.sharding import PartitionSpec as P
 
@@ -52,6 +56,93 @@
     return spread(share, PLANE).reshape(x.shape)
 
 
+def wide(value, width):
+    return jnp.concatenate([value] * (width // 128), axis=1)
+
+
+def eliminate(groups, lane, step):
+    width = groups[0].shape[1]
+    sublane = lax.broadcasted_iota(jnp.int32, (8, 1), 0)
+    for j in range(0, 8 * len(groups), step):
+        home, first = j // 8, j % 8
+        own = groups[home]
+        low = [[None] * step for _ in range(step)]
+        scales = []
+        for b in range(step):
+            at = lane + j + b
+            column = jnp.broadcast_to(own[:, at : at + 1], (8, 128))
+            for a in range(b, step):
+                v = jnp.broadcast_to(column[first + a : first + a + 1, :], (8, 128))
+                for c in range(b):
+                    v = v - low[a][c] * low[b][c]
+                if a == b:
+                    scales.append(lax.rsqrt(v))
+                else:
+                    low[a][b] = v * scales[b]
+        rows = []
+        for a in range(step):
+            v = jnp.broadcast_to(own[first + a : first + a + 1, :], (8, width))
+            for c in range(a):
+                v = v - wide(low[a][c], width) * rows[c]
+            rows.append(v * wide(scales[a], width))
+        for g in range(home, len(groups)):
+            value = groups[g]
+            if g > home or first + step < 8:
+                columns = []
+                new = value
+                for b in range(step):
+                    at = lane + j + b
+                    v = jnp.broadcast_to(value[:, at : at + 1], (8, 128))
+                    for c in range(b):
+                        v = v - columns[c] * low[b][c]
+                    columns.append(v * scales[b])
+                    new = new - wide(columns[b], width) * rows[b]
+                value = jnp.where(sublane >= first + step, new, value) if g == home else new
+            if g == home:
+                for a in range(step):
+                    value = jnp.where(sublane == first + a, rows[a], value)
+            groups[g] = value
+    return groups
+
+
+def orthonormalize_kernel(block, step, gram_ref, images_ref, out_ref, work, upper):
+    n, m = gram_ref.shape[0], images_ref.shape[0]
+    rows = lax.broadcasted_iota(jnp.int32, (n, n), 0)
+    cols = lax.broadcasted_iota(jnp.int32, (n, n), 1)
+    work[:, :n] = gram_ref[...] * (1 / NMU) + jnp.where(rows == cols, 1.0, 0.0)
+    padding = jnp.zeros((128 - m, n), jnp.float32)
+    work[:, n:] = jnp.concatenate([images_ref[...], padding], axis=0).T
+    for k in range(0, n, block):
+        t = k // 128 * 128
+        groups = [work[k + g : k + g + 8, t:] for g in range(0, block, 8)]
+        done = jnp.concatenate(eliminate(groups, k - t, step), axis=0)
+        upper[k : k + block, :] = done[:, n - t :]
+        r = (k + block) // 128 * 128
+        if k + block < n:
+            work[r:, r:] -= lax.dot_general(
+                done[:, r - t : n - t],
+                done[:, r - t :],
+                (((0,), (0,)), ((), ())),
+                precision=lax.Precision.HIGHEST,
+                preferred_element_type=jnp.float32,
+            )
+    out_ref[...] = upper[...].T[:m, :]
+
+
+def orthonormalize(gram_sum, images):
+    n, m = gram_sum.shape[0], images.shape[0]
+    return pl.pallas_call(
+        functools.partial(orthonormalize_kernel, 64, 8),
+        out_shape=jax.ShapeDtypeStruct((m, n), jnp.float32),
+        in_specs=[pl.BlockSpec(memory_space=pltpu.VMEM)] * 2,
+        out_specs=pl.BlockSpec(memory_space=pltpu.VMEM),
+        scratch_shapes=[
+            pltpu.VMEM((n, n + 128), jnp.float32),
+            pltpu.VMEM((n, 128), jnp.float32),
+        ],
+    )(gram_sum, images)
+
+
 def per_device(orbitals, coulomb, applied):
     width = orbitals.shape[1]
     paired = spread(jnp.concatenate([orbitals, applied], axis=1), ROW)
@@ -66,13 +157,7 @@
         jnp.dot(kernel, paired_applied, preferred_element_type=jnp.float32)
     )
     local_gram = jnp.einsum("ia,ib->ab", images, images, precision=lax.Precision.HIGHEST)
-    gram_sum = sum_everywhere(local_gram)
-    gram_matrix = jnp.eye(gram_sum.shape[0], dtype=jnp.float32) + gram_sum / NMU
-    factor = jnp.linalg.cholesky(gram_matrix)
-    projectors = lax.linalg.triangular_solve(
-        factor, images, left_side=False, lower=True, transpose_a=True
-    )
-    return projectors
+    return orthonormalize(sum_everywhere(local_gram), images)
 
 
 def solution(mesh):

time: 259 us -> 207 us (0.80)
  other arithmetic: 55.7 us -> 1.07 us
  blocking collectives: 76.2 us -> 91.9 us
  Pallas kernels: 0 us -> 10.4 us
  waiting for transfers between devices: 22.7 us -> 14 us
  starting transfers between devices: 73.6 us -> 66.4 us
  local copies, waits for them, and re-layouts: 21.5 us -> 16.7 us
    another operation x10 -> x0, other arithmetic: 54.5 us -> none  [the longest x6 34 us: per_device(): factor = jnp.linalg.cholesky(gram_matrix)]
    all_to_all x4 -> x5, blocking collectives: 76.2 us -> 91.9 us  [exchange(): return lax.all_to_all(chunks, axes, 0, 0, tiled=True)]
    pallas_call x0 -> x1, Pallas kernels: none -> 10.4 us  [orthonormalize(): pl.pallas_call(functools.partial(orthonormalize_kernel, 64, 8), out_shape...]
    all_to_all x2 -> x1, waiting for transfers between devices: 8.72 us -> 0.01 us  [exchange(): return lax.all_to_all(chunks, axes, 0, 0, tiled=True)]
    all_to_all x2 -> x1, starting transfers between devices: 16.1 us -> 8.92 us  [exchange(): return lax.all_to_all(chunks, axes, 0, 0, tiled=True)]
    another operation x9 -> x0, local copies, waits for them, and re-layouts: 3.83 us -> none
  transfers between devices with their start and end apart: 17 -> 16, of which waited for: 6 -> 5; matrix products, arithmetic and copies ran while one was open for 6% -> 8% of each run, Pallas kernels for 0% -> 0%
where the time goes in v3:
time: 207 us; the launch traced here: 206 us
  blocking collectives  91.9 us (44%)
  starting transfers between devices  66.4 us (32%)
  local copies, waits for them, and re-layouts  16.7 us (8%)
  waiting for transfers between devices  14 us (7%)
  Pallas kernels  10.4 us (5%)
  matrix products  5.59 us (3%)
    all_to_all x5, blocking collectives, exchange(): return lax.all_to_all(chunks, axes, 0, 0, tiled=True)  91.9 us
    ppermute x7, starting transfers between devices, gather_col(): behind = lax.ppermute(behind, 'z', down)  42.2 us
    ppermute x8, starting transfers between devices, gather_col(): ahead = lax.ppermute(ahead, 'z', up)  15.3 us
    pallas_call x1, Pallas kernels, orthonormalize(): pl.pallas_call(functools.partial(orthonormalize_kernel, 64, 8), out_shape...  10.4 us
    ppermute x8, waiting for transfers between devices, gather_col(): ahead = lax.ppermute(ahead, 'z', up)  10.2 us
    all_to_all x1, starting transfers between devices, exchange(): return lax.all_to_all(chunks, axes, 0, 0, tiled=True)  8.92 us
    dynamic_update_slice x8, local copies, waits for them, and re-layouts, gather_col(): lax.dynamic_update_slice(block, ahead, ((z - step & n - 1) * rows, 0))  5.73 us
    dot_general x1, matrix products, per_device(): jnp.dot(kernel, paired_applied, preferred_element_type=jnp.float32)  5.25 us
  transfers between devices with their start and end apart: 16, of which 5 were waited for; matrix products, arithmetic and copies ran while one was open for 8% of the time, Pallas kernels for 0%

profile of v3, /device:TPU:1, one launch (start us, length us, event | category | flops | bytes accessed | tf_op | source)
XLA Modules:
  0.0 206.4 jit_solution(9070305956191306032)
XLA Ops:
  0.0 0.9 broadcast_in_dim.11
  0.9 7.1 %all_to_all.30 = bf16[2,32,2048]{2,1,0:T(8,128)(2,1)S(1)} all-to-all(bf16[2,32,2048]{2,1,0:T(8,128)(2,1)S(1)} %broadcast_in_dim.11), channel_id=1, replica_groups=mesh['x_hi'=2,'y'=4,'core'=2,'z'=16,'x_lo'=2] {'x_lo'}, dimensions={0} | all-to-all | bytes 524288 | tf_op jit(solution)/shard_map/all_to_all | solution.py:20
  8.0 11.6 %collective-permute-start = (bf16[64,2048]{1,0:T(8,128)(2,1)S(1)}, bf16[64,2048]{1,0:T(8,128)(2,1)S(1)}, u32[]{:S(2)}, u32[]{:S(2)}) collective-permute-start(bf16[64,2048]{1,0:T(8,128)(2,1)S(1)} %bitcast.13), channel_id=1, source_target_pairs={{0,30},{2,0},{4,2},{6,4},{8,6},{10,8},{12,10},{14,12},{16,14},{18,... | collective-permute-start | bytes 786440 | tf_op jit(solution)/shard_map/ppermute | solution.py:41
  19.7 1.9 collective-permute-start.1
  21.6 0.9 pad_maximum_fusion
  22.5 1.7 broadcast_in_dim.12
  24.2 8.9 %all-to-all-start.1 = ((bf16[16,32,2304]{2,1,0:T(8,128)(2,1)}), bf16[16,32,2304]{2,1,0:T(8,128)(2,1)S(1)}, u32[]{:S(2)}, u32[]{:S(2)}) async-start(bf16[16,32,2304]{2,1,0:T(8,128)(2,1)} %broadcast_in_dim.12), calls=%async_computation.1 | async-start | bytes 4718592 | tf_op jit(solution)/shard_map/all_to_all | solution.py:20
  33.1 2.5 %broadcast_in_dim.10 = bf16[1024,2048]{1,0:T(8,128)(2,1)} broadcast(bf16[]{:T(256)} %constant.10.clone.1), dimensions={} | broadcast | bytes 4194306 | tf_op jit(solution)/shard_map/broadcast_in_dim | solution.py:33
  36.3 4.8 %collective-permute-start.2 = (bf16[64,2048]{1,0:T(8,128)(2,1)S(1)}, bf16[64,2048]{1,0:T(8,128)(2,1)S(1)}, u32[]{:S(2)}, u32[]{:S(2)}) collective-permute-start(bf16[64,2048]{1,0:T(8,128)(2,1)S(1)} %collective-permute-done), channel_id=1, source_target_pairs={{0,30},{2,0},{4,2},{6,4},{8,6},{10,8},{12,10},{14,12},{16,14},{18,... | collective-permute-start | bytes 786440 | tf_op jit(solution)/shard_map/ppermute | solution.py:41
  41.2 1.9 collective-permute-start.3
  44.5 2.1 %collective-permute-done.2 = bf16[64,2048]{1,0:T(8,128)(2,1)S(1)} collective-permute-done((bf16[64,2048]{1,0:T(8,128)(2,1)S(1)}, bf16[64,2048]{1,0:T(8,128)(2,1)S(1)}, u32[]{:S(2)}, u32[]{:S(2)}) %collective-permute-start.2) | collective-permute-done | bytes 262176 | tf_op jit(solution)/shard_map/ppermute | solution.py:41
  46.6 5.3 %collective-permute-start.4 = (bf16[64,2048]{1,0:T(8,128)(2,1)S(1)}, bf16[64,2048]{1,0:T(8,128)(2,1)S(1)}, u32[]{:S(2)}, u32[]{:S(2)}) collective-permute-start(bf16[64,2048]{1,0:T(8,128)(2,1)S(1)} %collective-permute-done.2), channel_id=1, source_target_pairs={{0,30},{2,0},{4,2},{6,4},{8,6},{10,8},{12,10},{14,12},{16,14},{18,... | collective-permute-start | bytes 786440 | tf_op jit(solution)/shard_map/ppermute | solution.py:41
  51.9 1.9 collective-permute-start.5
  55.3 1.2 collective-permute-done.4
  56.5 5.3 %collective-permute-start.6 = (bf16[64,2048]{1,0:T(8,128)(2,1)S(1)}, bf16[64,2048]{1,0:T(8,128)(2,1)S(1)}, u32[]{:S(2)}, u32[]{:S(2)}) collective-permute-start(bf16[64,2048]{1,0:T(8,128)(2,1)S(1)} %collective-permute-done.4), channel_id=1, source_target_pairs={{0,30},{2,0},{4,2},{6,4},{8,6},{10,8},{12,10},{14,12},{16,14},{18,... | collective-permute-start | bytes 786440 | tf_op jit(solution)/shard_map/ppermute | solution.py:41
  61.9 1.9 collective-permute-start.7
  65.6 5.3 %collective-permute-start.8 = (bf16[64,2048]{1,0:T(8,128)(2,1)S(1)}, bf16[64,2048]{1,0:T(8,128)(2,1)S(1)}, u32[]{:S(2)}, u32[]{:S(2)}) collective-permute-start(bf16[64,2048]{1,0:T(8,128)(2,1)S(1)} %collective-permute-done.6), channel_id=1, source_target_pairs={{0,30},{2,0},{4,2},{6,4},{8,6},{10,8},{12,10},{14,12},{16,14},{18,... | collective-permute-start | bytes 786440 | tf_op jit(solution)/shard_map/ppermute | solution.py:41
  70.9 1.9 collective-permute-start.9
  72.9 0.7 constant_dynamic-update-slice_fusion.8
  74.3 4.9 %collective-permute-start.10 = (bf16[64,2048]{1,0:T(8,128)(2,1)S(1)}, bf16[64,2048]{1,0:T(8,128)(2,1)S(1)}, u32[]{:S(2)}, u32[]{:S(2)}) collective-permute-start(bf16[64,2048]{1,0:T(8,128)(2,1)S(1)} %collective-permute-done.8), channel_id=1, source_target_pairs={{0,30},{2,0},{4,2},{6,4},{8,6},{10,8},{12,10},{14,12},{16,14},{18,... | collective-permute-start | bytes 786440 | tf_op jit(solution)/shard_map/ppermute | solution.py:41
  79.3 1.9 collective-permute-start.11
  82.6 4.9 %collective-permute-start.12 = (bf16[64,2048]{1,0:T(8,128)(2,1)S(1)}, bf16[64,2048]{1,0:T(8,128)(2,1)S(1)}, u32[]{:S(2)}, u32[]{:S(2)}) collective-permute-start(bf16[64,2048]{1,0:T(8,128)(2,1)S(1)} %collective-permute-done.10), channel_id=1, source_target_pairs={{0,30},{2,0},{4,2},{6,4},{8,6},{10,8},{12,10},{14,12},{16,14},{18,... | collective-permute-start | bytes 786440 | tf_op jit(solution)/shard_map/ppermute | solution.py:41
  87.6 1.9 collective-permute-start.13
  90.9 5.0 %collective-permute-done.13 = bf16[64,2048]{1,0:T(8,128)(2,1)S(1)} collective-permute-done((bf16[64,2048]{1,0:T(8,128)(2,1)S(1)}, bf16[64,2048]{1,0:T(8,128)(2,1)S(1)}, u32[]{:S(2)}, u32[]{:S(2)}) %collective-permute-start.13) | collective-permute-done | bytes 262176 | tf_op jit(solution)/shard_map/ppermute | solution.py:39
  95.9 1.9 collective-permute-start.14
  99.3 5.2 %collective-permute-done.14 = bf16[64,2048]{1,0:T(8,128)(2,1)S(1)} collective-permute-done((bf16[64,2048]{1,0:T(8,128)(2,1)S(1)}, bf16[64,2048]{1,0:T(8,128)(2,1)S(1)}, u32[]{:S(2)}, u32[]{:S(2)}) %collective-permute-start.14) | collective-permute-done | bytes 262176 | tf_op jit(solution)/shard_map/ppermute | solution.py:39
  105.2 5.2 %convolution_convert_fusion = bf16[1024,256]{1,0:T(8,128)(2,1)S(1)} fusion(bf16[1024,512]{1,0:T(8,128)(2,1)} %param.4, bf16[1024,2048]{1,0:T(8,128)(2,1)} %constant_dynamic-update-slice_fusion, bf16[512,2304]{1,0:T(8,128)(2,1)S(1)} %bitcast.12), kind=kOutput, calls=%fused_computation.3 | convolution fusion | flops 2417754112 | bytes 8126464 | tf_op jit(solution)/shard_map/dot_general | solution.py:157
  110.5 29.4 %all_to_all.31 = bf16[32,32,256]{2,1,0:T(8,128)(2,1)S(1)} all-to-all(bf16[32,32,256]{2,1,0:T(8,128)(2,1)S(1)} %bitcast.17), channel_id=1, replica_groups=mesh['x_hi'=2,'y'=4,'core'=2,'z'=16,'x_lo'=2] {'z','x_lo'}, dimensions={0} | all-to-all | bytes 1048576 | tf_op jit(solution)/shard_map/all_to_all | solution.py:20
  140.4 25.2 %all_to_all.32 = f32[32,8,256]{2,1,0:T(8,128)S(1)} all-to-all(f32[32,8,256]{2,1,0:T(8,128)S(1)} %fusion.7), channel_id=1, replica_groups=mesh['x_hi'=2,'y'=4,'core'=2,'z'=16,'x_lo'=2] {'x_hi','y','core','x_lo'}, dimensions={0} | all-to-all | bytes 524288 | tf_op jit(solution)/shard_map/all_to_all | solution.py:20
  165.6 14.5 %all_to_all.33 = f32[16,8,256]{2,1,0:T(8,128)S(1)} all-to-all(f32[16,8,256]{2,1,0:T(8,128)S(1)} %broadcast_in_dim.13), channel_id=1, replica_groups=mesh['x_hi'=2,'y'=4,'core'=2,'z'=16,'x_lo'=2] {'z'}, dimensions={0} | all-to-all | bytes 262144 | tf_op jit(solution)/shard_map/all_to_all | solution.py:20
  180.2 15.7 %all_to_all.34 = f32[32,8,256]{2,1,0:T(8,128)} all-to-all(f32[32,8,256]{2,1,0:T(8,128)S(1)} %broadcast_in_dim.14), channel_id=1, replica_groups=mesh['x_hi'=2,'y'=4,'core'=2,'z'=16,'x_lo'=2] {'x_hi','y','core','x_lo'}, dimensions={0} | all-to-all | bytes 524288 | tf_op jit(solution)/shard_map/all_to_all | solution.py:20
  195.9 10.4 %shard_map.37 = f32[32,256]{1,0:T(8,128)} custom-call(f32[256,256]{1,0:T(8,128)} %bitcast.16, f32[32,256]{1,0:T(8,128)} %copy-done), custom_call_target="tpu_custom_call" | custom-call | tf_op jit(solution)/shard_map/pallas_call | solution.py:134
  (36 shorter events, 11.9 us)
Async XLA Ops:
  8.0 28.3 %collective-permute-start = (bf16[64,2048]{1,0:T(8,128)(2,1)S(1)}, bf16[64,2048]{1,0:T(8,128)(2,1)S(1)}, u32[]{:S(2)}, u32[]{:S(2)}) collective-permute-start(bf16[64,2048]{1,0:T(8,128)(2,1)S(1)} %bitcast.13), channel_id=1, source_target_pairs={{0,30},{2,0},{4,2},{6,4},{8,6},{10,8},{12,10},{14,12},{16,14},{18,... | collective-permute-start | bytes 786440 | tf_op jit(solution)/shard_map/ppermute | solution.py:41
  19.7 21.5 %collective-permute-start.1 = (bf16[64,2048]{1,0:T(8,128)(2,1)S(1)}, bf16[64,2048]{1,0:T(8,128)(2,1)S(1)}, u32[]{:S(2)}, u32[]{:S(2)}) collective-permute-start(bf16[64,2048]{1,0:T(8,128)(2,1)S(1)} %bitcast.14), channel_id=1, source_target_pairs={{0,2},{2,4},{4,6},{6,8},{8,10},{10,12},{12,14},{14,16},{16,18},{18... | collective-permute-start | bytes 786440 | tf_op jit(solution)/shard_map/ppermute | solution.py:39
  24.2 81.0 %all-to-all-start.1 = ((bf16[16,32,2304]{2,1,0:T(8,128)(2,1)}), bf16[16,32,2304]{2,1,0:T(8,128)(2,1)S(1)}, u32[]{:S(2)}, u32[]{:S(2)}) async-start(bf16[16,32,2304]{2,1,0:T(8,128)(2,1)} %broadcast_in_dim.12), calls=%async_computation.1 | async-start | bytes 4718592 | tf_op jit(solution)/shard_map/all_to_all | solution.py:20
  36.3 10.3 %collective-permute-start.2 = (bf16[64,2048]{1,0:T(8,128)(2,1)S(1)}, bf16[64,2048]{1,0:T(8,128)(2,1)S(1)}, u32[]{:S(2)}, u32[]{:S(2)}) collective-permute-start(bf16[64,2048]{1,0:T(8,128)(2,1)S(1)} %collective-permute-done), channel_id=1, source_target_pairs={{0,30},{2,0},{4,2},{6,4},{8,6},{10,8},{12,10},{14,12},{16,14},{18,... | collective-permute-start | bytes 786440 | tf_op jit(solution)/shard_map/ppermute | solution.py:41
  41.2 10.8 %collective-permute-start.3 = (bf16[64,2048]{1,0:T(8,128)(2,1)S(1)}, bf16[64,2048]{1,0:T(8,128)(2,1)S(1)}, u32[]{:S(2)}, u32[]{:S(2)}) collective-permute-start(bf16[64,2048]{1,0:T(8,128)(2,1)S(1)} %collective-permute-done.1), channel_id=1, source_target_pairs={{0,2},{2,4},{4,6},{6,8},{8,10},{10,12},{12,14},{14,16},{16,18},{18... | collective-permute-start | bytes 786440 | tf_op jit(solution)/shard_map/ppermute | solution.py:39
  46.6 9.9 %collective-permute-start.4 = (bf16[64,2048]{1,0:T(8,128)(2,1)S(1)}, bf16[64,2048]{1,0:T(8,128)(2,1)S(1)}, u32[]{:S(2)}, u32[]{:S(2)}) collective-permute-start(bf16[64,2048]{1,0:T(8,128)(2,1)S(1)} %collective-permute-done.2), channel_id=1, source_target_pairs={{0,30},{2,0},{4,2},{6,4},{8,6},{10,8},{12,10},{14,12},{16,14},{18,... | collective-permute-start | bytes 786440 | tf_op jit(solution)/shard_map/ppermute | solution.py:41
  51.9 9.9 %collective-permute-start.5 = (bf16[64,2048]{1,0:T(8,128)(2,1)S(1)}, bf16[64,2048]{1,0:T(8,128)(2,1)S(1)}, u32[]{:S(2)}, u32[]{:S(2)}) collective-permute-start(bf16[64,2048]{1,0:T(8,128)(2,1)S(1)} %collective-permute-done.3), channel_id=1, source_target_pairs={{0,2},{2,4},{4,6},{6,8},{8,10},{10,12},{12,14},{14,16},{16,18},{18... | collective-permute-start | bytes 786440 | tf_op jit(solution)/shard_map/ppermute | solution.py:39
  56.5 9.1 %collective-permute-start.6 = (bf16[64,2048]{1,0:T(8,128)(2,1)S(1)}, bf16[64,2048]{1,0:T(8,128)(2,1)S(1)}, u32[]{:S(2)}, u32[]{:S(2)}) collective-permute-start(bf16[64,2048]{1,0:T(8,128)(2,1)S(1)} %collective-permute-done.4), channel_id=1, source_target_pairs={{0,30},{2,0},{4,2},{6,4},{8,6},{10,8},{12,10},{14,12},{16,14},{18,... | collective-permute-start | bytes 786440 | tf_op jit(solution)/shard_map/ppermute | solution.py:41
  61.9 9.1 %collective-permute-start.7 = (bf16[64,2048]{1,0:T(8,128)(2,1)S(1)}, bf16[64,2048]{1,0:T(8,128)(2,1)S(1)}, u32[]{:S(2)}, u32[]{:S(2)}) collective-permute-start(bf16[64,2048]{1,0:T(8,128)(2,1)S(1)} %collective-permute-done.5), channel_id=1, source_target_pairs={{0,2},{2,4},{4,6},{6,8},{8,10},{10,12},{12,14},{14,16},{16,18},{18... | collective-permute-start | bytes 786440 | tf_op jit(solution)/shard_map/ppermute | solution.py:39
  65.6 8.7 %collective-permute-start.8 = (bf16[64,2048]{1,0:T(8,128)(2,1)S(1)}, bf16[64,2048]{1,0:T(8,128)(2,1)S(1)}, u32[]{:S(2)}, u32[]{:S(2)}) collective-permute-start(bf16[64,2048]{1,0:T(8,128)(2,1)S(1)} %collective-permute-done.6), channel_id=1, source_target_pairs={{0,30},{2,0},{4,2},{6,4},{8,6},{10,8},{12,10},{14,12},{16,14},{18,... | collective-permute-start | bytes 786440 | tf_op jit(solution)/shard_map/ppermute | solution.py:41
  70.9 8.3 %collective-permute-start.9 = (bf16[64,2048]{1,0:T(8,128)(2,1)S(1)}, bf16[64,2048]{1,0:T(8,128)(2,1)S(1)}, u32[]{:S(2)}, u32[]{:S(2)}) collective-permute-start(bf16[64,2048]{1,0:T(8,128)(2,1)S(1)} %collective-permute-done.7), channel_id=1, source_target_pairs={{0,2},{2,4},{4,6},{6,8},{8,10},{10,12},{12,14},{14,16},{16,18},{18... | collective-permute-start | bytes 786440 | tf_op jit(solution)/shard_map/ppermute | solution.py:39
  74.3 8.3 %collective-permute-start.10 = (bf16[64,2048]{1,0:T(8,128)(2,1)S(1)}, bf16[64,2048]{1,0:T(8,128)(2,1)S(1)}, u32[]{:S(2)}, u32[]{:S(2)}) collective-permute-start(bf16[64,2048]{1,0:T(8,128)(2,1)S(1)} %collective-permute-done.8), channel_id=1, source_target_pairs={{0,30},{2,0},{4,2},{6,4},{8,6},{10,8},{12,10},{14,12},{16,14},{18,... | collective-permute-start | bytes 786440 | tf_op jit(solution)/shard_map/ppermute | solution.py:41
  79.3 8.3 %collective-permute-start.11 = (bf16[64,2048]{1,0:T(8,128)(2,1)S(1)}, bf16[64,2048]{1,0:T(8,128)(2,1)S(1)}, u32[]{:S(2)}, u32[]{:S(2)}) collective-permute-start(bf16[64,2048]{1,0:T(8,128)(2,1)S(1)} %collective-permute-done.9), channel_id=1, source_target_pairs={{0,2},{2,4},{4,6},{6,8},{8,10},{10,12},{12,14},{14,16},{16,18},{18... | collective-permute-start | bytes 786440 | tf_op jit(solution)/shard_map/ppermute | solution.py:39
  82.6 15.2 %collective-permute-start.12 = (bf16[64,2048]{1,0:T(8,128)(2,1)S(1)}, bf16[64,2048]{1,0:T(8,128)(2,1)S(1)}, u32[]{:S(2)}, u32[]{:S(2)}) collective-permute-start(bf16[64,2048]{1,0:T(8,128)(2,1)S(1)} %collective-permute-done.10), channel_id=1, source_target_pairs={{0,30},{2,0},{4,2},{6,4},{8,6},{10,8},{12,10},{14,12},{16,14},{18,... | collective-permute-start | bytes 786440 | tf_op jit(solution)/shard_map/ppermute | solution.py:41
  87.6 8.3 %collective-permute-start.13 = (bf16[64,2048]{1,0:T(8,128)(2,1)S(1)}, bf16[64,2048]{1,0:T(8,128)(2,1)S(1)}, u32[]{:S(2)}, u32[]{:S(2)}) collective-permute-start(bf16[64,2048]{1,0:T(8,128)(2,1)S(1)} %collective-permute-done.11), channel_id=1, source_target_pairs={{0,2},{2,4},{4,6},{6,8},{8,10},{10,12},{12,14},{14,16},{16,18},{18... | collective-permute-start | bytes 786440 | tf_op jit(solution)/shard_map/ppermute | solution.py:39
  95.9 8.6 %collective-permute-start.14 = (bf16[64,2048]{1,0:T(8,128)(2,1)S(1)}, bf16[64,2048]{1,0:T(8,128)(2,1)S(1)}, u32[]{:S(2)}, u32[]{:S(2)}) collective-permute-start(bf16[64,2048]{1,0:T(8,128)(2,1)S(1)} %collective-permute-done.13), channel_id=1, source_target_pairs={{0,2},{2,4},{4,6},{6,8},{8,10},{10,12},{12,14},{14,16},{16,18},{18... | collective-permute-start | bytes 786440 | tf_op jit(solution)/shard_map/ppermute | solution.py:39
  139.9 56.0 %copy-start = (f32[32,256]{1,0:T(8,128)}, f32[32,256]{1,0:T(8,128)S(1)}, u32[]{:S(2)}) copy-start(f32[32,256]{1,0:T(8,128)S(1)} %convert_reduce_fusion.images_ref) | copy-start | bytes 98308

commit v4 on v3

--- a/solution.py
+++ b/solution.py
@@ -11,7 +11,7 @@
 NMU = 16384
 ROW = ("x_hi", "y", "core")
 COL = ("z", "x_lo")
-PLANE = ("x_hi", "y", "core", "x_lo")
+PLANE = ("x_lo",) + ROW
 AXES = ROW + COL
 SIZES = (2, 4, 2, 16, 2)
 
@@ -25,16 +25,15 @@
     return exchange(copies, axes)
 
 
-def gather_col(orbitals):
+def gather_z(mine):
     n = lax.axis_size("z")
     z = lax.axis_index("z")
-    pair = spread(orbitals, "x_lo").reshape(-1, orbitals.shape[1])
-    rows = pair.shape[0]
-    block = jnp.zeros((n * rows, pair.shape[1]), pair.dtype)
-    block = lax.dynamic_update_slice(block, pair, (z * rows, 0))
+    rows = mine.shape[0]
+    block = jnp.zeros((n * rows, mine.shape[1]), mine.dtype)
+    block = lax.dynamic_update_slice(block, mine, (z * rows, 0))
     up = [(i, (i + 1) % n) for i in range(n)]
     down = [(i, (i - 1) % n) for i in range(n)]
-    ahead, behind = pair, pair
+    ahead, behind = mine, mine
     for step in range(1, n // 2 + 1):
         ahead = lax.ppermute(ahead, "z", up)
         if step < n // 2:
@@ -44,9 +43,20 @@
     return block
 
 
+def swap_sides(coulomb, count):
+    side = lax.axis_index("x_lo")
+    halves = coulomb.reshape(-1, 2, count, coulomb.shape[1])
+    first, second = halves[:, 0], halves[:, 1]
+    low = side == 0
+    kept = jnp.where(low, first, second)
+    moved = lax.ppermute(jnp.where(low, second, first), "x_lo", [(0, 1), (1, 0)])
+    left, right = jnp.where(low, kept, moved), jnp.where(low, moved, kept)
+    return jnp.concatenate([left, right], axis=-1).reshape(-1, 2 * coulomb.shape[1])
+
+
 def reduce_rows(partial):
-    chunks = partial.astype(jnp.bfloat16).reshape(lax.axis_size(COL), -1, partial.shape[1])
-    return jnp.sum(exchange(chunks, COL).astype(jnp.float32), axis=0)
+    chunks = partial.astype(jnp.bfloat16).reshape(lax.axis_size("z"), -1, partial.shape[1])
+    return jnp.sum(exchange(chunks, "z").astype(jnp.float32), axis=0)
 
 
 def sum_everywhere(x):
@@ -145,16 +155,16 @@
 
 def per_device(orbitals, coulomb, applied):
     width = orbitals.shape[1]
-    paired = spread(jnp.concatenate([orbitals, applied], axis=1), ROW)
+    paired = spread(jnp.concatenate([orbitals, applied], axis=1), PLANE)
     paired = paired.reshape(-1, paired.shape[-1])
-    paired_orbitals, paired_applied = paired[:, :width], paired[:, width:]
-    point_block = gather_col(orbitals)
+    tile = swap_sides(coulomb, orbitals.shape[0])
+    points = gather_z(orbitals)
     density = jnp.einsum(
-        "ik,jk->ij", point_block, paired_orbitals, preferred_element_type=jnp.float32
+        "ik,jk->ij", points, paired[:, :width], preferred_element_type=jnp.float32
     )
-    kernel = (coulomb.astype(jnp.float32) * density).astype(jnp.bfloat16)
+    kernel = (tile.astype(jnp.float32) * density).astype(jnp.bfloat16)
     images = reduce_rows(
-        jnp.dot(kernel, paired_applied, preferred_element_type=jnp.float32)
+        jnp.dot(kernel, paired[:, width:], preferred_element_type=jnp.float32)
     )
     local_gram = jnp.einsum("ia,ib->ab", images, images, precision=lax.Precision.HIGHEST)
     return orthonormalize(sum_everywhere(local_gram), images)

time: 207 us -> 204 us (0.986)
  waiting for transfers between devices: 14 us -> 35.3 us
  blocking collectives: 91.9 us -> 73.3 us
  local copies, waits for them, and re-layouts: 16.7 us -> 3.38 us
  starting transfers between devices: 66.4 us -> 72 us
  other arithmetic: 1.07 us -> 3.14 us
    ppermute x15 -> x16, waiting for transfers between devices: 14 us -> 35.3 us  [the longest x1 25.3 us: swap_sides(): lax.ppermute(jnp.where(low, second, first), 'x_lo', [(0, 1), (1, 0)])]
    all_to_all x5 -> x4, blocking collectives: 91.9 us -> 73.3 us  [exchange(): return lax.all_to_all(chunks, axes, 0, 0, tiled=True)]
    dynamic_update_slice x16, local copies, waits for them, and re-layouts: 11.5 us -> 0.27 us  [the longest x8 0.13 us: gather_z(): lax.dynamic_update_slice(block, ahead, ((z - step & n - 1) * rows, 0))]
    ppermute x15 -> x16, starting transfers between devices: 57.5 us -> 60.6 us  [the longest x7 42 us: gather_z(): behind = lax.ppermute(behind, 'z', down)]
    all_to_all x1, starting transfers between devices: 8.92 us -> 11.4 us  [exchange(): return lax.all_to_all(chunks, axes, 0, 0, tiled=True)]
    broadcast_in_dim x1, local copies, waits for them, and re-layouts: 2.47 us -> 0.24 us  [gather_z(): block = jnp.zeros((n * rows, mine.shape[1]), mine.dtype)]
  transfers between devices with their start and end apart: 16 -> 17, of which waited for: 5 -> 3; matrix products, arithmetic and copies ran while one was open for 8% -> 1% of each run, Pallas kernels for 0% -> 0%
where the time goes in v4:
time: 204 us; the launch traced here: 203 us
  blocking collectives  73.3 us (36%)
  starting transfers between devices  72 us (35%)
  waiting for transfers between devices  35.3 us (17%)
  Pallas kernels  10.4 us (5%)
  matrix products  5.42 us (3%)
  local copies, waits for them, and re-layouts  3.38 us (2%)
  other arithmetic  3.14 us (2%)
    all_to_all x4, blocking collectives, exchange(): return lax.all_to_all(chunks, axes, 0, 0, tiled=True)  73.3 us
    ppermute x7, starting transfers between devices, gather_z(): behind = lax.ppermute(behind, 'z', down)  42 us
    ppermute x1, waiting for transfers between devices, swap_sides(): lax.ppermute(jnp.where(low, second, first), 'x_lo', [(0, 1), (1, 0)])  25.3 us
    ppermute x8, starting transfers between devices, gather_z(): ahead = lax.ppermute(ahead, 'z', up)  15.3 us
    all_to_all x1, starting transfers between devices, exchange(): return lax.all_to_all(chunks, axes, 0, 0, tiled=True)  11.4 us
    pallas_call x1, Pallas kernels, orthonormalize(): pl.pallas_call(functools.partial(orthonormalize_kernel, 64, 8), out_shape...  10.4 us
    ppermute x8, waiting for transfers between devices, gather_z(): ahead = lax.ppermute(ahead, 'z', up)  9.97 us
    dot_general x1, matrix products, per_device(): jnp.dot(kernel, paired[:, width:], preferred_element_type=jnp.float32)  5.07 us
  transfers between devices with their start and end apart: 17, of which 3 were waited for; matrix products, arithmetic and copies ran while one was open for 1% of the time, Pallas kernels for 0%

profile of v4, /device:TPU:1, one launch (start us, length us, event | category | flops | bytes accessed | tf_op | source)
XLA Modules:
  0.0 203.5 jit_solution(11161753583796726044)
XLA Ops:
  0.0 0.9 pad_maximum_fusion.1
  0.9 2.7 %broadcast_in_dim.9 = bf16[32,32,2304]{2,1,0:T(8,128)(2,1)} broadcast(bf16[32,2304]{1,0:T(8,128)(2,1)S(1)} %pad_maximum_fusion.1), dimensions={1,2} | broadcast | bytes 4866048 | tf_op jit(solution)/shard_map/broadcast_in_dim | solution.py:24
  3.7 11.4 %all-to-all-start = ((bf16[32,32,2304]{2,1,0:T(8,128)(2,1)}), bf16[32,32,2304]{2,1,0:T(8,128)(2,1)}, u32[]{:S(2)}, u32[]{:S(2)}) async-start(bf16[32,32,2304]{2,1,0:T(8,128)(2,1)} %broadcast_in_dim.9), calls=%async_computation | async-start | bytes 9437184 | tf_op jit(solution)/shard_map/all_to_all | solution.py:20
  15.1 8.5 %collective-permute-start.1 = (bf16[32,2048]{1,0:T(8,128)(2,1)S(1)}, bf16[32,2048]{1,0:T(8,128)(2,1)S(1)}, u32[]{:S(2)}, u32[]{:S(2)}) collective-permute-start(bf16[32,2048]{1,0:T(8,128)(2,1)S(1)} %copy-done.1), channel_id=1, source_target_pairs={{0,30},{2,0},{4,2},{6,4},{8,6},{10,8},{12,10},{14,12},{16,14},{18,... | collective-permute-start | bytes 393224 | tf_op jit(solution)/shard_map/ppermute | solution.py:40
  23.6 1.9 collective-permute-start.2
  25.5 0.9 select_bitcast_fusion
  26.4 3.3 %collective-permute-start = (bf16[16,32,512]{2,1,0:T(8,128)(2,1)}, bf16[16,32,512]{2,1,0:T(8,128)(2,1)}, u32[]{:S(2)}, u32[]{:S(2)}) collective-permute-start(bf16[16,32,512]{2,1,0:T(8,128)(2,1)} %select_bitcast_fusion), channel_id=1, source_target_pairs={{0,1},{1,0},{2,3},{3,2},{4,5},{5,4},{6,7},{7,6},{8,9},{9,8},{10,11... | collective-permute-start | bytes 1572872 | tf_op jit(solution)/shard_map/ppermute | solution.py:52
  29.7 0.2 broadcast_in_dim.8
  30.0 4.6 %collective-permute-start.3 = (bf16[32,2048]{1,0:T(8,128)(2,1)S(1)}, bf16[32,2048]{1,0:T(8,128)(2,1)S(1)}, u32[]{:S(2)}, u32[]{:S(2)}) collective-permute-start(bf16[32,2048]{1,0:T(8,128)(2,1)S(1)} %collective-permute-done.1), channel_id=1, source_target_pairs={{0,30},{2,0},{4,2},{6,4},{8,6},{10,8},{12,10},{14,12},{16,14},{18,... | collective-permute-start | bytes 393224 | tf_op jit(solution)/shard_map/ppermute | solution.py:40
  34.6 1.9 collective-permute-start.4
  36.6 5.3 %collective-permute-start.5 = (bf16[32,2048]{1,0:T(8,128)(2,1)S(1)}, bf16[32,2048]{1,0:T(8,128)(2,1)S(1)}, u32[]{:S(2)}, u32[]{:S(2)}) collective-permute-start(bf16[32,2048]{1,0:T(8,128)(2,1)S(1)} %collective-permute-done.3), channel_id=1, source_target_pairs={{0,30},{2,0},{4,2},{6,4},{8,6},{10,8},{12,10},{14,12},{16,14},{18,... | collective-permute-start | bytes 393224 | tf_op jit(solution)/shard_map/ppermute | solution.py:40
  41.9 1.9 collective-permute-start.6
  43.9 5.3 %collective-permute-start.7 = (bf16[32,2048]{1,0:T(8,128)(2,1)S(1)}, bf16[32,2048]{1,0:T(8,128)(2,1)S(1)}, u32[]{:S(2)}, u32[]{:S(2)}) collective-permute-start(bf16[32,2048]{1,0:T(8,128)(2,1)S(1)} %collective-permute-done.5), channel_id=1, source_target_pairs={{0,30},{2,0},{4,2},{6,4},{8,6},{10,8},{12,10},{14,12},{16,14},{18,... | collective-permute-start | bytes 393224 | tf_op jit(solution)/shard_map/ppermute | solution.py:40
  49.2 1.9 collective-permute-start.8
  51.2 5.3 %collective-permute-start.9 = (bf16[32,2048]{1,0:T(8,128)(2,1)S(1)}, bf16[32,2048]{1,0:T(8,128)(2,1)S(1)}, u32[]{:S(2)}, u32[]{:S(2)}) collective-permute-start(bf16[32,2048]{1,0:T(8,128)(2,1)S(1)} %collective-permute-done.7), channel_id=1, source_target_pairs={{0,30},{2,0},{4,2},{6,4},{8,6},{10,8},{12,10},{14,12},{16,14},{18,... | collective-permute-start | bytes 393224 | tf_op jit(solution)/shard_map/ppermute | solution.py:40
  56.5 1.9 collective-permute-start.10
  58.5 25.3 %collective-permute-done = bf16[16,32,512]{2,1,0:T(8,128)(2,1)} collective-permute-done((bf16[16,32,512]{2,1,0:T(8,128)(2,1)}, bf16[16,32,512]{2,1,0:T(8,128)(2,1)}, u32[]{:S(2)}, u32[]{:S(2)}) %collective-permute-start) | collective-permute-done | bytes 524320 | tf_op jit(solution)/shard_map/ppermute | solution.py:52
  83.9 1.1 bitcast_select_fusion.1
  85.1 8.2 %collective-permute-start.11 = (bf16[32,2048]{1,0:T(8,128)(2,1)S(1)}, bf16[32,2048]{1,0:T(8,128)(2,1)S(1)}, u32[]{:S(2)}, u32[]{:S(2)}) collective-permute-start(bf16[32,2048]{1,0:T(8,128)(2,1)S(1)} %collective-permute-done.9), channel_id=1, source_target_pairs={{0,30},{2,0},{4,2},{6,4},{8,6},{10,8},{12,10},{14,12},{16,14},{18,... | collective-permute-start | bytes 393224 | tf_op jit(solution)/shard_map/ppermute | solution.py:40
  93.3 1.9 collective-permute-start.12
  95.3 4.9 %collective-permute-start.13 = (bf16[32,2048]{1,0:T(8,128)(2,1)S(1)}, bf16[32,2048]{1,0:T(8,128)(2,1)S(1)}, u32[]{:S(2)}, u32[]{:S(2)}) collective-permute-start(bf16[32,2048]{1,0:T(8,128)(2,1)S(1)} %collective-permute-done.11), channel_id=1, source_target_pairs={{0,30},{2,0},{4,2},{6,4},{8,6},{10,8},{12,10},{14,12},{16,14},{18,... | collective-permute-start | bytes 393224 | tf_op jit(solution)/shard_map/ppermute | solution.py:40
  100.2 1.9 collective-permute-start.14
  102.2 4.9 %collective-permute-done.14 = bf16[32,2048]{1,0:T(8,128)(2,1)S(1)} collective-permute-done((bf16[32,2048]{1,0:T(8,128)(2,1)S(1)}, bf16[32,2048]{1,0:T(8,128)(2,1)S(1)}, u32[]{:S(2)}, u32[]{:S(2)}) %collective-permute-start.14) | collective-permute-done | bytes 131104 | tf_op jit(solution)/shard_map/ppermute | solution.py:38
  107.1 1.9 collective-permute-start.15
  109.1 4.9 %collective-permute-done.15 = bf16[32,2048]{1,0:T(8,128)(2,1)S(1)} collective-permute-done((bf16[32,2048]{1,0:T(8,128)(2,1)S(1)}, bf16[32,2048]{1,0:T(8,128)(2,1)S(1)}, u32[]{:S(2)}, u32[]{:S(2)}) %collective-permute-start.15) | collective-permute-done | bytes 131104 | tf_op jit(solution)/shard_map/ppermute | solution.py:38
  114.1 5.1 %convolution_convert_fusion = bf16[512,256]{1,0:T(8,128)(2,1)S(1)} fusion(bf16[512,1024]{1,0:T(8,128)(2,1)S(1)} %bitcast.42, bf16[512,2048]{1,0:T(8,128)(2,1)S(1)} %constant_dynamic-update-slice_fusion, bf16[1024,2304]{1,0:T(8,128)(2,1)} %bitcast.4), kind=kOutput, calls=%fused_computation.4 | convolution fusion | flops 2417623040 | bytes 8126464 | tf_op jit(solution)/shard_map/dot_general | solution.py:167
  119.2 18.7 %all_to_all.25 = bf16[16,32,256]{2,1,0:T(8,128)(2,1)S(1)} all-to-all(bf16[16,32,256]{2,1,0:T(8,128)(2,1)S(1)} %bitcast.44), channel_id=1, replica_groups=mesh['x_hi'=2,'y'=4,'core'=2,'z'=16,'x_lo'=2] {'z'}, dimensions={0} | all-to-all | bytes 524288 | tf_op jit(solution)/shard_map/all_to_all | solution.py:20
  138.0 0.3 fusion.8
  138.4 23.0 %all_to_all.26 = f32[32,8,256]{2,1,0:T(8,128)S(1)} all-to-all(f32[32,8,256]{2,1,0:T(8,128)S(1)} %fusion.8), channel_id=1, replica_groups=mesh['x_hi'=2,'y'=4,'core'=2,'z'=16,'x_lo'=2] {'x_lo','x_hi','y','core'}, dimensions={0} | all-to-all | bytes 524288 | tf_op jit(solution)/shard_map/all_to_all | solution.py:20
  161.4 15.9 %all_to_all.27 = f32[16,8,256]{2,1,0:T(8,128)S(1)} all-to-all(f32[16,8,256]{2,1,0:T(8,128)S(1)} %broadcast_in_dim.10), channel_id=1, replica_groups=mesh['x_hi'=2,'y'=4,'core'=2,'z'=16,'x_lo'=2] {'z'}, dimensions={0} | all-to-all | bytes 262144 | tf_op jit(solution)/shard_map/all_to_all | solution.py:20
  177.4 15.7 %all_to_all.28 = f32[32,8,256]{2,1,0:T(8,128)} all-to-all(f32[32,8,256]{2,1,0:T(8,128)S(1)} %broadcast_in_dim.11), channel_id=1, replica_groups=mesh['x_hi'=2,'y'=4,'core'=2,'z'=16,'x_lo'=2] {'x_lo','x_hi','y','core'}, dimensions={0} | all-to-all | bytes 524288 | tf_op jit(solution)/shard_map/all_to_all | solution.py:20
  193.1 10.4 %shard_map.37 = f32[32,256]{1,0:T(8,128)} custom-call(f32[256,256]{1,0:T(8,128)} %bitcast.41, f32[32,256]{1,0:T(8,128)} %copy-done.2), custom_call_target="tpu_custom_call" | custom-call | tf_op jit(solution)/shard_map/pallas_call | solution.py:144
  (43 shorter events, 0.7 us)
Async XLA Ops:
  3.7 11.4 %copy-start.1 = (bf16[32,2048]{1,0:T(8,128)(2,1)S(1)}, bf16[32,2048]{1,0:T(8,128)(2,1)}, u32[]{:S(2)}) copy-start(bf16[32,2048]{1,0:T(8,128)(2,1)} %param.3) | copy-start | bytes 393220
  3.7 21.8 %copy-start = (bf16[1024,512]{1,0:T(8,128)(2,1)S(1)}, bf16[1024,512]{1,0:T(8,128)(2,1)}, u32[]{:S(2)}) copy-start(bf16[1024,512]{1,0:T(8,128)(2,1)} %param.4) | copy-start | bytes 3145732
  3.7 110.4 %all-to-all-start = ((bf16[32,32,2304]{2,1,0:T(8,128)(2,1)}), bf16[32,32,2304]{2,1,0:T(8,128)(2,1)}, u32[]{:S(2)}, u32[]{:S(2)}) async-start(bf16[32,32,2304]{2,1,0:T(8,128)(2,1)} %broadcast_in_dim.9), calls=%async_computation | async-start | bytes 9437184 | tf_op jit(solution)/shard_map/all_to_all | solution.py:20
  15.1 14.9 %collective-permute-start.1 = (bf16[32,2048]{1,0:T(8,128)(2,1)S(1)}, bf16[32,2048]{1,0:T(8,128)(2,1)S(1)}, u32[]{:S(2)}, u32[]{:S(2)}) collective-permute-start(bf16[32,2048]{1,0:T(8,128)(2,1)S(1)} %copy-done.1), channel_id=1, source_target_pairs={{0,30},{2,0},{4,2},{6,4},{8,6},{10,8},{12,10},{14,12},{16,14},{18,... | collective-permute-start | bytes 393224 | tf_op jit(solution)/shard_map/ppermute | solution.py:40
  23.6 11.0 %collective-permute-start.2 = (bf16[32,2048]{1,0:T(8,128)(2,1)S(1)}, bf16[32,2048]{1,0:T(8,128)(2,1)S(1)}, u32[]{:S(2)}, u32[]{:S(2)}) collective-permute-start(bf16[32,2048]{1,0:T(8,128)(2,1)S(1)} %copy-done.1), channel_id=1, source_target_pairs={{0,2},{2,4},{4,6},{6,8},{8,10},{10,12},{12,14},{14,16},{16,18},{18... | collective-permute-start | bytes 393224 | tf_op jit(solution)/shard_map/ppermute | solution.py:38
  26.4 57.5 %collective-permute-start = (bf16[16,32,512]{2,1,0:T(8,128)(2,1)}, bf16[16,32,512]{2,1,0:T(8,128)(2,1)}, u32[]{:S(2)}, u32[]{:S(2)}) collective-permute-start(bf16[16,32,512]{2,1,0:T(8,128)(2,1)} %select_bitcast_fusion), channel_id=1, source_target_pairs={{0,1},{1,0},{2,3},{3,2},{4,5},{5,4},{6,7},{7,6},{8,9},{9,8},{10,11... | collective-permute-start | bytes 1572872 | tf_op jit(solution)/shard_map/ppermute | solution.py:52
  30.0 6.6 %collective-permute-start.3 = (bf16[32,2048]{1,0:T(8,128)(2,1)S(1)}, bf16[32,2048]{1,0:T(8,128)(2,1)S(1)}, u32[]{:S(2)}, u32[]{:S(2)}) collective-permute-start(bf16[32,2048]{1,0:T(8,128)(2,1)S(1)} %collective-permute-done.1), channel_id=1, source_target_pairs={{0,30},{2,0},{4,2},{6,4},{8,6},{10,8},{12,10},{14,12},{16,14},{18,... | collective-permute-start | bytes 393224 | tf_op jit(solution)/shard_map/ppermute | solution.py:40
  34.6 7.3 %collective-permute-start.4 = (bf16[32,2048]{1,0:T(8,128)(2,1)S(1)}, bf16[32,2048]{1,0:T(8,128)(2,1)S(1)}, u32[]{:S(2)}, u32[]{:S(2)}) collective-permute-start(bf16[32,2048]{1,0:T(8,128)(2,1)S(1)} %collective-permute-done.2), channel_id=1, source_target_pairs={{0,2},{2,4},{4,6},{6,8},{8,10},{10,12},{12,14},{14,16},{16,18},{18... | collective-permute-start | bytes 393224 | tf_op jit(solution)/shard_map/ppermute | solution.py:38
  36.6 7.3 %collective-permute-start.5 = (bf16[32,2048]{1,0:T(8,128)(2,1)S(1)}, bf16[32,2048]{1,0:T(8,128)(2,1)S(1)}, u32[]{:S(2)}, u32[]{:S(2)}) collective-permute-start(bf16[32,2048]{1,0:T(8,128)(2,1)S(1)} %collective-permute-done.3), channel_id=1, source_target_pairs={{0,30},{2,0},{4,2},{6,4},{8,6},{10,8},{12,10},{14,12},{16,14},{18,... | collective-permute-start | bytes 393224 | tf_op jit(solution)/shard_map/ppermute | solution.py:40
  41.9 7.3 %collective-permute-start.6 = (bf16[32,2048]{1,0:T(8,128)(2,1)S(1)}, bf16[32,2048]{1,0:T(8,128)(2,1)S(1)}, u32[]{:S(2)}, u32[]{:S(2)}) collective-permute-start(bf16[32,2048]{1,0:T(8,128)(2,1)S(1)} %collective-permute-done.4), channel_id=1, source_target_pairs={{0,2},{2,4},{4,6},{6,8},{8,10},{10,12},{12,14},{14,16},{16,18},{18... | collective-permute-start | bytes 393224 | tf_op jit(solution)/shard_map/ppermute | solution.py:38
  43.9 7.3 %collective-permute-start.7 = (bf16[32,2048]{1,0:T(8,128)(2,1)S(1)}, bf16[32,2048]{1,0:T(8,128)(2,1)S(1)}, u32[]{:S(2)}, u32[]{:S(2)}) collective-permute-start(bf16[32,2048]{1,0:T(8,128)(2,1)S(1)} %collective-permute-done.5), channel_id=1, source_target_pairs={{0,30},{2,0},{4,2},{6,4},{8,6},{10,8},{12,10},{14,12},{16,14},{18,... | collective-permute-start | bytes 393224 | tf_op jit(solution)/shard_map/ppermute | solution.py:40
  49.2 7.3 %collective-permute-start.8 = (bf16[32,2048]{1,0:T(8,128)(2,1)S(1)}, bf16[32,2048]{1,0:T(8,128)(2,1)S(1)}, u32[]{:S(2)}, u32[]{:S(2)}) collective-permute-start(bf16[32,2048]{1,0:T(8,128)(2,1)S(1)} %collective-permute-done.6), channel_id=1, source_target_pairs={{0,2},{2,4},{4,6},{6,8},{8,10},{10,12},{12,14},{14,16},{16,18},{18... | collective-permute-start | bytes 393224 | tf_op jit(solution)/shard_map/ppermute | solution.py:38
  51.2 33.9 %collective-permute-start.9 = (bf16[32,2048]{1,0:T(8,128)(2,1)S(1)}, bf16[32,2048]{1,0:T(8,128)(2,1)S(1)}, u32[]{:S(2)}, u32[]{:S(2)}) collective-permute-start(bf16[32,2048]{1,0:T(8,128)(2,1)S(1)} %collective-permute-done.7), channel_id=1, source_target_pairs={{0,30},{2,0},{4,2},{6,4},{8,6},{10,8},{12,10},{14,12},{16,14},{18,... | collective-permute-start | bytes 393224 | tf_op jit(solution)/shard_map/ppermute | solution.py:40
  56.5 36.8 %collective-permute-start.10 = (bf16[32,2048]{1,0:T(8,128)(2,1)S(1)}, bf16[32,2048]{1,0:T(8,128)(2,1)S(1)}, u32[]{:S(2)}, u32[]{:S(2)}) collective-permute-start(bf16[32,2048]{1,0:T(8,128)(2,1)S(1)} %collective-permute-done.8), channel_id=1, source_target_pairs={{0,2},{2,4},{4,6},{6,8},{8,10},{10,12},{12,14},{14,16},{16,18},{18... | collective-permute-start | bytes 393224 | tf_op jit(solution)/shard_map/ppermute | solution.py:38
  85.1 10.2 %collective-permute-start.11 = (bf16[32,2048]{1,0:T(8,128)(2,1)S(1)}, bf16[32,2048]{1,0:T(8,128)(2,1)S(1)}, u32[]{:S(2)}, u32[]{:S(2)}) collective-permute-start(bf16[32,2048]{1,0:T(8,128)(2,1)S(1)} %collective-permute-done.9), channel_id=1, source_target_pairs={{0,30},{2,0},{4,2},{6,4},{8,6},{10,8},{12,10},{14,12},{16,14},{18,... | collective-permute-start | bytes 393224 | tf_op jit(solution)/shard_map/ppermute | solution.py:40
  93.3 6.9 %collective-permute-start.12 = (bf16[32,2048]{1,0:T(8,128)(2,1)S(1)}, bf16[32,2048]{1,0:T(8,128)(2,1)S(1)}, u32[]{:S(2)}, u32[]{:S(2)}) collective-permute-start(bf16[32,2048]{1,0:T(8,128)(2,1)S(1)} %collective-permute-done.10), channel_id=1, source_target_pairs={{0,2},{2,4},{4,6},{6,8},{8,10},{10,12},{12,14},{14,16},{16,18},{18... | collective-permute-start | bytes 393224 | tf_op jit(solution)/shard_map/ppermute | solution.py:38
  95.3 13.8 %collective-permute-start.13 = (bf16[32,2048]{1,0:T(8,128)(2,1)S(1)}, bf16[32,2048]{1,0:T(8,128)(2,1)S(1)}, u32[]{:S(2)}, u32[]{:S(2)}) collective-permute-start(bf16[32,2048]{1,0:T(8,128)(2,1)S(1)} %collective-permute-done.11), channel_id=1, source_target_pairs={{0,30},{2,0},{4,2},{6,4},{8,6},{10,8},{12,10},{14,12},{16,14},{18,... | collective-permute-start | bytes 393224 | tf_op jit(solution)/shard_map/ppermute | solution.py:40
  100.2 6.9 %collective-permute-start.14 = (bf16[32,2048]{1,0:T(8,128)(2,1)S(1)}, bf16[32,2048]{1,0:T(8,128)(2,1)S(1)}, u32[]{:S(2)}, u32[]{:S(2)}) collective-permute-start(bf16[32,2048]{1,0:T(8,128)(2,1)S(1)} %collective-permute-done.12), channel_id=1, source_target_pairs={{0,2},{2,4},{4,6},{6,8},{8,10},{10,12},{12,14},{14,16},{16,18},{18... | collective-permute-start | bytes 393224 | tf_op jit(solution)/shard_map/ppermute | solution.py:38
  107.1 6.9 %collective-permute-start.15 = (bf16[32,2048]{1,0:T(8,128)(2,1)S(1)}, bf16[32,2048]{1,0:T(8,128)(2,1)S(1)}, u32[]{:S(2)}, u32[]{:S(2)}) collective-permute-start(bf16[32,2048]{1,0:T(8,128)(2,1)S(1)} %collective-permute-done.14), channel_id=1, source_target_pairs={{0,2},{2,4},{4,6},{6,8},{8,10},{10,12},{12,14},{14,16},{16,18},{18... | collective-permute-start | bytes 393224 | tf_op jit(solution)/shard_map/ppermute | solution.py:38
  137.9 55.2 %copy-start.2 = (f32[32,256]{1,0:T(8,128)}, f32[32,256]{1,0:T(8,128)S(1)}, u32[]{:S(2)}) copy-start(f32[32,256]{1,0:T(8,128)S(1)} %convert_reduce_fusion.images_ref) | copy-start | bytes 98308

commit v5 on v4

--- a/solution.py
+++ b/solution.py
@@ -25,6 +25,10 @@
     return exchange(copies, axes)
 
 
+def after(value, *others):
+    return lax.optimization_barrier((value,) + others)[0]
+
+
 def gather_z(mine):
     n = lax.axis_size("z")
     z = lax.axis_index("z")
@@ -39,17 +43,19 @@
         if step < n // 2:
             behind = lax.ppermute(behind, "z", down)
             block = lax.dynamic_update_slice(block, behind, (((z + step) & (n - 1)) * rows, 0))
+            late = behind
         block = lax.dynamic_update_slice(block, ahead, (((z - step) & (n - 1)) * rows, 0))
-    return block
+    return block, late
 
 
-def swap_sides(coulomb, count):
+def swap_sides(coulomb, count, late):
     side = lax.axis_index("x_lo")
     halves = coulomb.reshape(-1, 2, count, coulomb.shape[1])
     first, second = halves[:, 0], halves[:, 1]
     low = side == 0
     kept = jnp.where(low, first, second)
     moved = lax.ppermute(jnp.where(low, second, first), "x_lo", [(0, 1), (1, 0)])
+    moved = after(moved, late)
     left, right = jnp.where(low, kept, moved), jnp.where(low, moved, kept)
     return jnp.concatenate([left, right], axis=-1).reshape(-1, 2 * coulomb.shape[1])
 
@@ -157,8 +163,8 @@
     width = orbitals.shape[1]
     paired = spread(jnp.concatenate([orbitals, applied], axis=1), PLANE)
     paired = paired.reshape(-1, paired.shape[-1])
-    tile = swap_sides(coulomb, orbitals.shape[0])
-    points = gather_z(orbitals)
+    points, late = gather_z(orbitals)
+    tile = swap_sides(coulomb, orbitals.shape[0], late)
     density = jnp.einsum(
         "ik,jk->ij", points, paired[:, :width], preferred_element_type=jnp.float32
     )

time: 204 us -> 187 us (0.917)
  waiting for transfers between devices: 35.3 us -> 18.7 us
  starting transfers between devices: 72 us -> 69.5 us
    ppermute x1, waiting for transfers between devices: 25.3 us -> 10.7 us  [swap_sides(): lax.ppermute(jnp.where(low, second, first), 'x_lo', [(0, 1), (1, 0)])]
    ppermute x7, starting transfers between devices: 42 us -> 39.6 us  [gather_z(): behind = lax.ppermute(behind, 'z', down)]
  transfers between devices with their start and end apart: 17 -> 17, of which waited for: 3 -> 2; matrix products, arithmetic and copies ran while one was open for 1% -> 1% of each run, Pallas kernels for 0% -> 0%
where the time goes in v5:
time: 187 us; the launch traced here: 186 us
  blocking collectives  74.9 us (40%)
  starting transfers between devices  69.5 us (37%)
  waiting for transfers between devices  18.7 us (10%)
  Pallas kernels  10.4 us (6%)
  matrix products  5.41 us (3%)
  local copies, waits for them, and re-layouts  3.38 us (2%)
  other arithmetic  3.14 us (2%)
    all_to_all x4, blocking collectives, exchange(): return lax.all_to_all(chunks, axes, 0, 0, tiled=True)  74.9 us
    ppermute x7, starting transfers between devices, gather_z(): behind = lax.ppermute(behind, 'z', down)  39.6 us
    ppermute x8, starting transfers between devices, gather_z(): ahead = lax.ppermute(ahead, 'z', up)  15.3 us
    all_to_all x1, starting transfers between devices, exchange(): return lax.all_to_all(chunks, axes, 0, 0, tiled=True)  11.4 us
    ppermute x1, waiting for transfers between devices, swap_sides(): lax.ppermute(jnp.where(low, second, first), 'x_lo', [(0, 1), (1, 0)])  10.7 us
    pallas_call x1, Pallas kernels, orthonormalize(): pl.pallas_call(functools.partial(orthonormalize_kernel, 64, 8), out_shape...  10.4 us
    ppermute x8, waiting for transfers between devices, gather_z(): ahead = lax.ppermute(ahead, 'z', up)  7.93 us
    dot_general x1, matrix products, per_device(): jnp.dot(kernel, paired[:, width:], preferred_element_type=jnp.float32)  5.07 us
  transfers between devices with their start and end apart: 17, of which 2 were waited for; matrix products, arithmetic and copies ran while one was open for 1% of the time, Pallas kernels for 0%

profile of v5, /device:TPU:1, one launch (start us, length us, event | category | flops | bytes accessed | tf_op | source)
XLA Modules:
  0.0 186.0 jit_solution(14365056821465805963)
XLA Ops:
  0.0 0.9 pad_maximum_fusion.1
  0.9 2.7 %broadcast_in_dim.9 = bf16[32,32,2304]{2,1,0:T(8,128)(2,1)} broadcast(bf16[32,2304]{1,0:T(8,128)(2,1)S(1)} %pad_maximum_fusion.1), dimensions={1,2} | broadcast | bytes 4866048 | tf_op jit(solution)/shard_map/broadcast_in_dim | solution.py:24
  3.7 11.4 %all-to-all-start = ((bf16[32,32,2304]{2,1,0:T(8,128)(2,1)}), bf16[32,32,2304]{2,1,0:T(8,128)(2,1)}, u32[]{:S(2)}, u32[]{:S(2)}) async-start(bf16[32,32,2304]{2,1,0:T(8,128)(2,1)} %broadcast_in_dim.9), calls=%async_computation | async-start | bytes 9437184 | tf_op jit(solution)/shard_map/all_to_all | solution.py:20
  15.1 8.5 %collective-permute-start.1 = (bf16[32,2048]{1,0:T(8,128)(2,1)S(1)}, bf16[32,2048]{1,0:T(8,128)(2,1)S(1)}, u32[]{:S(2)}, u32[]{:S(2)}) collective-permute-start(bf16[32,2048]{1,0:T(8,128)(2,1)S(1)} %copy-done.1), channel_id=1, source_target_pairs={{0,30},{2,0},{4,2},{6,4},{8,6},{10,8},{12,10},{14,12},{16,14},{18,... | collective-permute-start | bytes 393224 | tf_op jit(solution)/shard_map/ppermute | solution.py:44
  23.6 1.9 %collective-permute-start.8 = (bf16[32,2048]{1,0:T(8,128)(2,1)S(1)}, bf16[32,2048]{1,0:T(8,128)(2,1)S(1)}, u32[]{:S(2)}, u32[]{:S(2)}) collective-permute-start(bf16[32,2048]{1,0:T(8,128)(2,1)S(1)} %copy-done.1), channel_id=1, source_target_pairs={{0,2},{2,4},{4,6},{6,8},{8,10},{10,12},{12,14},{14,16},{16,18},{18... | collective-permute-start | bytes 393224 | tf_op jit(solution)/shard_map/ppermute | solution.py:42
  25.5 0.9 select_bitcast_fusion
  26.4 3.3 %collective-permute-start = (bf16[16,32,512]{2,1,0:T(8,128)(2,1)}, bf16[16,32,512]{2,1,0:T(8,128)(2,1)}, u32[]{:S(2)}, u32[]{:S(2)}) collective-permute-start(bf16[16,32,512]{2,1,0:T(8,128)(2,1)} %select_bitcast_fusion), channel_id=1, source_target_pairs={{0,1},{1,0},{2,3},{3,2},{4,5},{5,4},{6,7},{7,6},{8,9},{9,8},{10,11... | collective-permute-start | bytes 1572872 | tf_op jit(solution)/shard_map/ppermute | solution.py:57
  29.7 0.2 broadcast_in_dim.8
  30.0 4.6 %collective-permute-start.2 = (bf16[32,2048]{1,0:T(8,128)(2,1)S(1)}, bf16[32,2048]{1,0:T(8,128)(2,1)S(1)}, u32[]{:S(2)}, u32[]{:S(2)}) collective-permute-start(bf16[32,2048]{1,0:T(8,128)(2,1)S(1)} %collective-permute-done.1), channel_id=1, source_target_pairs={{0,30},{2,0},{4,2},{6,4},{8,6},{10,8},{12,10},{14,12},{16,14},{18,... | collective-permute-start | bytes 393224 | tf_op jit(solution)/shard_map/ppermute | solution.py:44
  34.6 1.9 %collective-permute-start.9 = (bf16[32,2048]{1,0:T(8,128)(2,1)S(1)}, bf16[32,2048]{1,0:T(8,128)(2,1)S(1)}, u32[]{:S(2)}, u32[]{:S(2)}) collective-permute-start(bf16[32,2048]{1,0:T(8,128)(2,1)S(1)} %collective-permute-done.8), channel_id=1, source_target_pairs={{0,2},{2,4},{4,6},{6,8},{8,10},{10,12},{12,14},{14,16},{16,18},{18... | collective-permute-start | bytes 393224 | tf_op jit(solution)/shard_map/ppermute | solution.py:42
  36.6 5.3 %collective-permute-start.3 = (bf16[32,2048]{1,0:T(8,128)(2,1)S(1)}, bf16[32,2048]{1,0:T(8,128)(2,1)S(1)}, u32[]{:S(2)}, u32[]{:S(2)}) collective-permute-start(bf16[32,2048]{1,0:T(8,128)(2,1)S(1)} %collective-permute-done.2), channel_id=1, source_target_pairs={{0,30},{2,0},{4,2},{6,4},{8,6},{10,8},{12,10},{14,12},{16,14},{18,... | collective-permute-start | bytes 393224 | tf_op jit(solution)/shard_map/ppermute | solution.py:44
  41.9 1.9 %collective-permute-start.10 = (bf16[32,2048]{1,0:T(8,128)(2,1)S(1)}, bf16[32,2048]{1,0:T(8,128)(2,1)S(1)}, u32[]{:S(2)}, u32[]{:S(2)}) collective-permute-start(bf16[32,2048]{1,0:T(8,128)(2,1)S(1)} %collective-permute-done.9), channel_id=1, source_target_pairs={{0,2},{2,4},{4,6},{6,8},{8,10},{10,12},{12,14},{14,16},{16,18},{18... | collective-permute-start | bytes 393224 | tf_op jit(solution)/shard_map/ppermute | solution.py:42
  43.9 5.3 %collective-permute-start.4 = (bf16[32,2048]{1,0:T(8,128)(2,1)S(1)}, bf16[32,2048]{1,0:T(8,128)(2,1)S(1)}, u32[]{:S(2)}, u32[]{:S(2)}) collective-permute-start(bf16[32,2048]{1,0:T(8,128)(2,1)S(1)} %collective-permute-done.3), channel_id=1, source_target_pairs={{0,30},{2,0},{4,2},{6,4},{8,6},{10,8},{12,10},{14,12},{16,14},{18,... | collective-permute-start | bytes 393224 | tf_op jit(solution)/shard_map/ppermute | solution.py:44
  49.2 1.9 %collective-permute-start.11 = (bf16[32,2048]{1,0:T(8,128)(2,1)S(1)}, bf16[32,2048]{1,0:T(8,128)(2,1)S(1)}, u32[]{:S(2)}, u32[]{:S(2)}) collective-permute-start(bf16[32,2048]{1,0:T(8,128)(2,1)S(1)} %collective-permute-done.10), channel_id=1, source_target_pairs={{0,2},{2,4},{4,6},{6,8},{8,10},{10,12},{12,14},{14,16},{16,18},{18... | collective-permute-start | bytes 393224 | tf_op jit(solution)/shard_map/ppermute | solution.py:42
  51.2 5.3 %collective-permute-start.5 = (bf16[32,2048]{1,0:T(8,128)(2,1)S(1)}, bf16[32,2048]{1,0:T(8,128)(2,1)S(1)}, u32[]{:S(2)}, u32[]{:S(2)}) collective-permute-start(bf16[32,2048]{1,0:T(8,128)(2,1)S(1)} %collective-permute-done.4), channel_id=1, source_target_pairs={{0,30},{2,0},{4,2},{6,4},{8,6},{10,8},{12,10},{14,12},{16,14},{18,... | collective-permute-start | bytes 393224 | tf_op jit(solution)/shard_map/ppermute | solution.py:44
  56.5 1.9 %collective-permute-start.12 = (bf16[32,2048]{1,0:T(8,128)(2,1)S(1)}, bf16[32,2048]{1,0:T(8,128)(2,1)S(1)}, u32[]{:S(2)}, u32[]{:S(2)}) collective-permute-start(bf16[32,2048]{1,0:T(8,128)(2,1)S(1)} %collective-permute-done.11), channel_id=1, source_target_pairs={{0,2},{2,4},{4,6},{6,8},{8,10},{10,12},{12,14},{14,16},{16,18},{18... | collective-permute-start | bytes 393224 | tf_op jit(solution)/shard_map/ppermute | solution.py:42
  58.5 5.3 %collective-permute-start.6 = (bf16[32,2048]{1,0:T(8,128)(2,1)S(1)}, bf16[32,2048]{1,0:T(8,128)(2,1)S(1)}, u32[]{:S(2)}, u32[]{:S(2)}) collective-permute-start(bf16[32,2048]{1,0:T(8,128)(2,1)S(1)} %collective-permute-done.5), channel_id=1, source_target_pairs={{0,30},{2,0},{4,2},{6,4},{8,6},{10,8},{12,10},{14,12},{16,14},{18,... | collective-permute-start | bytes 393224 | tf_op jit(solution)/shard_map/ppermute | solution.py:44
  63.9 1.9 %collective-permute-start.13 = (bf16[32,2048]{1,0:T(8,128)(2,1)S(1)}, bf16[32,2048]{1,0:T(8,128)(2,1)S(1)}, u32[]{:S(2)}, u32[]{:S(2)}) collective-permute-start(bf16[32,2048]{1,0:T(8,128)(2,1)S(1)} %collective-permute-done.12), channel_id=1, source_target_pairs={{0,2},{2,4},{4,6},{6,8},{8,10},{10,12},{12,14},{14,16},{16,18},{18... | collective-permute-start | bytes 393224 | tf_op jit(solution)/shard_map/ppermute | solution.py:42
  65.8 5.3 %collective-permute-start.7 = (bf16[32,2048]{1,0:T(8,128)(2,1)S(1)}, bf16[32,2048]{1,0:T(8,128)(2,1)S(1)}, u32[]{:S(2)}, u32[]{:S(2)}) collective-permute-start(bf16[32,2048]{1,0:T(8,128)(2,1)S(1)} %collective-permute-done.6), channel_id=1, source_target_pairs={{0,30},{2,0},{4,2},{6,4},{8,6},{10,8},{12,10},{14,12},{16,14},{18,... | collective-permute-start | bytes 393224 | tf_op jit(solution)/shard_map/ppermute | solution.py:44
  71.2 1.9 %collective-permute-start.14 = (bf16[32,2048]{1,0:T(8,128)(2,1)S(1)}, bf16[32,2048]{1,0:T(8,128)(2,1)S(1)}, u32[]{:S(2)}, u32[]{:S(2)}) collective-permute-start(bf16[32,2048]{1,0:T(8,128)(2,1)S(1)} %collective-permute-done.13), channel_id=1, source_target_pairs={{0,2},{2,4},{4,6},{6,8},{8,10},{10,12},{12,14},{14,16},{16,18},{18... | collective-permute-start | bytes 393224 | tf_op jit(solution)/shard_map/ppermute | solution.py:42
  73.1 10.7 %collective-permute-done = bf16[16,32,512]{2,1,0:T(8,128)(2,1)} collective-permute-done((bf16[16,32,512]{2,1,0:T(8,128)(2,1)}, bf16[16,32,512]{2,1,0:T(8,128)(2,1)}, u32[]{:S(2)}, u32[]{:S(2)}) %collective-permute-start) | collective-permute-done | bytes 524320 | tf_op jit(solution)/shard_map/ppermute | solution.py:57
  83.9 1.9 %collective-permute-start.15 = (bf16[32,2048]{1,0:T(8,128)(2,1)S(1)}, bf16[32,2048]{1,0:T(8,128)(2,1)S(1)}, u32[]{:S(2)}, u32[]{:S(2)}) collective-permute-start(bf16[32,2048]{1,0:T(8,128)(2,1)S(1)} %collective-permute-done.14), channel_id=1, source_target_pairs={{0,2},{2,4},{4,6},{6,8},{8,10},{10,12},{12,14},{14,16},{16,18},{18... | collective-permute-start | bytes 393224 | tf_op jit(solution)/shard_map/ppermute | solution.py:42
  85.8 1.1 bitcast_select_fusion.1
  87.0 0.1 pad_maximum_fusion
  87.1 7.8 %collective-permute-done.15 = bf16[32,2048]{1,0:T(8,128)(2,1)S(1)} collective-permute-done((bf16[32,2048]{1,0:T(8,128)(2,1)S(1)}, bf16[32,2048]{1,0:T(8,128)(2,1)S(1)}, u32[]{:S(2)}, u32[]{:S(2)}) %collective-permute-start.15) | collective-permute-done | bytes 131104 | tf_op jit(solution)/shard_map/ppermute | solution.py:42
  94.9 5.1 %convolution_convert_fusion = bf16[512,256]{1,0:T(8,128)(2,1)S(1)} fusion(bf16[512,1024]{1,0:T(8,128)(2,1)S(1)} %bitcast.42, bf16[512,2048]{1,0:T(8,128)(2,1)S(1)} %constant_dynamic-update-slice_fusion, bf16[1024,2304]{1,0:T(8,128)(2,1)} %bitcast.4), kind=kOutput, calls=%fused_computation.4 | convolution fusion | flops 2417623040 | bytes 8126464 | tf_op jit(solution)/shard_map/dot_general | solution.py:173
  100.0 20.3 %all_to_all.25 = bf16[16,32,256]{2,1,0:T(8,128)(2,1)S(1)} all-to-all(bf16[16,32,256]{2,1,0:T(8,128)(2,1)S(1)} %bitcast.44), channel_id=1, replica_groups=mesh['x_hi'=2,'y'=4,'core'=2,'z'=16,'x_lo'=2] {'z'}, dimensions={0} | all-to-all | bytes 524288 | tf_op jit(solution)/shard_map/all_to_all | solution.py:20
  120.5 0.3 fusion.8
  120.9 21.8 %all_to_all.26 = f32[32,8,256]{2,1,0:T(8,128)S(1)} all-to-all(f32[32,8,256]{2,1,0:T(8,128)S(1)} %fusion.8), channel_id=1, replica_groups=mesh['x_hi'=2,'y'=4,'core'=2,'z'=16,'x_lo'=2] {'x_lo','x_hi','y','core'}, dimensions={0} | all-to-all | bytes 524288 | tf_op jit(solution)/shard_map/all_to_all | solution.py:20
  142.7 17.1 %all_to_all.27 = f32[16,8,256]{2,1,0:T(8,128)S(1)} all-to-all(f32[16,8,256]{2,1,0:T(8,128)S(1)} %broadcast_in_dim.10), channel_id=1, replica_groups=mesh['x_hi'=2,'y'=4,'core'=2,'z'=16,'x_lo'=2] {'z'}, dimensions={0} | all-to-all | bytes 262144 | tf_op jit(solution)/shard_map/all_to_all | solution.py:20
  159.9 15.7 %all_to_all.28 = f32[32,8,256]{2,1,0:T(8,128)} all-to-all(f32[32,8,256]{2,1,0:T(8,128)S(1)} %broadcast_in_dim.11), channel_id=1, replica_groups=mesh['x_hi'=2,'y'=4,'core'=2,'z'=16,'x_lo'=2] {'x_lo','x_hi','y','core'}, dimensions={0} | all-to-all | bytes 524288 | tf_op jit(solution)/shard_map/all_to_all | solution.py:20
  175.6 10.4 %shard_map.37 = f32[32,256]{1,0:T(8,128)} custom-call(f32[256,256]{1,0:T(8,128)} %bitcast.41, f32[32,256]{1,0:T(8,128)} %copy-done.2), custom_call_target="tpu_custom_call" | custom-call | tf_op jit(solution)/shard_map/pallas_call | solution.py:150
  (43 shorter events, 0.6 us)
Async XLA Ops:
  3.7 11.4 %copy-start.1 = (bf16[32,2048]{1,0:T(8,128)(2,1)S(1)}, bf16[32,2048]{1,0:T(8,128)(2,1)}, u32[]{:S(2)}) copy-start(bf16[32,2048]{1,0:T(8,128)(2,1)} %param.3) | copy-start | bytes 393220
  3.7 21.8 %copy-start = (bf16[1024,512]{1,0:T(8,128)(2,1)S(1)}, bf16[1024,512]{1,0:T(8,128)(2,1)}, u32[]{:S(2)}) copy-start(bf16[1024,512]{1,0:T(8,128)(2,1)} %param.4) | copy-start | bytes 3145732
  3.7 91.3 %all-to-all-start = ((bf16[32,32,2304]{2,1,0:T(8,128)(2,1)}), bf16[32,32,2304]{2,1,0:T(8,128)(2,1)}, u32[]{:S(2)}, u32[]{:S(2)}) async-start(bf16[32,32,2304]{2,1,0:T(8,128)(2,1)} %broadcast_in_dim.9), calls=%async_computation | async-start | bytes 9437184 | tf_op jit(solution)/shard_map/all_to_all | solution.py:20
  15.1 14.9 %collective-permute-start.1 = (bf16[32,2048]{1,0:T(8,128)(2,1)S(1)}, bf16[32,2048]{1,0:T(8,128)(2,1)S(1)}, u32[]{:S(2)}, u32[]{:S(2)}) collective-permute-start(bf16[32,2048]{1,0:T(8,128)(2,1)S(1)} %copy-done.1), channel_id=1, source_target_pairs={{0,30},{2,0},{4,2},{6,4},{8,6},{10,8},{12,10},{14,12},{16,14},{18,... | collective-permute-start | bytes 393224 | tf_op jit(solution)/shard_map/ppermute | solution.py:44
  23.6 11.0 %collective-permute-start.8 = (bf16[32,2048]{1,0:T(8,128)(2,1)S(1)}, bf16[32,2048]{1,0:T(8,128)(2,1)S(1)}, u32[]{:S(2)}, u32[]{:S(2)}) collective-permute-start(bf16[32,2048]{1,0:T(8,128)(2,1)S(1)} %copy-done.1), channel_id=1, source_target_pairs={{0,2},{2,4},{4,6},{6,8},{8,10},{10,12},{12,14},{14,16},{16,18},{18... | collective-permute-start | bytes 393224 | tf_op jit(solution)/shard_map/ppermute | solution.py:42
  26.4 57.5 %collective-permute-start = (bf16[16,32,512]{2,1,0:T(8,128)(2,1)}, bf16[16,32,512]{2,1,0:T(8,128)(2,1)}, u32[]{:S(2)}, u32[]{:S(2)}) collective-permute-start(bf16[16,32,512]{2,1,0:T(8,128)(2,1)} %select_bitcast_fusion), channel_id=1, source_target_pairs={{0,1},{1,0},{2,3},{3,2},{4,5},{5,4},{6,7},{7,6},{8,9},{9,8},{10,11... | collective-permute-start | bytes 1572872 | tf_op jit(solution)/shard_map/ppermute | solution.py:57
  30.0 6.6 %collective-permute-start.2 = (bf16[32,2048]{1,0:T(8,128)(2,1)S(1)}, bf16[32,2048]{1,0:T(8,128)(2,1)S(1)}, u32[]{:S(2)}, u32[]{:S(2)}) collective-permute-start(bf16[32,2048]{1,0:T(8,128)(2,1)S(1)} %collective-permute-done.1), channel_id=1, source_target_pairs={{0,30},{2,0},{4,2},{6,4},{8,6},{10,8},{12,10},{14,12},{16,14},{18,... | collective-permute-start | bytes 393224 | tf_op jit(solution)/shard_map/ppermute | solution.py:44
  34.6 7.3 %collective-permute-start.9 = (bf16[32,2048]{1,0:T(8,128)(2,1)S(1)}, bf16[32,2048]{1,0:T(8,128)(2,1)S(1)}, u32[]{:S(2)}, u32[]{:S(2)}) collective-permute-start(bf16[32,2048]{1,0:T(8,128)(2,1)S(1)} %collective-permute-done.8), channel_id=1, source_target_pairs={{0,2},{2,4},{4,6},{6,8},{8,10},{10,12},{12,14},{14,16},{16,18},{18... | collective-permute-start | bytes 393224 | tf_op jit(solution)/shard_map/ppermute | solution.py:42
  36.6 7.3 %collective-permute-start.3 = (bf16[32,2048]{1,0:T(8,128)(2,1)S(1)}, bf16[32,2048]{1,0:T(8,128)(2,1)S(1)}, u32[]{:S(2)}, u32[]{:S(2)}) collective-permute-start(bf16[32,2048]{1,0:T(8,128)(2,1)S(1)} %collective-permute-done.2), channel_id=1, source_target_pairs={{0,30},{2,0},{4,2},{6,4},{8,6},{10,8},{12,10},{14,12},{16,14},{18,... | collective-permute-start | bytes 393224 | tf_op jit(solution)/shard_map/ppermute | solution.py:44
  41.9 7.3 %collective-permute-start.10 = (bf16[32,2048]{1,0:T(8,128)(2,1)S(1)}, bf16[32,2048]{1,0:T(8,128)(2,1)S(1)}, u32[]{:S(2)}, u32[]{:S(2)}) collective-permute-start(bf16[32,2048]{1,0:T(8,128)(2,1)S(1)} %collective-permute-done.9), channel_id=1, source_target_pairs={{0,2},{2,4},{4,6},{6,8},{8,10},{10,12},{12,14},{14,16},{16,18},{18... | collective-permute-start | bytes 393224 | tf_op jit(solution)/shard_map/ppermute | solution.py:42
  43.9 7.3 %collective-permute-start.4 = (bf16[32,2048]{1,0:T(8,128)(2,1)S(1)}, bf16[32,2048]{1,0:T(8,128)(2,1)S(1)}, u32[]{:S(2)}, u32[]{:S(2)}) collective-permute-start(bf16[32,2048]{1,0:T(8,128)(2,1)S(1)} %collective-permute-done.3), channel_id=1, source_target_pairs={{0,30},{2,0},{4,2},{6,4},{8,6},{10,8},{12,10},{14,12},{16,14},{18,... | collective-permute-start | bytes 393224 | tf_op jit(solution)/shard_map/ppermute | solution.py:44
  49.2 7.3 %collective-permute-start.11 = (bf16[32,2048]{1,0:T(8,128)(2,1)S(1)}, bf16[32,2048]{1,0:T(8,128)(2,1)S(1)}, u32[]{:S(2)}, u32[]{:S(2)}) collective-permute-start(bf16[32,2048]{1,0:T(8,128)(2,1)S(1)} %collective-permute-done.10), channel_id=1, source_target_pairs={{0,2},{2,4},{4,6},{6,8},{8,10},{10,12},{12,14},{14,16},{16,18},{18... | collective-permute-start | bytes 393224 | tf_op jit(solution)/shard_map/ppermute | solution.py:42
  51.2 7.3 %collective-permute-start.5 = (bf16[32,2048]{1,0:T(8,128)(2,1)S(1)}, bf16[32,2048]{1,0:T(8,128)(2,1)S(1)}, u32[]{:S(2)}, u32[]{:S(2)}) collective-permute-start(bf16[32,2048]{1,0:T(8,128)(2,1)S(1)} %collective-permute-done.4), channel_id=1, source_target_pairs={{0,30},{2,0},{4,2},{6,4},{8,6},{10,8},{12,10},{14,12},{16,14},{18,... | collective-permute-start | bytes 393224 | tf_op jit(solution)/shard_map/ppermute | solution.py:44
  56.5 7.3 %collective-permute-start.12 = (bf16[32,2048]{1,0:T(8,128)(2,1)S(1)}, bf16[32,2048]{1,0:T(8,128)(2,1)S(1)}, u32[]{:S(2)}, u32[]{:S(2)}) collective-permute-start(bf16[32,2048]{1,0:T(8,128)(2,1)S(1)} %collective-permute-done.11), channel_id=1, source_target_pairs={{0,2},{2,4},{4,6},{6,8},{8,10},{10,12},{12,14},{14,16},{16,18},{18... | collective-permute-start | bytes 393224 | tf_op jit(solution)/shard_map/ppermute | solution.py:42
  58.5 7.3 %collective-permute-start.6 = (bf16[32,2048]{1,0:T(8,128)(2,1)S(1)}, bf16[32,2048]{1,0:T(8,128)(2,1)S(1)}, u32[]{:S(2)}, u32[]{:S(2)}) collective-permute-start(bf16[32,2048]{1,0:T(8,128)(2,1)S(1)} %collective-permute-done.5), channel_id=1, source_target_pairs={{0,30},{2,0},{4,2},{6,4},{8,6},{10,8},{12,10},{14,12},{16,14},{18,... | collective-permute-start | bytes 393224 | tf_op jit(solution)/shard_map/ppermute | solution.py:44
  63.9 7.3 %collective-permute-start.13 = (bf16[32,2048]{1,0:T(8,128)(2,1)S(1)}, bf16[32,2048]{1,0:T(8,128)(2,1)S(1)}, u32[]{:S(2)}, u32[]{:S(2)}) collective-permute-start(bf16[32,2048]{1,0:T(8,128)(2,1)S(1)} %collective-permute-done.12), channel_id=1, source_target_pairs={{0,2},{2,4},{4,6},{6,8},{8,10},{10,12},{12,14},{14,16},{16,18},{18... | collective-permute-start | bytes 393224 | tf_op jit(solution)/shard_map/ppermute | solution.py:42
  65.8 18.0 %collective-permute-start.7 = (bf16[32,2048]{1,0:T(8,128)(2,1)S(1)}, bf16[32,2048]{1,0:T(8,128)(2,1)S(1)}, u32[]{:S(2)}, u32[]{:S(2)}) collective-permute-start(bf16[32,2048]{1,0:T(8,128)(2,1)S(1)} %collective-permute-done.6), channel_id=1, source_target_pairs={{0,30},{2,0},{4,2},{6,4},{8,6},{10,8},{12,10},{14,12},{16,14},{18,... | collective-permute-start | bytes 393224 | tf_op jit(solution)/shard_map/ppermute | solution.py:44
  71.2 12.7 %collective-permute-start.14 = (bf16[32,2048]{1,0:T(8,128)(2,1)S(1)}, bf16[32,2048]{1,0:T(8,128)(2,1)S(1)}, u32[]{:S(2)}, u32[]{:S(2)}) collective-permute-start(bf16[32,2048]{1,0:T(8,128)(2,1)S(1)} %collective-permute-done.13), channel_id=1, source_target_pairs={{0,2},{2,4},{4,6},{6,8},{8,10},{10,12},{12,14},{14,16},{16,18},{18... | collective-permute-start | bytes 393224 | tf_op jit(solution)/shard_map/ppermute | solution.py:42
  83.9 11.1 %collective-permute-start.15 = (bf16[32,2048]{1,0:T(8,128)(2,1)S(1)}, bf16[32,2048]{1,0:T(8,128)(2,1)S(1)}, u32[]{:S(2)}, u32[]{:S(2)}) collective-permute-start(bf16[32,2048]{1,0:T(8,128)(2,1)S(1)} %collective-permute-done.14), channel_id=1, source_target_pairs={{0,2},{2,4},{4,6},{6,8},{8,10},{10,12},{12,14},{14,16},{16,18},{18... | collective-permute-start | bytes 393224 | tf_op jit(solution)/shard_map/ppermute | solution.py:42
  120.4 55.2 %copy-start.2 = (f32[32,256]{1,0:T(8,128)}, f32[32,256]{1,0:T(8,128)S(1)}, u32[]{:S(2)}) copy-start(f32[32,256]{1,0:T(8,128)S(1)} %convert_reduce_fusion.images_ref) | copy-start | bytes 98308

commit v6 on v4

--- a/solution.py
+++ b/solution.py
@@ -12,6 +12,7 @@
 ROW = ("x_hi", "y", "core")
 COL = ("z", "x_lo")
 PLANE = ("x_lo",) + ROW
+CHIPS = ("x_lo", "y", "x_hi")
 AXES = ROW + COL
 SIZES = (2, 4, 2, 16, 2)
 
@@ -25,33 +26,57 @@
     return exchange(copies, axes)
 
 
-def gather_z(mine):
+def after(value, *others):
+    return lax.optimization_barrier((value,) + others)[0]
+
+
+def gather_points(orbitals, applied, coulomb):
     n = lax.axis_size("z")
     z = lax.axis_index("z")
-    rows = mine.shape[0]
-    block = jnp.zeros((n * rows, mine.shape[1]), mine.dtype)
-    block = lax.dynamic_update_slice(block, mine, (z * rows, 0))
+    rows, width = orbitals.shape
     up = [(i, (i + 1) % n) for i in range(n)]
     down = [(i, (i - 1) % n) for i in range(n)]
-    ahead, behind = mine, mine
+    mine = jnp.concatenate([orbitals, applied], axis=1)
+    turned = lax.ppermute(mine, ("x_hi", "core"), [(0, 0), (1, 2), (2, 1), (3, 3)])
+    own = spread(turned, CHIPS)
+    kept, moved = swap_sides(coulomb, rows)
+    block = jnp.zeros((n * rows, width), orbitals.dtype)
+    block = lax.dynamic_update_slice(block, orbitals, (z * rows, 0))
+    ahead, behind = orbitals, orbitals
     for step in range(1, n // 2 + 1):
         ahead = lax.ppermute(ahead, "z", up)
         if step < n // 2:
             behind = lax.ppermute(behind, "z", down)
             block = lax.dynamic_update_slice(block, behind, (((z + step) & (n - 1)) * rows, 0))
         block = lax.dynamic_update_slice(block, ahead, (((z - step) & (n - 1)) * rows, 0))
-    return block
+        if step == n // 2 - 2:
+            own = after(own, behind).reshape(-1, width + applied.shape[1])
+            other = lax.ppermute(own, "core", [(0, 1), (1, 0)])
+        if step == n // 2 - 1:
+            other = after(other, behind)
+            moved = after(moved, behind)
+    return block, own, other, order_tile(kept, moved)
 
 
 def swap_sides(coulomb, count):
-    side = lax.axis_index("x_lo")
     halves = coulomb.reshape(-1, 2, count, coulomb.shape[1])
     first, second = halves[:, 0], halves[:, 1]
-    low = side == 0
+    low = lax.axis_index("x_lo") == 0
     kept = jnp.where(low, first, second)
     moved = lax.ppermute(jnp.where(low, second, first), "x_lo", [(0, 1), (1, 0)])
+    return kept, moved
+
+
+def order_tile(kept, moved):
+    low = lax.axis_index("x_lo") == 0
+    same = lax.axis_index("core") == 0
+    half = kept.shape[-1] // 2
     left, right = jnp.where(low, kept, moved), jnp.where(low, moved, kept)
-    return jnp.concatenate([left, right], axis=-1).reshape(-1, 2 * coulomb.shape[1])
+    tiles = []
+    for flag in (same, jnp.logical_not(same)):
+        parts = [jnp.where(flag, x[..., :half], x[..., half:]) for x in (left, right)]
+        tiles.append(jnp.concatenate(parts, axis=-1).reshape(-1, 2 * half))
+    return tiles
 
 
 def reduce_rows(partial):
@@ -155,17 +180,15 @@
 
 def per_device(orbitals, coulomb, applied):
     width = orbitals.shape[1]
-    paired = spread(jnp.concatenate([orbitals, applied], axis=1), PLANE)
-    paired = paired.reshape(-1, paired.shape[-1])
-    tile = swap_sides(coulomb, orbitals.shape[0])
-    points = gather_z(orbitals)
-    density = jnp.einsum(
-        "ik,jk->ij", points, paired[:, :width], preferred_element_type=jnp.float32
-    )
-    kernel = (tile.astype(jnp.float32) * density).astype(jnp.bfloat16)
-    images = reduce_rows(
-        jnp.dot(kernel, paired[:, width:], preferred_element_type=jnp.float32)
-    )
+    points, own, other, tiles = gather_points(orbitals, applied, coulomb)
+    partial = 0.0
+    for theirs, tile in zip((own, other), tiles):
+        density = jnp.einsum(
+            "ik,jk->ij", points, theirs[:, :width], preferred_element_type=jnp.float32
+        )
+        kernel = (tile.astype(jnp.float32) * density).astype(jnp.bfloat16)
+        partial += jnp.dot(kernel, theirs[:, width:], preferred_element_type=jnp.float32)
+    images = reduce_rows(partial)
     local_gram = jnp.einsum("ia,ib->ab", images, images, precision=lax.Precision.HIGHEST)
     return orthonormalize(sum_everywhere(local_gram), images)
 

time: 204 us -> 195 us (0.956)
  waiting for transfers between devices: 35.3 us -> 1.76 us
  local copies, waits for them, and re-layouts: 3.38 us -> 19.5 us
  matrix products: 5.42 us -> 8.22 us
  blocking collectives: 73.3 us -> 75.4 us
    ppermute x1, waiting for transfers between devices: 25.3 us -> 0.01 us  [swap_sides(): lax.ppermute(jnp.where(low, second, first), 'x_lo', [(0, 1), (1, 0)])]
    dynamic_update_slice x16, local copies, waits for them, and re-layouts: 0.27 us -> 16.1 us  [the longest x7 8.39 us: gather_points(): lax.dynamic_update_slice(block, behind, ((z + step & n - 1) * rows, 0))]
    ppermute x15 -> x17, starting transfers between devices: 57.3 us -> 66 us  [the longest x7 39.7 us: gather_points(): behind = lax.ppermute(behind, 'z', down)]
    ppermute x15 -> x17, waiting for transfers between devices: 9.99 us -> 1.75 us  [the longest x8 1.73 us: gather_points(): ahead = lax.ppermute(ahead, 'z', up)]
    all_to_all x1, starting transfers between devices: 11.4 us -> 5.16 us  [exchange(): return lax.all_to_all(chunks, axes, 0, 0, tiled=True)]
    dot_general x1 -> x2, matrix products: 5.07 us -> 7.87 us  [per_device(): jnp.dot(kernel, theirs[:, width:], preferred_element_type=jnp.float32)]
    all_to_all x4, blocking collectives: 73.3 us -> 75.4 us  [exchange(): return lax.all_to_all(chunks, axes, 0, 0, tiled=True)]
  transfers between devices with their start and end apart: 17 -> 19, of which waited for: 3 -> 1; matrix products, arithmetic and copies ran while one was open for 1% -> 14% of each run, Pallas kernels for 0% -> 0%
where the time goes in v6:
time: 195 us; the launch traced here: 193 us
  blocking collectives  75.4 us (39%)
  starting transfers between devices  73.3 us (38%)
  local copies, waits for them, and re-layouts  19.5 us (10%)
  Pallas kernels  10.4 us (5%)
  matrix products  8.22 us (4%)
  other arithmetic  4.41 us (2%)
    all_to_all x4, blocking collectives, exchange(): return lax.all_to_all(chunks, axes, 0, 0, tiled=True)  75.4 us
    ppermute x7, starting transfers between devices, gather_points(): behind = lax.ppermute(behind, 'z', down)  39.7 us
    ppermute x8, starting transfers between devices, gather_points(): ahead = lax.ppermute(ahead, 'z', up)  15.4 us
    pallas_call x1, Pallas kernels, orthonormalize(): pl.pallas_call(functools.partial(orthonormalize_kernel, 64, 8), out_shape...  10.4 us
    dynamic_update_slice x7, local copies, waits for them, and re-layouts, gather_points(): lax.dynamic_update_slice(block, behind, ((z + step & n - 1) * rows, 0))  8.39 us
    dot_general x2, matrix products, per_device(): jnp.dot(kernel, theirs[:, width:], preferred_element_type=jnp.float32)  7.87 us
    dynamic_update_slice x8, local copies, waits for them, and re-layouts, gather_points(): lax.dynamic_update_slice(block, ahead, ((z - step & n - 1) * rows, 0))  7.09 us
    ppermute x1, starting transfers between devices, gather_points(): lax.ppermute(mine, ('x_hi', 'core'), [(0, 0), (1, 2), (2, 1), (3, 3)])  5.49 us
  transfers between devices with their start and end apart: 19, of which 1 were waited for; matrix products, arithmetic and copies ran while one was open for 14% of the time, Pallas kernels for 0%

profile of v6, /device:TPU:1, one launch (start us, length us, event | category | flops | bytes accessed | tf_op | source)
XLA Modules:
  0.0 193.5 jit_solution(8800883287540215220)
XLA Ops:
  0.0 12.1 %collective-permute-start.1 = (bf16[32,2048]{1,0:T(8,128)(2,1)}, bf16[32,2048]{1,0:T(8,128)(2,1)}, u32[]{:S(2)}, u32[]{:S(2)}) collective-permute-start(bf16[32,2048]{1,0:T(8,128)(2,1)} %param.3), channel_id=1, source_target_pairs={{0,30},{2,0},{4,2},{6,4},{8,6},{10,8},{12,10},{14,12},{16,14},{18,... | collective-permute-start | bytes 393224 | tf_op jit(solution)/shard_map/ppermute | solution.py:49
  12.1 1.9 collective-permute-start.8
  15.0 5.5 %collective-permute-start.16 = (bf16[32,2304]{1,0:T(8,128)(2,1)S(1)}, bf16[32,2304]{1,0:T(8,128)(2,1)S(1)}, u32[]{:S(2)}, u32[]{:S(2)}) collective-permute-start(bf16[32,2304]{1,0:T(8,128)(2,1)S(1)} %pad_maximum_fusion.2), channel_id=1, source_target_pairs={{0,0},{32,256},{256,32},{288,288},{1,1},{33,257},{257,33},{289,289... | collective-permute-start | bytes 442376 | tf_op jit(solution)/shard_map/ppermute | solution.py:40
  20.5 2.1 %select_bitcast_fusion = bf16[16,32,512]{2,1,0:T(8,128)(2,1)} fusion(pred[]{:T(512)S(6)} %eq.8, bf16[16,2,32,512]{3,2,1,0:T(8,128)(2,1)} %bitcast.42), kind=kLoop, calls=%fused_computation.20 | loop fusion | flops 262144 | bytes 1572865 | tf_op jit(solution)/shard_map/jit(_where)/select_n | solution.py:66
  22.5 2.2 %collective-permute-start = (bf16[16,32,512]{2,1,0:T(8,128)(2,1)}, bf16[16,32,512]{2,1,0:T(8,128)(2,1)}, u32[]{:S(2)}, u32[]{:S(2)}) collective-permute-start(bf16[16,32,512]{2,1,0:T(8,128)(2,1)} %select_bitcast_fusion), channel_id=1, source_target_pairs={{0,1},{1,0},{2,3},{3,2},{4,5},{5,4},{6,7},{7,6},{8,9},{9,8},{10,11... | collective-permute-start | bytes 1572872 | tf_op jit(solution)/shard_map/ppermute | solution.py:66
  24.8 1.6 broadcast_in_dim.8
  27.1 4.9 %collective-permute-start.2 = (bf16[32,2048]{1,0:T(8,128)(2,1)}, bf16[32,2048]{1,0:T(8,128)(2,1)}, u32[]{:S(2)}, u32[]{:S(2)}) collective-permute-start(bf16[32,2048]{1,0:T(8,128)(2,1)} %collective-permute-done.1), channel_id=1, source_target_pairs={{0,30},{2,0},{4,2},{6,4},{8,6},{10,8},{12,10},{14,12},{16,14},{18,... | collective-permute-start | bytes 393224 | tf_op jit(solution)/shard_map/ppermute | solution.py:49
  31.9 1.9 collective-permute-start.9
  33.9 1.7 broadcast_in_dim.9
  35.6 5.2 %all-to-all-start = ((bf16[16,32,2304]{2,1,0:T(8,128)(2,1)}), bf16[16,32,2304]{2,1,0:T(8,128)(2,1)S(1)}, u32[]{:S(2)}, u32[]{:S(2)}) async-start(bf16[16,32,2304]{2,1,0:T(8,128)(2,1)} %broadcast_in_dim.9), calls=%async_computation | async-start | bytes 4718592 | tf_op jit(solution)/shard_map/all_to_all | solution.py:21
  40.7 1.7 constant_dynamic-update-slice_fusion.14
  43.1 4.6 %collective-permute-start.3 = (bf16[32,2048]{1,0:T(8,128)(2,1)}, bf16[32,2048]{1,0:T(8,128)(2,1)S(1)}, u32[]{:S(2)}, u32[]{:S(2)}) collective-permute-start(bf16[32,2048]{1,0:T(8,128)(2,1)} %collective-permute-done.2), channel_id=1, source_target_pairs={{0,30},{2,0},{4,2},{6,4},{8,6},{10,8},{12,10},{14,12},{16,14},{18,... | collective-permute-start | bytes 393224 | tf_op jit(solution)/shard_map/ppermute | solution.py:49
  47.6 1.9 collective-permute-start.10
  52.7 4.6 %collective-permute-start.4 = (bf16[32,2048]{1,0:T(8,128)(2,1)S(1)}, bf16[32,2048]{1,0:T(8,128)(2,1)S(1)}, u32[]{:S(2)}, u32[]{:S(2)}) collective-permute-start(bf16[32,2048]{1,0:T(8,128)(2,1)S(1)} %collective-permute-done.3), channel_id=1, source_target_pairs={{0,30},{2,0},{4,2},{6,4},{8,6},{10,8},{12,10},{14,12},{16,14},{18,... | collective-permute-start | bytes 393224 | tf_op jit(solution)/shard_map/ppermute | solution.py:49
  57.3 1.9 collective-permute-start.11
  60.6 4.5 %collective-permute-start.5 = (bf16[32,2048]{1,0:T(8,128)(2,1)S(1)}, bf16[32,2048]{1,0:T(8,128)(2,1)S(1)}, u32[]{:S(2)}, u32[]{:S(2)}) collective-permute-start(bf16[32,2048]{1,0:T(8,128)(2,1)S(1)} %collective-permute-done.4), channel_id=1, source_target_pairs={{0,30},{2,0},{4,2},{6,4},{8,6},{10,8},{12,10},{14,12},{16,14},{18,... | collective-permute-start | bytes 393224 | tf_op jit(solution)/shard_map/ppermute | solution.py:49
  65.1 1.9 collective-permute-start.12
  68.4 4.6 %collective-permute-start.6 = (bf16[32,2048]{1,0:T(8,128)(2,1)S(1)}, bf16[32,2048]{1,0:T(8,128)(2,1)}, u32[]{:S(2)}, u32[]{:S(2)}) collective-permute-start(bf16[32,2048]{1,0:T(8,128)(2,1)S(1)} %collective-permute-done.5), channel_id=1, source_target_pairs={{0,30},{2,0},{4,2},{6,4},{8,6},{10,8},{12,10},{14,12},{16,14},{18,... | collective-permute-start | bytes 393224 | tf_op jit(solution)/shard_map/ppermute | solution.py:49
  73.0 1.9 collective-permute-start.13
  76.2 4.6 %collective-permute-start.7 = (bf16[32,2048]{1,0:T(8,128)(2,1)}, bf16[32,2048]{1,0:T(8,128)(2,1)}, u32[]{:S(2)}, u32[]{:S(2)}) collective-permute-start(bf16[32,2048]{1,0:T(8,128)(2,1)} %collective-permute-done.6), channel_id=1, source_target_pairs={{0,30},{2,0},{4,2},{6,4},{8,6},{10,8},{12,10},{14,12},{16,14},{18,... | collective-permute-start | bytes 393224 | tf_op jit(solution)/shard_map/ppermute | solution.py:49
  80.8 1.9 collective-permute-start.14
  82.8 5.4 %collective-permute-start.17 = (bf16[512,2304]{1,0:T(8,128)(2,1)S(1)}, bf16[512,2304]{1,0:T(8,128)(2,1)}, u32[]{:S(2)}, u32[]{:S(2)}) collective-permute-start(bf16[512,2304]{1,0:T(8,128)(2,1)S(1)} %bitcast.44), channel_id=1, source_target_pairs={{0,32},{32,0},{1,33},{33,1},{2,34},{34,2},{3,35},{35,3},{4,36},{36... | collective-permute-start | bytes 7077896 | tf_op jit(solution)/shard_map/ppermute | solution.py:54
  88.2 1.6 constant_dynamic-update-slice_fusion.4
  91.3 1.9 collective-permute-start.15
  96.8 1.7 collective-permute-done.15
  99.2 3.9 %fusion.18 = f32[512,256]{1,0:T(8,128)} fusion(bf16[512,2048]{1,0:T(8,128)(2,1)} %constant_dynamic-update-slice_fusion, bf16[512,2304]{1,0:T(8,128)(2,1)S(1)} %bitcast.45, bf16[512,512]{1,0:T(8,128)(2,1)S(1)} %bitcast.48), kind=kOutput, calls=%fused_computation.10 | convolution fusion | flops 1208745984 | bytes 5505024 | tf_op jit(solution)/shard_map/dot_general | solution.py:190
  103.1 3.9 %fusion.16 = bf16[512,256]{1,0:T(8,128)(2,1)S(1)} fusion(f32[512,256]{1,0:T(8,128)} %fusion.18, bf16[512,2048]{1,0:T(8,128)(2,1)} %constant_dynamic-update-slice_fusion, bf16[512,2304]{1,0:T(8,128)(2,1)} %collective-permute-done.17, bf16[512,512]{1,0:T(8,128)(2,1)S(1)} %bitcast.47), kind=kOutput, calls=%fused_computation.9 | convolution fusion | flops 1209008128 | bytes 5767168 | tf_op jit(solution)/shard_map/dot_general | solution.py:190
  107.0 19.9 %all_to_all.25 = bf16[16,32,256]{2,1,0:T(8,128)(2,1)S(1)} all-to-all(bf16[16,32,256]{2,1,0:T(8,128)(2,1)S(1)} %bitcast.50), channel_id=1, replica_groups=mesh['x_hi'=2,'y'=4,'core'=2,'z'=16,'x_lo'=2] {'z'}, dimensions={0} | all-to-all | bytes 524288 | tf_op jit(solution)/shard_map/all_to_all | solution.py:21
  127.5 22.6 %all_to_all.26 = f32[32,8,256]{2,1,0:T(8,128)S(1)} all-to-all(f32[32,8,256]{2,1,0:T(8,128)S(1)} %fusion.26), channel_id=1, replica_groups=mesh['x_hi'=2,'y'=4,'core'=2,'z'=16,'x_lo'=2] {'x_lo','x_hi','y','core'}, dimensions={0} | all-to-all | bytes 524288 | tf_op jit(solution)/shard_map/all_to_all | solution.py:21
  150.1 17.2 %all_to_all.27 = f32[16,8,256]{2,1,0:T(8,128)S(1)} all-to-all(f32[16,8,256]{2,1,0:T(8,128)S(1)} %broadcast_in_dim.10), channel_id=1, replica_groups=mesh['x_hi'=2,'y'=4,'core'=2,'z'=16,'x_lo'=2] {'z'}, dimensions={0} | all-to-all | bytes 262144 | tf_op jit(solution)/shard_map/all_to_all | solution.py:21
  167.4 15.7 %all_to_all.28 = f32[32,8,256]{2,1,0:T(8,128)} all-to-all(f32[32,8,256]{2,1,0:T(8,128)S(1)} %broadcast_in_dim.11), channel_id=1, replica_groups=mesh['x_hi'=2,'y'=4,'core'=2,'z'=16,'x_lo'=2] {'x_lo','x_hi','y','core'}, dimensions={0} | all-to-all | bytes 524288 | tf_op jit(solution)/shard_map/all_to_all | solution.py:21
  183.0 10.4 %shard_map.37 = f32[32,256]{1,0:T(8,128)} custom-call(f32[256,256]{1,0:T(8,128)} %bitcast.46, f32[32,256]{1,0:T(8,128)} %copy-done.2), custom_call_target="tpu_custom_call" | custom-call | tf_op jit(solution)/shard_map/pallas_call | solution.py:169
  (50 shorter events, 15.8 us)
Async XLA Ops:
  0.0 26.4 %copy-start.1 = (bf16[32,2048]{1,0:T(8,128)(2,1)S(1)}, bf16[32,2048]{1,0:T(8,128)(2,1)}, u32[]{:S(2)}) copy-start(bf16[32,2048]{1,0:T(8,128)(2,1)} %param.3) | copy-start | bytes 393220
  0.0 27.1 %collective-permute-start.1 = (bf16[32,2048]{1,0:T(8,128)(2,1)}, bf16[32,2048]{1,0:T(8,128)(2,1)}, u32[]{:S(2)}, u32[]{:S(2)}) collective-permute-start(bf16[32,2048]{1,0:T(8,128)(2,1)} %param.3), channel_id=1, source_target_pairs={{0,30},{2,0},{4,2},{6,4},{8,6},{10,8},{12,10},{14,12},{16,14},{18,... | collective-permute-start | bytes 393224 | tf_op jit(solution)/shard_map/ppermute | solution.py:49
  12.1 19.9 %collective-permute-start.8 = (bf16[32,2048]{1,0:T(8,128)(2,1)}, bf16[32,2048]{1,0:T(8,128)(2,1)S(1)}, u32[]{:S(2)}, u32[]{:S(2)}) collective-permute-start(bf16[32,2048]{1,0:T(8,128)(2,1)} %param.3), channel_id=1, source_target_pairs={{0,2},{2,4},{4,6},{6,8},{8,10},{10,12},{12,14},{14,16},{16,18},{18... | collective-permute-start | bytes 393224 | tf_op jit(solution)/shard_map/ppermute | solution.py:47
  15.0 18.9 %collective-permute-start.16 = (bf16[32,2304]{1,0:T(8,128)(2,1)S(1)}, bf16[32,2304]{1,0:T(8,128)(2,1)S(1)}, u32[]{:S(2)}, u32[]{:S(2)}) collective-permute-start(bf16[32,2304]{1,0:T(8,128)(2,1)S(1)} %pad_maximum_fusion.2), channel_id=1, source_target_pairs={{0,0},{32,256},{256,32},{288,288},{1,1},{33,257},{257,33},{289,289... | collective-permute-start | bytes 442376 | tf_op jit(solution)/shard_map/ppermute | solution.py:40
  22.5 68.8 %collective-permute-start = (bf16[16,32,512]{2,1,0:T(8,128)(2,1)}, bf16[16,32,512]{2,1,0:T(8,128)(2,1)}, u32[]{:S(2)}, u32[]{:S(2)}) collective-permute-start(bf16[16,32,512]{2,1,0:T(8,128)(2,1)} %select_bitcast_fusion), channel_id=1, source_target_pairs={{0,1},{1,0},{2,3},{3,2},{4,5},{5,4},{6,7},{7,6},{8,9},{9,8},{10,11... | collective-permute-start | bytes 1572872 | tf_op jit(solution)/shard_map/ppermute | solution.py:66
  27.1 16.0 %collective-permute-start.2 = (bf16[32,2048]{1,0:T(8,128)(2,1)}, bf16[32,2048]{1,0:T(8,128)(2,1)}, u32[]{:S(2)}, u32[]{:S(2)}) collective-permute-start(bf16[32,2048]{1,0:T(8,128)(2,1)} %collective-permute-done.1), channel_id=1, source_target_pairs={{0,30},{2,0},{4,2},{6,4},{8,6},{10,8},{12,10},{14,12},{16,14},{18,... | collective-permute-start | bytes 393224 | tf_op jit(solution)/shard_map/ppermute | solution.py:49
  31.9 15.7 %collective-permute-start.9 = (bf16[32,2048]{1,0:T(8,128)(2,1)S(1)}, bf16[32,2048]{1,0:T(8,128)(2,1)}, u32[]{:S(2)}, u32[]{:S(2)}) collective-permute-start(bf16[32,2048]{1,0:T(8,128)(2,1)S(1)} %collective-permute-done.8), channel_id=1, source_target_pairs={{0,2},{2,4},{4,6},{6,8},{8,10},{10,12},{12,14},{14,16},{16,18},{18... | collective-permute-start | bytes 393224 | tf_op jit(solution)/shard_map/ppermute | solution.py:47
  35.6 47.2 %all-to-all-start = ((bf16[16,32,2304]{2,1,0:T(8,128)(2,1)}), bf16[16,32,2304]{2,1,0:T(8,128)(2,1)S(1)}, u32[]{:S(2)}, u32[]{:S(2)}) async-start(bf16[16,32,2304]{2,1,0:T(8,128)(2,1)} %broadcast_in_dim.9), calls=%async_computation | async-start | bytes 4718592 | tf_op jit(solution)/shard_map/all_to_all | solution.py:21
  40.7 54.7 %copy-start = (bf16[1024,512]{1,0:T(8,128)(2,1)S(1)}, bf16[1024,512]{1,0:T(8,128)(2,1)}, u32[]{:S(2)}) copy-start(bf16[1024,512]{1,0:T(8,128)(2,1)} %param.4) | copy-start | bytes 3145732
  43.1 9.6 %collective-permute-start.3 = (bf16[32,2048]{1,0:T(8,128)(2,1)}, bf16[32,2048]{1,0:T(8,128)(2,1)S(1)}, u32[]{:S(2)}, u32[]{:S(2)}) collective-permute-start(bf16[32,2048]{1,0:T(8,128)(2,1)} %collective-permute-done.2), channel_id=1, source_target_pairs={{0,30},{2,0},{4,2},{6,4},{8,6},{10,8},{12,10},{14,12},{16,14},{18,... | collective-permute-start | bytes 393224 | tf_op jit(solution)/shard_map/ppermute | solution.py:49
  47.6 9.6 %collective-permute-start.10 = (bf16[32,2048]{1,0:T(8,128)(2,1)}, bf16[32,2048]{1,0:T(8,128)(2,1)S(1)}, u32[]{:S(2)}, u32[]{:S(2)}) collective-permute-start(bf16[32,2048]{1,0:T(8,128)(2,1)} %collective-permute-done.9), channel_id=1, source_target_pairs={{0,2},{2,4},{4,6},{6,8},{8,10},{10,12},{12,14},{14,16},{16,18},{18... | collective-permute-start | bytes 393224 | tf_op jit(solution)/shard_map/ppermute | solution.py:47
  52.7 7.8 %collective-permute-start.4 = (bf16[32,2048]{1,0:T(8,128)(2,1)S(1)}, bf16[32,2048]{1,0:T(8,128)(2,1)S(1)}, u32[]{:S(2)}, u32[]{:S(2)}) collective-permute-start(bf16[32,2048]{1,0:T(8,128)(2,1)S(1)} %collective-permute-done.3), channel_id=1, source_target_pairs={{0,30},{2,0},{4,2},{6,4},{8,6},{10,8},{12,10},{14,12},{16,14},{18,... | collective-permute-start | bytes 393224 | tf_op jit(solution)/shard_map/ppermute | solution.py:49
  57.3 7.8 %collective-permute-start.11 = (bf16[32,2048]{1,0:T(8,128)(2,1)S(1)}, bf16[32,2048]{1,0:T(8,128)(2,1)S(1)}, u32[]{:S(2)}, u32[]{:S(2)}) collective-permute-start(bf16[32,2048]{1,0:T(8,128)(2,1)S(1)} %collective-permute-done.10), channel_id=1, source_target_pairs={{0,2},{2,4},{4,6},{6,8},{8,10},{10,12},{12,14},{14,16},{16,18},{18... | collective-permute-start | bytes 393224 | tf_op jit(solution)/shard_map/ppermute | solution.py:47
  60.6 7.8 %collective-permute-start.5 = (bf16[32,2048]{1,0:T(8,128)(2,1)S(1)}, bf16[32,2048]{1,0:T(8,128)(2,1)S(1)}, u32[]{:S(2)}, u32[]{:S(2)}) collective-permute-start(bf16[32,2048]{1,0:T(8,128)(2,1)S(1)} %collective-permute-done.4), channel_id=1, source_target_pairs={{0,30},{2,0},{4,2},{6,4},{8,6},{10,8},{12,10},{14,12},{16,14},{18,... | collective-permute-start | bytes 393224 | tf_op jit(solution)/shard_map/ppermute | solution.py:49
  65.1 7.9 %collective-permute-start.12 = (bf16[32,2048]{1,0:T(8,128)(2,1)S(1)}, bf16[32,2048]{1,0:T(8,128)(2,1)S(1)}, u32[]{:S(2)}, u32[]{:S(2)}) collective-permute-start(bf16[32,2048]{1,0:T(8,128)(2,1)S(1)} %collective-permute-done.11), channel_id=1, source_target_pairs={{0,2},{2,4},{4,6},{6,8},{8,10},{10,12},{12,14},{14,16},{16,18},{18... | collective-permute-start | bytes 393224 | tf_op jit(solution)/shard_map/ppermute | solution.py:47
  68.4 7.9 %collective-permute-start.6 = (bf16[32,2048]{1,0:T(8,128)(2,1)S(1)}, bf16[32,2048]{1,0:T(8,128)(2,1)}, u32[]{:S(2)}, u32[]{:S(2)}) collective-permute-start(bf16[32,2048]{1,0:T(8,128)(2,1)S(1)} %collective-permute-done.5), channel_id=1, source_target_pairs={{0,30},{2,0},{4,2},{6,4},{8,6},{10,8},{12,10},{14,12},{16,14},{18,... | collective-permute-start | bytes 393224 | tf_op jit(solution)/shard_map/ppermute | solution.py:49
  73.0 7.8 %collective-permute-start.13 = (bf16[32,2048]{1,0:T(8,128)(2,1)S(1)}, bf16[32,2048]{1,0:T(8,128)(2,1)}, u32[]{:S(2)}, u32[]{:S(2)}) collective-permute-start(bf16[32,2048]{1,0:T(8,128)(2,1)S(1)} %collective-permute-done.12), channel_id=1, source_target_pairs={{0,2},{2,4},{4,6},{6,8},{8,10},{10,12},{12,14},{14,16},{16,18},{18... | collective-permute-start | bytes 393224 | tf_op jit(solution)/shard_map/ppermute | solution.py:47
  76.2 15.1 %collective-permute-start.7 = (bf16[32,2048]{1,0:T(8,128)(2,1)}, bf16[32,2048]{1,0:T(8,128)(2,1)}, u32[]{:S(2)}, u32[]{:S(2)}) collective-permute-start(bf16[32,2048]{1,0:T(8,128)(2,1)} %collective-permute-done.6), channel_id=1, source_target_pairs={{0,30},{2,0},{4,2},{6,4},{8,6},{10,8},{12,10},{14,12},{16,14},{18,... | collective-permute-start | bytes 393224 | tf_op jit(solution)/shard_map/ppermute | solution.py:49
  80.8 10.5 %collective-permute-start.14 = (bf16[32,2048]{1,0:T(8,128)(2,1)}, bf16[32,2048]{1,0:T(8,128)(2,1)S(1)}, u32[]{:S(2)}, u32[]{:S(2)}) collective-permute-start(bf16[32,2048]{1,0:T(8,128)(2,1)} %collective-permute-done.13), channel_id=1, source_target_pairs={{0,2},{2,4},{4,6},{6,8},{8,10},{10,12},{12,14},{14,16},{16,18},{18... | collective-permute-start | bytes 393224 | tf_op jit(solution)/shard_map/ppermute | solution.py:47
  82.8 20.4 %collective-permute-start.17 = (bf16[512,2304]{1,0:T(8,128)(2,1)S(1)}, bf16[512,2304]{1,0:T(8,128)(2,1)}, u32[]{:S(2)}, u32[]{:S(2)}) collective-permute-start(bf16[512,2304]{1,0:T(8,128)(2,1)S(1)} %bitcast.44), channel_id=1, source_target_pairs={{0,32},{32,0},{1,33},{33,1},{2,34},{34,2},{3,35},{35,3},{4,36},{36... | collective-permute-start | bytes 7077896 | tf_op jit(solution)/shard_map/ppermute | solution.py:54
  91.3 7.2 %collective-permute-start.15 = (bf16[32,2048]{1,0:T(8,128)(2,1)S(1)}, bf16[32,2048]{1,0:T(8,128)(2,1)S(1)}, u32[]{:S(2)}, u32[]{:S(2)}) collective-permute-start(bf16[32,2048]{1,0:T(8,128)(2,1)S(1)} %collective-permute-done.14), channel_id=1, source_target_pairs={{0,2},{2,4},{4,6},{6,8},{8,10},{10,12},{12,14},{14,16},{16,18},{18... | collective-permute-start | bytes 393224 | tf_op jit(solution)/shard_map/ppermute | solution.py:47
  127.0 56.0 %copy-start.2 = (f32[32,256]{1,0:T(8,128)}, f32[32,256]{1,0:T(8,128)S(1)}, u32[]{:S(2)}) copy-start(f32[32,256]{1,0:T(8,128)S(1)} %convert_reduce_fusion.images_ref) | copy-start | bytes 98308

commit v7 on v6

--- a/solution.py
+++ b/solution.py
@@ -32,30 +32,34 @@
 
 def gather_points(orbitals, applied, coulomb):
     n = lax.axis_size("z")
-    z = lax.axis_index("z")
     rows, width = orbitals.shape
-    up = [(i, (i + 1) % n) for i in range(n)]
-    down = [(i, (i - 1) % n) for i in range(n)]
+
+    def shifted(value, hops):
+        return lax.ppermute(value, "z", [(i, (i + hops) % n) for i in range(n)])
+
     mine = jnp.concatenate([orbitals, applied], axis=1)
     turned = lax.ppermute(mine, ("x_hi", "core"), [(0, 0), (1, 2), (2, 1), (3, 3)])
-    own = spread(turned, CHIPS)
     kept, moved = swap_sides(coulomb, rows)
-    block = jnp.zeros((n * rows, width), orbitals.dtype)
-    block = lax.dynamic_update_slice(block, orbitals, (z * rows, 0))
-    ahead, behind = orbitals, orbitals
-    for step in range(1, n // 2 + 1):
-        ahead = lax.ppermute(ahead, "z", up)
-        if step < n // 2:
-            behind = lax.ppermute(behind, "z", down)
-            block = lax.dynamic_update_slice(block, behind, (((z + step) & (n - 1)) * rows, 0))
-        block = lax.dynamic_update_slice(block, ahead, (((z - step) & (n - 1)) * rows, 0))
-        if step == n // 2 - 2:
-            own = after(own, behind).reshape(-1, width + applied.shape[1])
+    blocks = {0: orbitals}
+    far, back = orbitals, orbitals
+    for turn in range(1, n // 4 + 1):
+        reach = 2 * turn
+        near, far = shifted(far, 1), shifted(far, 2)
+        if turn < n // 4:
+            close, back = shifted(back, -1), shifted(back, -2)
+            if turn == n // 4 - 1:
+                far, moved = lax.optimization_barrier((far, moved))
+            near, far, close, back = lax.optimization_barrier((near, far, close, back))
+            blocks[reach - 1], blocks[reach] = close, back
+        else:
+            blocks[reach - 1] = shifted(back, -1)
+        blocks[1 - reach], blocks[-reach] = near, far
+        if turn == 1:
+            own = spread(after(turned, far), CHIPS)
+        if turn == n // 4 - 1:
+            own = after(own, far).reshape(-1, width + applied.shape[1])
             other = lax.ppermute(own, "core", [(0, 1), (1, 0)])
-        if step == n // 2 - 1:
-            other = after(other, behind)
-            moved = after(moved, behind)
-    return block, own, other, order_tile(kept, moved)
+    return blocks, own, other, kept, moved
 
 
 def swap_sides(coulomb, count):
@@ -64,23 +68,65 @@
     low = lax.axis_index("x_lo") == 0
     kept = jnp.where(low, first, second)
     moved = lax.ppermute(jnp.where(low, second, first), "x_lo", [(0, 1), (1, 0)])
-    return kept, moved
-
-
-def order_tile(kept, moved):
-    low = lax.axis_index("x_lo") == 0
-    same = lax.axis_index("core") == 0
-    half = kept.shape[-1] // 2
-    left, right = jnp.where(low, kept, moved), jnp.where(low, moved, kept)
-    tiles = []
-    for flag in (same, jnp.logical_not(same)):
-        parts = [jnp.where(flag, x[..., :half], x[..., half:]) for x in (left, right)]
-        tiles.append(jnp.concatenate(parts, axis=-1).reshape(-1, 2 * half))
-    return tiles
+    return kept.reshape(-1, coulomb.shape[1]), moved.reshape(-1, coulomb.shape[1])
+
+
+def images_kernel(offsets, step, place_ref, own_ref, other_ref, kept_ref, moved_ref, *refs):
+    blocks, (out_ref, points, arrived) = refs[:-3], refs[-3:]
+    count, width = blocks[0].shape
+    place = place_ref[0]
+    z, low, same = place // 4, place % 4 // 2 == 0, place % 2 == 0
+    copies = []
+    for i, (offset, block) in enumerate(zip(offsets, blocks)):
+        at = pl.multiple_of(((z + offset) & (len(offsets) - 1)) * count, count)
+        copies.append(pltpu.make_async_copy(block, points.at[pl.ds(at, count), :], arrived.at[i]))
+        copies[-1].start()
+    for copy in copies:
+        copy.wait()
+    half = kept_ref.shape[1] // 2
+    for top in range(0, points.shape[0], step):
+        rows = pl.ds(top, step)
+        total = None
+        for theirs, flag in ((own_ref, same), (other_ref, jnp.logical_not(same))):
+            density = lax.dot_general(
+                points[rows, :],
+                theirs[:, :width],
+                (((1,), (1,)), ((), ())),
+                preferred_element_type=jnp.float32,
+            )
+            mine = jnp.where(flag, kept_ref[rows, :half], kept_ref[rows, half:])
+            sent = jnp.where(flag, moved_ref[rows, :half], moved_ref[rows, half:])
+            tile = jnp.concatenate(
+                [jnp.where(low, mine, sent), jnp.where(low, sent, mine)], axis=1
+            )
+            kernel = (tile.astype(jnp.float32) * density).astype(jnp.bfloat16)
+            part = jnp.dot(kernel, theirs[:, width:], preferred_element_type=jnp.float32)
+            total = part if total is None else total + part
+        out_ref[rows, :] = total.astype(jnp.bfloat16)
+
+
+def partial_images(place, blocks, own, other, kept, moved):
+    offsets = sorted(blocks)
+    count, width = blocks[0].shape
+    rows = len(offsets) * count
+    vmem = pl.BlockSpec(memory_space=pltpu.VMEM)
+    return pl.pallas_call(
+        functools.partial(images_kernel, offsets, 256),
+        out_shape=jax.ShapeDtypeStruct((rows, own.shape[1] - width), jnp.bfloat16),
+        in_specs=[pl.BlockSpec(memory_space=pltpu.SMEM)]
+        + [vmem] * 4
+        + [pl.BlockSpec(memory_space=pl.ANY)] * len(offsets),
+        out_specs=vmem,
+        scratch_shapes=[
+            pltpu.VMEM((rows, width), jnp.bfloat16),
+            pltpu.SemaphoreType.DMA((len(offsets),)),
+        ],
+        compiler_params=pltpu.CompilerParams(vmem_limit_bytes=24 << 20),
+    )(place, own, other, kept, moved, *[blocks[offset] for offset in offsets])
 
 
 def reduce_rows(partial):
-    chunks = partial.astype(jnp.bfloat16).reshape(lax.axis_size("z"), -1, partial.shape[1])
+    chunks = partial.reshape(lax.axis_size("z"), -1, partial.shape[1])
     return jnp.sum(exchange(chunks, "z").astype(jnp.float32), axis=0)
 
 
@@ -179,15 +225,10 @@
 
 
 def per_device(orbitals, coulomb, applied):
-    width = orbitals.shape[1]
-    points, own, other, tiles = gather_points(orbitals, applied, coulomb)
-    partial = 0.0
-    for theirs, tile in zip((own, other), tiles):
-        density = jnp.einsum(
-            "ik,jk->ij", points, theirs[:, :width], preferred_element_type=jnp.float32
-        )
-        kernel = (tile.astype(jnp.float32) * density).astype(jnp.bfloat16)
-        partial += jnp.dot(kernel, theirs[:, width:], preferred_element_type=jnp.float32)
+    side, core = lax.axis_index("x_lo"), lax.axis_index("core")
+    place = (lax.axis_index("z") * 4 + side * 2 + core).reshape(1)
+    gathered = gather_points(orbitals, applied, coulomb)
+    partial = partial_images(place, *gathered)
     images = reduce_rows(partial)
     local_gram = jnp.einsum("ia,ib->ab", images, images, precision=lax.Precision.HIGHEST)
     return orthonormalize(sum_everywhere(local_gram), images)

time: 195 us -> 211 us (1.082)
  waiting for transfers between devices: 1.76 us -> 18.5 us
  matrix products: 8.22 us -> 0.34 us
  Pallas kernels: 10.4 us -> 18.1 us
  local copies, waits for them, and re-layouts: 19.5 us -> 16.7 us
  starting transfers between devices: 73.3 us -> 76 us
  blocking collectives: 75.4 us -> 78 us
    dynamic_update_slice x16 -> x0, local copies, waits for them, and re-layouts: 16.1 us -> none  [the longest x7 8.39 us: gather_points(): lax.dynamic_update_slice(block, behind, ((z + step & n - 1) * rows, 0))]
    unnamed x6 -> x44, local copies, waits for them, and re-layouts: 0.01 us -> 14.9 us
    ppermute x15, waiting for transfers between devices: 1.74 us -> 14.8 us  [shifted(): return lax.ppermute(value, 'z', [(i, (i + hops) % n) for i in range(n)])]
    dot_general x2 -> x0, matrix products: 7.87 us -> none  [per_device(): jnp.dot(kernel, theirs[:, width:], preferred_element_type=jnp.float32)]
    pallas_call x0 -> x1, Pallas kernels: none -> 7.66 us  [partial_images(): pl.pallas_call(functools.partial(images_kernel, offsets, 256), out_shape=...]
    ppermute x1, waiting for transfers between devices: 0.01 us -> 3.68 us  [swap_sides(): lax.ppermute(jnp.where(low, second, first), 'x_lo', [(0, 1), (1, 0)])]
    all_to_all x4, blocking collectives: 75.4 us -> 78 us  [exchange(): return lax.all_to_all(chunks, axes, 0, 0, tiled=True)]
    ppermute x15, starting transfers between devices: 55.1 us -> 57.4 us  [shifted(): return lax.ppermute(value, 'z', [(i, (i + hops) % n) for i in range(n)])]
  transfers between devices with their start and end apart: 19 -> 19, of which waited for: 1 -> 9; matrix products, arithmetic and copies ran while one was open for 14% -> 1% of each run, Pallas kernels for 0% -> 0%
where the time goes in v7:
time: 211 us; the launch traced here: 210 us
  blocking collectives  78 us (37%)
  starting transfers between devices  76 us (36%)
  waiting for transfers between devices  18.5 us (9%)
  Pallas kernels  18.1 us (9%)
  local copies, waits for them, and re-layouts  16.7 us (8%)
  other arithmetic  2.31 us (1%)
    all_to_all x4, blocking collectives, exchange(): return lax.all_to_all(chunks, axes, 0, 0, tiled=True)  78 us
    ppermute x15, starting transfers between devices, shifted(): return lax.ppermute(value, 'z', [(i, (i + hops) % n) for i in range(n)])  57.4 us
    unnamed x44, local copies, waits for them, and re-layouts  14.9 us
    ppermute x15, waiting for transfers between devices, shifted(): return lax.ppermute(value, 'z', [(i, (i + hops) % n) for i in range(n)])  14.8 us
    pallas_call x1, Pallas kernels, orthonormalize(): pl.pallas_call(functools.partial(orthonormalize_kernel, 64, 8), out_shape...  10.4 us
    pallas_call x1, Pallas kernels, partial_images(): pl.pallas_call(functools.partial(images_kernel, offsets, 256), out_shape=...  7.66 us
    ppermute x1, starting transfers between devices, gather_points(): lax.ppermute(mine, ('x_hi', 'core'), [(0, 0), (1, 2), (2, 1), (3, 3)])  6.03 us
    all_to_all x1, starting transfers between devices, exchange(): return lax.all_to_all(chunks, axes, 0, 0, tiled=True)  5.32 us
  transfers between devices with their start and end apart: 19, of which 9 were waited for; matrix products, arithmetic and copies ran while one was open for 1% of the time, Pallas kernels for 0%

profile of v7, /device:TPU:1, one launch (start us, length us, event | category | flops | bytes accessed | tf_op | source)
XLA Modules:
  0.0 210.2 jit_solution(9412803647484720233)
XLA Ops:
  0.9 6.0 %collective-permute-start = (bf16[32,2304]{1,0:T(8,128)(2,1)S(1)}, bf16[32,2304]{1,0:T(8,128)(2,1)S(1)}, u32[]{:S(2)}, u32[]{:S(2)}) collective-permute-start(bf16[32,2304]{1,0:T(8,128)(2,1)S(1)} %pad_maximum_fusion), channel_id=1, source_target_pairs={{0,0},{32,256},{256,32},{288,288},{1,1},{33,257},{257,33},{289,289... | collective-permute-start | bytes 442376 | tf_op jit(solution)/shard_map/ppermute | solution.py:41
  7.0 11.1 %collective-permute-start.3 = (bf16[32,2048]{1,0:T(8,128)(2,1)}, bf16[32,2048]{1,0:T(8,128)(2,1)S(1)}, u32[]{:S(2)}, u32[]{:S(2)}) collective-permute-start(bf16[32,2048]{1,0:T(8,128)(2,1)} %refs_8_.1), channel_id=1, source_target_pairs={{0,30},{2,0},{4,2},{6,4},{8,6},{10,8},{12,10},{14,12},{16,14},{18,... | collective-permute-start | bytes 393224 | tf_op jit(solution)/shard_map/ppermute | solution.py:38
  18.1 1.9 collective-permute-start.2
  20.0 1.9 collective-permute-start.1
  22.0 5.5 %collective-permute-start.4 = (bf16[32,2048]{1,0:T(8,128)(2,1)}, bf16[32,2048]{1,0:T(8,128)(2,1)}, u32[]{:S(2)}, u32[]{:S(2)}) collective-permute-start(bf16[32,2048]{1,0:T(8,128)(2,1)} %refs_8_.1), channel_id=1, source_target_pairs={{0,28},{2,30},{4,0},{6,2},{8,4},{10,6},{12,8},{14,10},{16,12},{18,... | collective-permute-start | bytes 393224 | tf_op jit(solution)/shard_map/ppermute | solution.py:38
  29.3 1.8 collective-permute-done.4.refs_10_
  31.1 1.7 broadcast_in_dim.6
  32.8 5.3 %all-to-all-start = ((bf16[16,32,2304]{2,1,0:T(8,128)(2,1)}), bf16[16,32,2304]{2,1,0:T(8,128)(2,1)S(1)}, u32[]{:S(2)}, u32[]{:S(2)}) async-start(bf16[16,32,2304]{2,1,0:T(8,128)(2,1)} %broadcast_in_dim.6), calls=%async_computation | async-start | bytes 4718592 | tf_op jit(solution)/shard_map/all_to_all | solution.py:21
  39.4 3.3 %collective-permute-start.11 = (bf16[16,32,512]{2,1,0:T(8,128)(2,1)S(1)}, bf16[16,32,512]{2,1,0:T(8,128)(2,1)S(1)}, u32[]{:S(2)}, u32[]{:S(2)}) collective-permute-start(bf16[16,32,512]{2,1,0:T(8,128)(2,1)S(1)} %get-tuple-element.38), channel_id=1, source_target_pairs={{0,1},{1,0},{2,3},{3,2},{4,5},{5,4},{6,7},{7,6},{8,9},{9,8},{10,11... | collective-permute-start | bytes 1572872 | tf_op jit(solution)/shard_map/ppermute | solution.py:70
  42.6 5.9 %collective-permute-start.8 = (bf16[32,2048]{1,0:T(8,128)(2,1)}, bf16[32,2048]{1,0:T(8,128)(2,1)S(1)}, u32[]{:S(2)}, u32[]{:S(2)}) collective-permute-start(bf16[32,2048]{1,0:T(8,128)(2,1)} %collective-permute-done.4.refs_10_), channel_id=1, source_target_pairs={{0,28},{2,30},{4,0},{6,2},{8,4},{10,6},{12,8},{14,10},{16,12},{18,... | collective-permute-start | bytes 393224 | tf_op jit(solution)/shard_map/ppermute | solution.py:38
  48.5 1.9 collective-permute-start.7
  50.5 2.3 %collective-permute-start.6 = (bf16[32,2048]{1,0:T(8,128)(2,1)}, bf16[32,2048]{1,0:T(8,128)(2,1)S(1)}, u32[]{:S(2)}, u32[]{:S(2)}) collective-permute-start(bf16[32,2048]{1,0:T(8,128)(2,1)} %collective-permute-done.2.refs_6_), channel_id=1, source_target_pairs={{0,4},{2,6},{4,8},{6,10},{8,12},{10,14},{12,16},{14,18},{16,20},{1... | collective-permute-start | bytes 393224 | tf_op jit(solution)/shard_map/ppermute | solution.py:38
  52.8 3.0 %collective-permute-start.5 = (bf16[32,2048]{1,0:T(8,128)(2,1)}, bf16[32,2048]{1,0:T(8,128)(2,1)S(1)}, u32[]{:S(2)}, u32[]{:S(2)}) collective-permute-start(bf16[32,2048]{1,0:T(8,128)(2,1)} %collective-permute-done.2.refs_6_), channel_id=1, source_target_pairs={{0,2},{2,4},{4,6},{6,8},{8,10},{10,12},{12,14},{14,16},{16,18},{18... | collective-permute-start | bytes 393224 | tf_op jit(solution)/shard_map/ppermute | solution.py:38
  57.3 2.3 %collective-permute-done.6.refs_4_ = bf16[32,2048]{1,0:T(8,128)(2,1)S(1)} collective-permute-done((bf16[32,2048]{1,0:T(8,128)(2,1)}, bf16[32,2048]{1,0:T(8,128)(2,1)S(1)}, u32[]{:S(2)}, u32[]{:S(2)}) %collective-permute-start.6) | collective-permute-done | bytes 131104 | tf_op jit(solution)/shard_map/ppermute | solution.py:38
  59.6 4.7 %collective-permute-done.5.refs_5_ = bf16[32,2048]{1,0:T(8,128)(2,1)S(1)} collective-permute-done((bf16[32,2048]{1,0:T(8,128)(2,1)}, bf16[32,2048]{1,0:T(8,128)(2,1)S(1)}, u32[]{:S(2)}, u32[]{:S(2)}) %collective-permute-start.5) | collective-permute-done | bytes 131104 | tf_op jit(solution)/shard_map/ppermute | solution.py:38
  65.0 1.9 collective-permute-start.10
  66.9 1.9 collective-permute-start.9
  69.5 5.5 %collective-permute-start.13 = (bf16[32,2048]{1,0:T(8,128)(2,1)S(1)}, bf16[32,2048]{1,0:T(8,128)(2,1)S(1)}, u32[]{:S(2)}, u32[]{:S(2)}) collective-permute-start(bf16[32,2048]{1,0:T(8,128)(2,1)S(1)} %collective-permute-done.8.refs_12_), channel_id=1, source_target_pairs={{0,28},{2,30},{4,0},{6,2},{8,4},{10,6},{12,8},{14,10},{16,12},{18,... | collective-permute-start | bytes 393224 | tf_op jit(solution)/shard_map/ppermute | solution.py:38
  74.9 3.4 %collective-permute-start.12 = (bf16[32,2048]{1,0:T(8,128)(2,1)S(1)}, bf16[32,2048]{1,0:T(8,128)(2,1)S(1)}, u32[]{:S(2)}, u32[]{:S(2)}) collective-permute-start(bf16[32,2048]{1,0:T(8,128)(2,1)S(1)} %collective-permute-done.8.refs_12_), channel_id=1, source_target_pairs={{0,30},{2,0},{4,2},{6,4},{8,6},{10,8},{12,10},{14,12},{16,14},{18,... | collective-permute-start | bytes 393224 | tf_op jit(solution)/shard_map/ppermute | solution.py:38
  79.0 3.7 %collective-permute-done.11 = bf16[16,32,512]{2,1,0:T(8,128)(2,1)S(1)} collective-permute-done((bf16[16,32,512]{2,1,0:T(8,128)(2,1)S(1)}, bf16[16,32,512]{2,1,0:T(8,128)(2,1)S(1)}, u32[]{:S(2)}, u32[]{:S(2)}) %collective-permute-start.11) | collective-permute-done | bytes 524320 | tf_op jit(solution)/shard_map/ppermute | solution.py:70
  84.6 3.9 %collective-permute-start.14 = (bf16[512,2304]{1,0:T(8,128)(2,1)S(1)}, bf16[512,2304]{1,0:T(8,128)(2,1)}, u32[]{:S(2)}, u32[]{:S(2)}) collective-permute-start(bf16[512,2304]{1,0:T(8,128)(2,1)S(1)} %bitcast.28), channel_id=1, source_target_pairs={{0,32},{32,0},{1,33},{33,1},{2,34},{34,2},{3,35},{35,3},{4,36},{36... | collective-permute-start | bytes 7077896 | tf_op jit(solution)/shard_map/ppermute | solution.py:61
  88.6 4.4 %collective-permute-start.17 = (bf16[32,2048]{1,0:T(8,128)(2,1)}, bf16[32,2048]{1,0:T(8,128)(2,1)}, u32[]{:S(2)}, u32[]{:S(2)}) collective-permute-start(bf16[32,2048]{1,0:T(8,128)(2,1)} %copy-done.17), channel_id=1, source_target_pairs={{0,30},{2,0},{4,2},{6,4},{8,6},{10,8},{12,10},{14,12},{16,14},{18,... | collective-permute-start | bytes 393224 | tf_op jit(solution)/shard_map/ppermute | solution.py:38
  93.0 1.9 collective-permute-start.16
  94.9 4.9 %collective-permute-start.15 = (bf16[32,2048]{1,0:T(8,128)(2,1)}, bf16[32,2048]{1,0:T(8,128)(2,1)}, u32[]{:S(2)}, u32[]{:S(2)}) collective-permute-start(bf16[32,2048]{1,0:T(8,128)(2,1)} %copy-done.13), channel_id=1, source_target_pairs={{0,4},{2,6},{4,8},{6,10},{8,12},{10,14},{12,16},{14,18},{16,20},{1... | collective-permute-start | bytes 393224 | tf_op jit(solution)/shard_map/ppermute | solution.py:38
  99.9 1.3 collective-permute-done.16.refs_1_
  101.2 3.3 %collective-permute-done.15.refs_0_ = bf16[32,2048]{1,0:T(8,128)(2,1)} collective-permute-done((bf16[32,2048]{1,0:T(8,128)(2,1)}, bf16[32,2048]{1,0:T(8,128)(2,1)}, u32[]{:S(2)}, u32[]{:S(2)}) %collective-permute-start.15) | collective-permute-done | bytes 131104 | tf_op jit(solution)/shard_map/ppermute | solution.py:38
  113.5 7.7 %shard_map.37 = bf16[512,256]{1,0:T(8,128)(2,1)S(1)} custom-call(s32[1]{0:T(128)} %bitcast.place_ref, bf16[512,2304]{1,0:T(8,128)(2,1)S(1)} %bitcast.29, bf16[512,2304]{1,0:T(8,128)(2,1)} %collective-permute-done.14.other_ref, bf16[512,512]{1,0:T(8,128)(2,1)S(1)} %bitcast.30, bf16[512,512]{1,0:T(8,128)(2,1)S(1)} %bitcast.32, ...), custom_call_target="tpu_custom_call" | custom-call | tf_op jit(solution)/shard_map/pallas_call | solution.py:113
  121.2 27.0 %all_to_all.25 = bf16[16,32,256]{2,1,0:T(8,128)(2,1)S(1)} all-to-all(bf16[16,32,256]{2,1,0:T(8,128)(2,1)S(1)} %bitcast.31), channel_id=1, replica_groups=mesh['x_hi'=2,'y'=4,'core'=2,'z'=16,'x_lo'=2] {'z'}, dimensions={0} | all-to-all | bytes 524288 | tf_op jit(solution)/shard_map/all_to_all | solution.py:21
  148.7 17.7 %all_to_all.26 = f32[32,8,256]{2,1,0:T(8,128)S(1)} all-to-all(f32[32,8,256]{2,1,0:T(8,128)S(1)} %fusion), channel_id=1, replica_groups=mesh['x_hi'=2,'y'=4,'core'=2,'z'=16,'x_lo'=2] {'x_lo','x_hi','y','core'}, dimensions={0} | all-to-all | bytes 524288 | tf_op jit(solution)/shard_map/all_to_all | solution.py:21
  166.4 17.6 %all_to_all.27 = f32[16,8,256]{2,1,0:T(8,128)S(1)} all-to-all(f32[16,8,256]{2,1,0:T(8,128)S(1)} %broadcast_in_dim.7), channel_id=1, replica_groups=mesh['x_hi'=2,'y'=4,'core'=2,'z'=16,'x_lo'=2] {'z'}, dimensions={0} | all-to-all | bytes 262144 | tf_op jit(solution)/shard_map/all_to_all | solution.py:21
  184.1 15.7 %all_to_all.28 = f32[32,8,256]{2,1,0:T(8,128)} all-to-all(f32[32,8,256]{2,1,0:T(8,128)S(1)} %broadcast_in_dim.8), channel_id=1, replica_groups=mesh['x_hi'=2,'y'=4,'core'=2,'z'=16,'x_lo'=2] {'x_lo','x_hi','y','core'}, dimensions={0} | all-to-all | bytes 524288 | tf_op jit(solution)/shard_map/all_to_all | solution.py:21
  199.8 10.4 %shard_map.38 = f32[32,256]{1,0:T(8,128)} custom-call(f32[256,256]{1,0:T(8,128)} %bitcast.34, f32[32,256]{1,0:T(8,128)} %copy-done.21), custom_call_target="tpu_custom_call" | custom-call | tf_op jit(solution)/shard_map/pallas_call | solution.py:215
  (66 shorter events, 19.1 us)
Async XLA Ops:
  0.9 30.2 %collective-permute-start = (bf16[32,2304]{1,0:T(8,128)(2,1)S(1)}, bf16[32,2304]{1,0:T(8,128)(2,1)S(1)}, u32[]{:S(2)}, u32[]{:S(2)}) collective-permute-start(bf16[32,2304]{1,0:T(8,128)(2,1)S(1)} %pad_maximum_fusion), channel_id=1, source_target_pairs={{0,0},{32,256},{256,32},{288,288},{1,1},{33,257},{257,33},{289,289... | collective-permute-start | bytes 442376 | tf_op jit(solution)/shard_map/ppermute | solution.py:41
  7.0 20.5 %collective-permute-start.3 = (bf16[32,2048]{1,0:T(8,128)(2,1)}, bf16[32,2048]{1,0:T(8,128)(2,1)S(1)}, u32[]{:S(2)}, u32[]{:S(2)}) collective-permute-start(bf16[32,2048]{1,0:T(8,128)(2,1)} %refs_8_.1), channel_id=1, source_target_pairs={{0,30},{2,0},{4,2},{6,4},{8,6},{10,8},{12,10},{14,12},{16,14},{18,... | collective-permute-start | bytes 393224 | tf_op jit(solution)/shard_map/ppermute | solution.py:38
  18.1 10.1 %collective-permute-start.2 = (bf16[32,2048]{1,0:T(8,128)(2,1)}, bf16[32,2048]{1,0:T(8,128)(2,1)}, u32[]{:S(2)}, u32[]{:S(2)}) collective-permute-start(bf16[32,2048]{1,0:T(8,128)(2,1)} %refs_8_.1), channel_id=1, source_target_pairs={{0,4},{2,6},{4,8},{6,10},{8,12},{10,14},{12,16},{14,18},{16,20},{1... | collective-permute-start | bytes 393224 | tf_op jit(solution)/shard_map/ppermute | solution.py:38
  20.0 8.6 %collective-permute-start.1 = (bf16[32,2048]{1,0:T(8,128)(2,1)}, bf16[32,2048]{1,0:T(8,128)(2,1)S(1)}, u32[]{:S(2)}, u32[]{:S(2)}) collective-permute-start(bf16[32,2048]{1,0:T(8,128)(2,1)} %refs_8_.1), channel_id=1, source_target_pairs={{0,2},{2,4},{4,6},{6,8},{8,10},{10,12},{12,14},{14,16},{16,18},{18... | collective-permute-start | bytes 393224 | tf_op jit(solution)/shard_map/ppermute | solution.py:38
  22.0 9.1 %collective-permute-start.4 = (bf16[32,2048]{1,0:T(8,128)(2,1)}, bf16[32,2048]{1,0:T(8,128)(2,1)}, u32[]{:S(2)}, u32[]{:S(2)}) collective-permute-start(bf16[32,2048]{1,0:T(8,128)(2,1)} %refs_8_.1), channel_id=1, source_target_pairs={{0,28},{2,30},{4,0},{6,2},{8,4},{10,6},{12,8},{14,10},{16,12},{18,... | collective-permute-start | bytes 393224 | tf_op jit(solution)/shard_map/ppermute | solution.py:38
  32.8 71.7 %copy-start = (bf16[32,2048]{1,0:T(8,128)(2,1)S(1)}, bf16[32,2048]{1,0:T(8,128)(2,1)}, u32[]{:S(2)}) copy-start(bf16[32,2048]{1,0:T(8,128)(2,1)} %refs_8_.1) | copy-start | bytes 393220
  32.8 51.9 %all-to-all-start = ((bf16[16,32,2304]{2,1,0:T(8,128)(2,1)}), bf16[16,32,2304]{2,1,0:T(8,128)(2,1)S(1)}, u32[]{:S(2)}, u32[]{:S(2)}) async-start(bf16[16,32,2304]{2,1,0:T(8,128)(2,1)} %broadcast_in_dim.6), calls=%async_computation | async-start | bytes 4718592 | tf_op jit(solution)/shard_map/all_to_all | solution.py:21
  39.4 43.3 %collective-permute-start.11 = (bf16[16,32,512]{2,1,0:T(8,128)(2,1)S(1)}, bf16[16,32,512]{2,1,0:T(8,128)(2,1)S(1)}, u32[]{:S(2)}, u32[]{:S(2)}) collective-permute-start(bf16[16,32,512]{2,1,0:T(8,128)(2,1)S(1)} %get-tuple-element.38), channel_id=1, source_target_pairs={{0,1},{1,0},{2,3},{3,2},{4,5},{5,4},{6,7},{7,6},{8,9},{9,8},{10,11... | collective-permute-start | bytes 1572872 | tf_op jit(solution)/shard_map/ppermute | solution.py:70
  42.6 13.1 %collective-permute-start.8 = (bf16[32,2048]{1,0:T(8,128)(2,1)}, bf16[32,2048]{1,0:T(8,128)(2,1)S(1)}, u32[]{:S(2)}, u32[]{:S(2)}) collective-permute-start(bf16[32,2048]{1,0:T(8,128)(2,1)} %collective-permute-done.4.refs_10_), channel_id=1, source_target_pairs={{0,28},{2,30},{4,0},{6,2},{8,4},{10,6},{12,8},{14,10},{16,12},{18,... | collective-permute-start | bytes 393224 | tf_op jit(solution)/shard_map/ppermute | solution.py:38
  48.5 8.1 %collective-permute-start.7 = (bf16[32,2048]{1,0:T(8,128)(2,1)}, bf16[32,2048]{1,0:T(8,128)(2,1)S(1)}, u32[]{:S(2)}, u32[]{:S(2)}) collective-permute-start(bf16[32,2048]{1,0:T(8,128)(2,1)} %collective-permute-done.4.refs_10_), channel_id=1, source_target_pairs={{0,30},{2,0},{4,2},{6,4},{8,6},{10,8},{12,10},{14,12},{16,14},{18,... | collective-permute-start | bytes 393224 | tf_op jit(solution)/shard_map/ppermute | solution.py:38
  50.5 9.1 %collective-permute-start.6 = (bf16[32,2048]{1,0:T(8,128)(2,1)}, bf16[32,2048]{1,0:T(8,128)(2,1)S(1)}, u32[]{:S(2)}, u32[]{:S(2)}) collective-permute-start(bf16[32,2048]{1,0:T(8,128)(2,1)} %collective-permute-done.2.refs_6_), channel_id=1, source_target_pairs={{0,4},{2,6},{4,8},{6,10},{8,12},{10,14},{12,16},{14,18},{16,20},{1... | collective-permute-start | bytes 393224 | tf_op jit(solution)/shard_map/ppermute | solution.py:38
  52.8 11.5 %collective-permute-start.5 = (bf16[32,2048]{1,0:T(8,128)(2,1)}, bf16[32,2048]{1,0:T(8,128)(2,1)S(1)}, u32[]{:S(2)}, u32[]{:S(2)}) collective-permute-start(bf16[32,2048]{1,0:T(8,128)(2,1)} %collective-permute-done.2.refs_6_), channel_id=1, source_target_pairs={{0,2},{2,4},{4,6},{6,8},{8,10},{10,12},{12,14},{14,16},{16,18},{18... | collective-permute-start | bytes 393224 | tf_op jit(solution)/shard_map/ppermute | solution.py:38
  65.0 14.0 %collective-permute-start.10 = (bf16[32,2048]{1,0:T(8,128)(2,1)S(1)}, bf16[32,2048]{1,0:T(8,128)(2,1)S(1)}, u32[]{:S(2)}, u32[]{:S(2)}) collective-permute-start(bf16[32,2048]{1,0:T(8,128)(2,1)S(1)} %collective-permute-done.6.refs_4_), channel_id=1, source_target_pairs={{0,4},{2,6},{4,8},{6,10},{8,12},{10,14},{12,16},{14,18},{16,20},{1... | collective-permute-start | bytes 393224 | tf_op jit(solution)/shard_map/ppermute | solution.py:38
  66.9 15.8 %collective-permute-start.9 = (bf16[32,2048]{1,0:T(8,128)(2,1)S(1)}, bf16[32,2048]{1,0:T(8,128)(2,1)S(1)}, u32[]{:S(2)}, u32[]{:S(2)}) collective-permute-start(bf16[32,2048]{1,0:T(8,128)(2,1)S(1)} %collective-permute-done.6.refs_4_), channel_id=1, source_target_pairs={{0,2},{2,4},{4,6},{6,8},{8,10},{10,12},{12,14},{14,16},{16,18},{18... | collective-permute-start | bytes 393224 | tf_op jit(solution)/shard_map/ppermute | solution.py:38
  69.5 13.8 %collective-permute-start.13 = (bf16[32,2048]{1,0:T(8,128)(2,1)S(1)}, bf16[32,2048]{1,0:T(8,128)(2,1)S(1)}, u32[]{:S(2)}, u32[]{:S(2)}) collective-permute-start(bf16[32,2048]{1,0:T(8,128)(2,1)S(1)} %collective-permute-done.8.refs_12_), channel_id=1, source_target_pairs={{0,28},{2,30},{4,0},{6,2},{8,4},{10,6},{12,8},{14,10},{16,12},{18,... | collective-permute-start | bytes 393224 | tf_op jit(solution)/shard_map/ppermute | solution.py:38
  74.9 9.0 %collective-permute-start.12 = (bf16[32,2048]{1,0:T(8,128)(2,1)S(1)}, bf16[32,2048]{1,0:T(8,128)(2,1)S(1)}, u32[]{:S(2)}, u32[]{:S(2)}) collective-permute-start(bf16[32,2048]{1,0:T(8,128)(2,1)S(1)} %collective-permute-done.8.refs_12_), channel_id=1, source_target_pairs={{0,30},{2,0},{4,2},{6,4},{8,6},{10,8},{12,10},{14,12},{16,14},{18,... | collective-permute-start | bytes 393224 | tf_op jit(solution)/shard_map/ppermute | solution.py:38
  79.0 4.3 %copy-start.13 = (bf16[32,2048]{1,0:T(8,128)(2,1)}, bf16[32,2048]{1,0:T(8,128)(2,1)S(1)}, u32[]{:S(2)}) copy-start(bf16[32,2048]{1,0:T(8,128)(2,1)S(1)} %collective-permute-done.10.refs_2_) | copy-start | bytes 393220
  84.6 19.8 %collective-permute-start.14 = (bf16[512,2304]{1,0:T(8,128)(2,1)S(1)}, bf16[512,2304]{1,0:T(8,128)(2,1)}, u32[]{:S(2)}, u32[]{:S(2)}) collective-permute-start(bf16[512,2304]{1,0:T(8,128)(2,1)S(1)} %bitcast.28), channel_id=1, source_target_pairs={{0,32},{32,0},{1,33},{33,1},{2,34},{34,2},{3,35},{35,3},{4,36},{36... | collective-permute-start | bytes 7077896 | tf_op jit(solution)/shard_map/ppermute | solution.py:61
  88.6 11.3 %collective-permute-start.17 = (bf16[32,2048]{1,0:T(8,128)(2,1)}, bf16[32,2048]{1,0:T(8,128)(2,1)}, u32[]{:S(2)}, u32[]{:S(2)}) collective-permute-start(bf16[32,2048]{1,0:T(8,128)(2,1)} %copy-done.17), channel_id=1, source_target_pairs={{0,30},{2,0},{4,2},{6,4},{8,6},{10,8},{12,10},{14,12},{16,14},{18,... | collective-permute-start | bytes 393224 | tf_op jit(solution)/shard_map/ppermute | solution.py:38
  93.0 8.2 %collective-permute-start.16 = (bf16[32,2048]{1,0:T(8,128)(2,1)}, bf16[32,2048]{1,0:T(8,128)(2,1)}, u32[]{:S(2)}, u32[]{:S(2)}) collective-permute-start(bf16[32,2048]{1,0:T(8,128)(2,1)} %copy-done.13), channel_id=1, source_target_pairs={{0,2},{2,4},{4,6},{6,8},{8,10},{10,12},{12,14},{14,16},{16,18},{18... | collective-permute-start | bytes 393224 | tf_op jit(solution)/shard_map/ppermute | solution.py:38
  94.9 9.5 %collective-permute-start.15 = (bf16[32,2048]{1,0:T(8,128)(2,1)}, bf16[32,2048]{1,0:T(8,128)(2,1)}, u32[]{:S(2)}, u32[]{:S(2)}) collective-permute-start(bf16[32,2048]{1,0:T(8,128)(2,1)} %copy-done.13), channel_id=1, source_target_pairs={{0,4},{2,6},{4,8},{6,10},{8,12},{10,14},{12,16},{14,18},{16,20},{1... | collective-permute-start | bytes 393224 | tf_op jit(solution)/shard_map/ppermute | solution.py:38
  104.4 0.9 copy-start.2
  105.4 0.9 copy-start.4
  106.3 0.9 copy-start.6
  107.2 0.9 copy-start.8
  108.1 0.9 copy-start.10
  109.0 0.9 copy-start.12
  109.9 0.9 copy-start.14
  110.8 0.9 copy-start.16
  111.7 0.9 copy-start.18
  112.6 0.9 copy-start.20
  148.2 51.6 %copy-start.21 = (f32[32,256]{1,0:T(8,128)}, f32[32,256]{1,0:T(8,128)S(1)}, u32[]{:S(2)}) copy-start(f32[32,256]{1,0:T(8,128)S(1)} %convert_reduce_fusion.images_ref) | copy-start | bytes 98308
  (9 other events, 5.9 us)

commit v8 on v5

--- a/solution.py
+++ b/solution.py
@@ -7,6 +7,7 @@
 from jax.experimental.pallas import tpu as pltpu
 from jax.sharding import Mesh
 from jax.sharding import PartitionSpec as P
+
 
 NMU = 16384
 ROW = ("x_hi", "y", "core")
@@ -39,11 +40,16 @@
     down = [(i, (i - 1) % n) for i in range(n)]
     ahead, behind = mine, mine
     for step in range(1, n // 2 + 1):
+        if step == n // 2:
+            ahead, behind = ahead[: rows // 2], behind[rows // 2 :]
         ahead = lax.ppermute(ahead, "z", up)
-        if step < n // 2:
-            behind = lax.ppermute(behind, "z", down)
-            block = lax.dynamic_update_slice(block, behind, (((z + step) & (n - 1)) * rows, 0))
-            late = behind
+        behind = lax.ppermute(behind, "z", down)
+        at = ((z + step) & (n - 1)) * rows
+        if step == n // 2:
+            block = lax.dynamic_update_slice(block, behind, (at + rows // 2, 0))
+        else:
+            block = lax.dynamic_update_slice(block, behind, (at, 0))
+            late = ahead
         block = lax.dynamic_update_slice(block, ahead, (((z - step) & (n - 1)) * rows, 0))
     return block, late
 
@@ -178,6 +184,7 @@
 
 def solution(mesh):
     fine = Mesh(mesh.devices.reshape(SIZES), AXES)
+
     return jax.shard_map(
         per_device,
         mesh=fine,

time: 187 us -> 181 us (0.968)
  waiting for transfers between devices: 18.7 us -> 7.99 us
  blocking collectives: 74.9 us -> 79.1 us
    ppermute x1, waiting for transfers between devices: 10.7 us -> 3.44 us  [swap_sides(): lax.ppermute(jnp.where(low, second, first), 'x_lo', [(0, 1), (1, 0)])]
    all_to_all x4, blocking collectives: 74.9 us -> 79.1 us  [exchange(): return lax.all_to_all(chunks, axes, 0, 0, tiled=True)]
    ppermute x8, waiting for transfers between devices: 7.93 us -> 4.52 us  [gather_z(): ahead = lax.ppermute(ahead, 'z', up)]
    ppermute x7 -> x8, starting transfers between devices: 39.6 us -> 40.5 us  [gather_z(): behind = lax.ppermute(behind, 'z', down)]
  transfers between devices with their start and end apart: 17 -> 18, of which waited for: 2 -> 7; matrix products, arithmetic and copies ran while one was open for 1% -> 1% of each run, Pallas kernels for 0% -> 0%
where the time goes in v8:
time: 181 us; the launch traced here: 180 us
  blocking collectives  79.1 us (44%)
  starting transfers between devices  70.4 us (39%)
  Pallas kernels  10.4 us (6%)
  waiting for transfers between devices  7.99 us (4%)
  matrix products  5.42 us (3%)
  local copies, waits for them, and re-layouts  3.39 us (2%)
  other arithmetic  3.14 us (2%)
    all_to_all x4, blocking collectives, exchange(): return lax.all_to_all(chunks, axes, 0, 0, tiled=True)  79.1 us
    ppermute x8, starting transfers between devices, gather_z(): behind = lax.ppermute(behind, 'z', down)  40.5 us
    ppermute x8, starting transfers between devices, gather_z(): ahead = lax.ppermute(ahead, 'z', up)  15.3 us
    all_to_all x1, starting transfers between devices, exchange(): return lax.all_to_all(chunks, axes, 0, 0, tiled=True)  11.4 us
    pallas_call x1, Pallas kernels, orthonormalize(): pl.pallas_call(functools.partial(orthonormalize_kernel, 64, 8), out_shape...  10.4 us
    dot_general x1, matrix products, per_device(): jnp.dot(kernel, paired[:, width:], preferred_element_type=jnp.float32)  5.07 us
    ppermute x8, waiting for transfers between devices, gather_z(): ahead = lax.ppermute(ahead, 'z', up)  4.52 us
  transfers between devices with their start and end apart: 18, of which 7 were waited for; matrix products, arithmetic and copies ran while one was open for 1% of the time, Pallas kernels for 0%

profile of v8, /device:TPU:1, one launch (start us, length us, event | category | flops | bytes accessed | tf_op | source)
XLA Modules:
  0.0 180.4 jit_solution(14948254644301849816)
XLA Ops:
  0.0 0.9 pad_maximum_fusion.1
  0.9 2.7 %broadcast_in_dim.9 = bf16[32,32,2304]{2,1,0:T(8,128)(2,1)} broadcast(bf16[32,2304]{1,0:T(8,128)(2,1)S(1)} %pad_maximum_fusion.1), dimensions={1,2} | broadcast | bytes 4866048 | tf_op jit(solution)/shard_map/broadcast_in_dim | solution.py:25
  3.7 11.4 %all-to-all-start = ((bf16[32,32,2304]{2,1,0:T(8,128)(2,1)}), bf16[32,32,2304]{2,1,0:T(8,128)(2,1)}, u32[]{:S(2)}, u32[]{:S(2)}) async-start(bf16[32,32,2304]{2,1,0:T(8,128)(2,1)} %broadcast_in_dim.9), calls=%async_computation | async-start | bytes 9437184 | tf_op jit(solution)/shard_map/all_to_all | solution.py:21
  15.1 1.9 %collective-permute-start.1 = (bf16[32,2048]{1,0:T(8,128)(2,1)S(1)}, bf16[32,2048]{1,0:T(8,128)(2,1)S(1)}, u32[]{:S(2)}, u32[]{:S(2)}) collective-permute-start(bf16[32,2048]{1,0:T(8,128)(2,1)S(1)} %copy-done.1), channel_id=1, source_target_pairs={{0,2},{2,4},{4,6},{6,8},{8,10},{10,12},{12,14},{14,16},{16,18},{18... | collective-permute-start | bytes 393224 | tf_op jit(solution)/shard_map/ppermute | solution.py:45
  17.0 8.5 %collective-permute-start.8 = (bf16[32,2048]{1,0:T(8,128)(2,1)S(1)}, bf16[32,2048]{1,0:T(8,128)(2,1)S(1)}, u32[]{:S(2)}, u32[]{:S(2)}) collective-permute-start(bf16[32,2048]{1,0:T(8,128)(2,1)S(1)} %copy-done.1), channel_id=1, source_target_pairs={{0,30},{2,0},{4,2},{6,4},{8,6},{10,8},{12,10},{14,12},{16,14},{18,... | collective-permute-start | bytes 393224 | tf_op jit(solution)/shard_map/ppermute | solution.py:46
  25.5 0.9 select_bitcast_fusion
  26.4 3.3 %collective-permute-start = (bf16[16,32,512]{2,1,0:T(8,128)(2,1)}, bf16[16,32,512]{2,1,0:T(8,128)(2,1)}, u32[]{:S(2)}, u32[]{:S(2)}) collective-permute-start(bf16[16,32,512]{2,1,0:T(8,128)(2,1)} %select_bitcast_fusion), channel_id=1, source_target_pairs={{0,1},{1,0},{2,3},{3,2},{4,5},{5,4},{6,7},{7,6},{8,9},{9,8},{10,11... | collective-permute-start | bytes 1572872 | tf_op jit(solution)/shard_map/ppermute | solution.py:63
  30.0 1.9 %collective-permute-start.2 = (bf16[32,2048]{1,0:T(8,128)(2,1)S(1)}, bf16[32,2048]{1,0:T(8,128)(2,1)S(1)}, u32[]{:S(2)}, u32[]{:S(2)}) collective-permute-start(bf16[32,2048]{1,0:T(8,128)(2,1)S(1)} %collective-permute-done.1), channel_id=1, source_target_pairs={{0,2},{2,4},{4,6},{6,8},{8,10},{10,12},{12,14},{14,16},{16,18},{18... | collective-permute-start | bytes 393224 | tf_op jit(solution)/shard_map/ppermute | solution.py:45
  31.9 4.6 %collective-permute-start.9 = (bf16[32,2048]{1,0:T(8,128)(2,1)S(1)}, bf16[32,2048]{1,0:T(8,128)(2,1)S(1)}, u32[]{:S(2)}, u32[]{:S(2)}) collective-permute-start(bf16[32,2048]{1,0:T(8,128)(2,1)S(1)} %collective-permute-done.8), channel_id=1, source_target_pairs={{0,30},{2,0},{4,2},{6,4},{8,6},{10,8},{12,10},{14,12},{16,14},{18,... | collective-permute-start | bytes 393224 | tf_op jit(solution)/shard_map/ppermute | solution.py:46
  36.6 0.8 collective-permute-done.2
  37.3 1.9 %collective-permute-start.3 = (bf16[32,2048]{1,0:T(8,128)(2,1)S(1)}, bf16[32,2048]{1,0:T(8,128)(2,1)S(1)}, u32[]{:S(2)}, u32[]{:S(2)}) collective-permute-start(bf16[32,2048]{1,0:T(8,128)(2,1)S(1)} %collective-permute-done.2), channel_id=1, source_target_pairs={{0,2},{2,4},{4,6},{6,8},{8,10},{10,12},{12,14},{14,16},{16,18},{18... | collective-permute-start | bytes 393224 | tf_op jit(solution)/shard_map/ppermute | solution.py:45
  39.2 4.6 %collective-permute-start.10 = (bf16[32,2048]{1,0:T(8,128)(2,1)S(1)}, bf16[32,2048]{1,0:T(8,128)(2,1)S(1)}, u32[]{:S(2)}, u32[]{:S(2)}) collective-permute-start(bf16[32,2048]{1,0:T(8,128)(2,1)S(1)} %collective-permute-done.9), channel_id=1, source_target_pairs={{0,30},{2,0},{4,2},{6,4},{8,6},{10,8},{12,10},{14,12},{16,14},{18,... | collective-permute-start | bytes 393224 | tf_op jit(solution)/shard_map/ppermute | solution.py:46
  43.9 0.8 collective-permute-done.3
  44.6 1.9 %collective-permute-start.4 = (bf16[32,2048]{1,0:T(8,128)(2,1)S(1)}, bf16[32,2048]{1,0:T(8,128)(2,1)S(1)}, u32[]{:S(2)}, u32[]{:S(2)}) collective-permute-start(bf16[32,2048]{1,0:T(8,128)(2,1)S(1)} %collective-permute-done.3), channel_id=1, source_target_pairs={{0,2},{2,4},{4,6},{6,8},{8,10},{10,12},{12,14},{14,16},{16,18},{18... | collective-permute-start | bytes 393224 | tf_op jit(solution)/shard_map/ppermute | solution.py:45
  46.6 4.6 %collective-permute-start.11 = (bf16[32,2048]{1,0:T(8,128)(2,1)S(1)}, bf16[32,2048]{1,0:T(8,128)(2,1)S(1)}, u32[]{:S(2)}, u32[]{:S(2)}) collective-permute-start(bf16[32,2048]{1,0:T(8,128)(2,1)S(1)} %collective-permute-done.10), channel_id=1, source_target_pairs={{0,30},{2,0},{4,2},{6,4},{8,6},{10,8},{12,10},{14,12},{16,14},{18,... | collective-permute-start | bytes 393224 | tf_op jit(solution)/shard_map/ppermute | solution.py:46
  51.2 0.8 collective-permute-done.4
  51.9 1.9 %collective-permute-start.5 = (bf16[32,2048]{1,0:T(8,128)(2,1)S(1)}, bf16[32,2048]{1,0:T(8,128)(2,1)S(1)}, u32[]{:S(2)}, u32[]{:S(2)}) collective-permute-start(bf16[32,2048]{1,0:T(8,128)(2,1)S(1)} %collective-permute-done.4), channel_id=1, source_target_pairs={{0,2},{2,4},{4,6},{6,8},{8,10},{10,12},{12,14},{14,16},{16,18},{18... | collective-permute-start | bytes 393224 | tf_op jit(solution)/shard_map/ppermute | solution.py:45
  53.9 4.6 %collective-permute-start.12 = (bf16[32,2048]{1,0:T(8,128)(2,1)S(1)}, bf16[32,2048]{1,0:T(8,128)(2,1)S(1)}, u32[]{:S(2)}, u32[]{:S(2)}) collective-permute-start(bf16[32,2048]{1,0:T(8,128)(2,1)S(1)} %collective-permute-done.11), channel_id=1, source_target_pairs={{0,30},{2,0},{4,2},{6,4},{8,6},{10,8},{12,10},{14,12},{16,14},{18,... | collective-permute-start | bytes 393224 | tf_op jit(solution)/shard_map/ppermute | solution.py:46
  59.3 1.9 %collective-permute-start.6 = (bf16[32,2048]{1,0:T(8,128)(2,1)S(1)}, bf16[32,2048]{1,0:T(8,128)(2,1)S(1)}, u32[]{:S(2)}, u32[]{:S(2)}) collective-permute-start(bf16[32,2048]{1,0:T(8,128)(2,1)S(1)} %collective-permute-done.5), channel_id=1, source_target_pairs={{0,2},{2,4},{4,6},{6,8},{8,10},{10,12},{12,14},{14,16},{16,18},{18... | collective-permute-start | bytes 393224 | tf_op jit(solution)/shard_map/ppermute | solution.py:45
  61.2 4.6 %collective-permute-start.13 = (bf16[32,2048]{1,0:T(8,128)(2,1)S(1)}, bf16[32,2048]{1,0:T(8,128)(2,1)S(1)}, u32[]{:S(2)}, u32[]{:S(2)}) collective-permute-start(bf16[32,2048]{1,0:T(8,128)(2,1)S(1)} %collective-permute-done.12), channel_id=1, source_target_pairs={{0,30},{2,0},{4,2},{6,4},{8,6},{10,8},{12,10},{14,12},{16,14},{18,... | collective-permute-start | bytes 393224 | tf_op jit(solution)/shard_map/ppermute | solution.py:46
  66.6 1.9 %collective-permute-start.7 = (bf16[32,2048]{1,0:T(8,128)(2,1)S(1)}, bf16[32,2048]{1,0:T(8,128)(2,1)S(1)}, u32[]{:S(2)}, u32[]{:S(2)}) collective-permute-start(bf16[32,2048]{1,0:T(8,128)(2,1)S(1)} %collective-permute-done.6), channel_id=1, source_target_pairs={{0,2},{2,4},{4,6},{6,8},{8,10},{10,12},{12,14},{14,16},{16,18},{18... | collective-permute-start | bytes 393224 | tf_op jit(solution)/shard_map/ppermute | solution.py:45
  68.5 4.6 %collective-permute-start.14 = (bf16[32,2048]{1,0:T(8,128)(2,1)S(1)}, bf16[32,2048]{1,0:T(8,128)(2,1)S(1)}, u32[]{:S(2)}, u32[]{:S(2)}) collective-permute-start(bf16[32,2048]{1,0:T(8,128)(2,1)S(1)} %collective-permute-done.13), channel_id=1, source_target_pairs={{0,30},{2,0},{4,2},{6,4},{8,6},{10,8},{12,10},{14,12},{16,14},{18,... | collective-permute-start | bytes 393224 | tf_op jit(solution)/shard_map/ppermute | solution.py:46
  73.9 1.9 %collective-permute-start.16 = (bf16[16,2048]{1,0:T(8,128)(2,1)S(1)}, bf16[16,2048]{1,0:T(8,128)(2,1)S(1)}, u32[]{:S(2)}, u32[]{:S(2)}) collective-permute-start(bf16[16,2048]{1,0:T(8,128)(2,1)S(1)} %slice.27), channel_id=1, source_target_pairs={{0,2},{2,4},{4,6},{6,8},{8,10},{10,12},{12,14},{14,16},{16,18},{18... | collective-permute-start | bytes 196616 | tf_op jit(solution)/shard_map/ppermute | solution.py:45
  75.8 4.6 %collective-permute-start.15 = (bf16[16,2048]{1,0:T(8,128)(2,1)S(1)}, bf16[16,2048]{1,0:T(8,128)(2,1)S(1)}, u32[]{:S(2)}, u32[]{:S(2)}) collective-permute-start(bf16[16,2048]{1,0:T(8,128)(2,1)S(1)} %slice.26), channel_id=1, source_target_pairs={{0,30},{2,0},{4,2},{6,4},{8,6},{10,8},{12,10},{14,12},{16,14},{18,... | collective-permute-start | bytes 196616 | tf_op jit(solution)/shard_map/ppermute | solution.py:46
  80.4 3.4 %collective-permute-done = bf16[16,32,512]{2,1,0:T(8,128)(2,1)} collective-permute-done((bf16[16,32,512]{2,1,0:T(8,128)(2,1)}, bf16[16,32,512]{2,1,0:T(8,128)(2,1)}, u32[]{:S(2)}, u32[]{:S(2)}) %collective-permute-start) | collective-permute-done | bytes 524320 | tf_op jit(solution)/shard_map/ppermute | solution.py:63
  83.9 1.1 bitcast_select_fusion.1
  85.2 5.1 %convolution_convert_fusion = bf16[512,256]{1,0:T(8,128)(2,1)S(1)} fusion(bf16[512,1024]{1,0:T(8,128)(2,1)S(1)} %bitcast.42, bf16[512,2048]{1,0:T(8,128)(2,1)S(1)} %constant_dynamic-update-slice_fusion, bf16[1024,2304]{1,0:T(8,128)(2,1)} %bitcast.4), kind=kOutput, calls=%fused_computation.4 | convolution fusion | flops 2417623040 | bytes 8126464 | tf_op jit(solution)/shard_map/dot_general | solution.py:179
  90.3 24.7 %all_to_all.25 = bf16[16,32,256]{2,1,0:T(8,128)(2,1)S(1)} all-to-all(bf16[16,32,256]{2,1,0:T(8,128)(2,1)S(1)} %bitcast.44), channel_id=1, replica_groups=mesh['x_hi'=2,'y'=4,'core'=2,'z'=16,'x_lo'=2] {'z'}, dimensions={0} | all-to-all | bytes 524288 | tf_op jit(solution)/shard_map/all_to_all | solution.py:21
  115.5 21.5 %all_to_all.26 = f32[32,8,256]{2,1,0:T(8,128)S(1)} all-to-all(f32[32,8,256]{2,1,0:T(8,128)S(1)} %fusion.8), channel_id=1, replica_groups=mesh['x_hi'=2,'y'=4,'core'=2,'z'=16,'x_lo'=2] {'x_lo','x_hi','y','core'}, dimensions={0} | all-to-all | bytes 524288 | tf_op jit(solution)/shard_map/all_to_all | solution.py:21
  137.0 17.2 %all_to_all.27 = f32[16,8,256]{2,1,0:T(8,128)S(1)} all-to-all(f32[16,8,256]{2,1,0:T(8,128)S(1)} %broadcast_in_dim.10), channel_id=1, replica_groups=mesh['x_hi'=2,'y'=4,'core'=2,'z'=16,'x_lo'=2] {'z'}, dimensions={0} | all-to-all | bytes 262144 | tf_op jit(solution)/shard_map/all_to_all | solution.py:21
  154.3 15.7 %all_to_all.28 = f32[32,8,256]{2,1,0:T(8,128)} all-to-all(f32[32,8,256]{2,1,0:T(8,128)S(1)} %broadcast_in_dim.11), channel_id=1, replica_groups=mesh['x_hi'=2,'y'=4,'core'=2,'z'=16,'x_lo'=2] {'x_lo','x_hi','y','core'}, dimensions={0} | all-to-all | bytes 524288 | tf_op jit(solution)/shard_map/all_to_all | solution.py:21
  170.0 10.4 %shard_map.37 = f32[32,256]{1,0:T(8,128)} custom-call(f32[256,256]{1,0:T(8,128)} %bitcast.41, f32[32,256]{1,0:T(8,128)} %copy-done.2), custom_call_target="tpu_custom_call" | custom-call | tf_op jit(solution)/shard_map/pallas_call | solution.py:156
  (48 shorter events, 3.5 us)
Async XLA Ops:
  3.7 11.4 %copy-start.1 = (bf16[32,2048]{1,0:T(8,128)(2,1)S(1)}, bf16[32,2048]{1,0:T(8,128)(2,1)}, u32[]{:S(2)}) copy-start(bf16[32,2048]{1,0:T(8,128)(2,1)} %param.3) | copy-start | bytes 393220
  3.7 21.8 %copy-start = (bf16[1024,512]{1,0:T(8,128)(2,1)S(1)}, bf16[1024,512]{1,0:T(8,128)(2,1)}, u32[]{:S(2)}) copy-start(bf16[1024,512]{1,0:T(8,128)(2,1)} %param.4) | copy-start | bytes 3145732
  3.7 81.6 %all-to-all-start = ((bf16[32,32,2304]{2,1,0:T(8,128)(2,1)}), bf16[32,32,2304]{2,1,0:T(8,128)(2,1)}, u32[]{:S(2)}, u32[]{:S(2)}) async-start(bf16[32,32,2304]{2,1,0:T(8,128)(2,1)} %broadcast_in_dim.9), calls=%async_computation | async-start | bytes 9437184 | tf_op jit(solution)/shard_map/all_to_all | solution.py:21
  15.1 14.9 %collective-permute-start.1 = (bf16[32,2048]{1,0:T(8,128)(2,1)S(1)}, bf16[32,2048]{1,0:T(8,128)(2,1)S(1)}, u32[]{:S(2)}, u32[]{:S(2)}) collective-permute-start(bf16[32,2048]{1,0:T(8,128)(2,1)S(1)} %copy-done.1), channel_id=1, source_target_pairs={{0,2},{2,4},{4,6},{6,8},{8,10},{10,12},{12,14},{14,16},{16,18},{18... | collective-permute-start | bytes 393224 | tf_op jit(solution)/shard_map/ppermute | solution.py:45
  17.0 14.9 %collective-permute-start.8 = (bf16[32,2048]{1,0:T(8,128)(2,1)S(1)}, bf16[32,2048]{1,0:T(8,128)(2,1)S(1)}, u32[]{:S(2)}, u32[]{:S(2)}) collective-permute-start(bf16[32,2048]{1,0:T(8,128)(2,1)S(1)} %copy-done.1), channel_id=1, source_target_pairs={{0,30},{2,0},{4,2},{6,4},{8,6},{10,8},{12,10},{14,12},{16,14},{18,... | collective-permute-start | bytes 393224 | tf_op jit(solution)/shard_map/ppermute | solution.py:46
  26.4 57.5 %collective-permute-start = (bf16[16,32,512]{2,1,0:T(8,128)(2,1)}, bf16[16,32,512]{2,1,0:T(8,128)(2,1)}, u32[]{:S(2)}, u32[]{:S(2)}) collective-permute-start(bf16[16,32,512]{2,1,0:T(8,128)(2,1)} %select_bitcast_fusion), channel_id=1, source_target_pairs={{0,1},{1,0},{2,3},{3,2},{4,5},{5,4},{6,7},{7,6},{8,9},{9,8},{10,11... | collective-permute-start | bytes 1572872 | tf_op jit(solution)/shard_map/ppermute | solution.py:63
  30.0 7.3 %collective-permute-start.2 = (bf16[32,2048]{1,0:T(8,128)(2,1)S(1)}, bf16[32,2048]{1,0:T(8,128)(2,1)S(1)}, u32[]{:S(2)}, u32[]{:S(2)}) collective-permute-start(bf16[32,2048]{1,0:T(8,128)(2,1)S(1)} %collective-permute-done.1), channel_id=1, source_target_pairs={{0,2},{2,4},{4,6},{6,8},{8,10},{10,12},{12,14},{14,16},{16,18},{18... | collective-permute-start | bytes 393224 | tf_op jit(solution)/shard_map/ppermute | solution.py:45
  31.9 7.3 %collective-permute-start.9 = (bf16[32,2048]{1,0:T(8,128)(2,1)S(1)}, bf16[32,2048]{1,0:T(8,128)(2,1)S(1)}, u32[]{:S(2)}, u32[]{:S(2)}) collective-permute-start(bf16[32,2048]{1,0:T(8,128)(2,1)S(1)} %collective-permute-done.8), channel_id=1, source_target_pairs={{0,30},{2,0},{4,2},{6,4},{8,6},{10,8},{12,10},{14,12},{16,14},{18,... | collective-permute-start | bytes 393224 | tf_op jit(solution)/shard_map/ppermute | solution.py:46
  37.3 7.3 %collective-permute-start.3 = (bf16[32,2048]{1,0:T(8,128)(2,1)S(1)}, bf16[32,2048]{1,0:T(8,128)(2,1)S(1)}, u32[]{:S(2)}, u32[]{:S(2)}) collective-permute-start(bf16[32,2048]{1,0:T(8,128)(2,1)S(1)} %collective-permute-done.2), channel_id=1, source_target_pairs={{0,2},{2,4},{4,6},{6,8},{8,10},{10,12},{12,14},{14,16},{16,18},{18... | collective-permute-start | bytes 393224 | tf_op jit(solution)/shard_map/ppermute | solution.py:45
  39.2 7.3 %collective-permute-start.10 = (bf16[32,2048]{1,0:T(8,128)(2,1)S(1)}, bf16[32,2048]{1,0:T(8,128)(2,1)S(1)}, u32[]{:S(2)}, u32[]{:S(2)}) collective-permute-start(bf16[32,2048]{1,0:T(8,128)(2,1)S(1)} %collective-permute-done.9), channel_id=1, source_target_pairs={{0,30},{2,0},{4,2},{6,4},{8,6},{10,8},{12,10},{14,12},{16,14},{18,... | collective-permute-start | bytes 393224 | tf_op jit(solution)/shard_map/ppermute | solution.py:46
  44.6 7.3 %collective-permute-start.4 = (bf16[32,2048]{1,0:T(8,128)(2,1)S(1)}, bf16[32,2048]{1,0:T(8,128)(2,1)S(1)}, u32[]{:S(2)}, u32[]{:S(2)}) collective-permute-start(bf16[32,2048]{1,0:T(8,128)(2,1)S(1)} %collective-permute-done.3), channel_id=1, source_target_pairs={{0,2},{2,4},{4,6},{6,8},{8,10},{10,12},{12,14},{14,16},{16,18},{18... | collective-permute-start | bytes 393224 | tf_op jit(solution)/shard_map/ppermute | solution.py:45
  46.6 7.3 %collective-permute-start.11 = (bf16[32,2048]{1,0:T(8,128)(2,1)S(1)}, bf16[32,2048]{1,0:T(8,128)(2,1)S(1)}, u32[]{:S(2)}, u32[]{:S(2)}) collective-permute-start(bf16[32,2048]{1,0:T(8,128)(2,1)S(1)} %collective-permute-done.10), channel_id=1, source_target_pairs={{0,30},{2,0},{4,2},{6,4},{8,6},{10,8},{12,10},{14,12},{16,14},{18,... | collective-permute-start | bytes 393224 | tf_op jit(solution)/shard_map/ppermute | solution.py:46
  51.9 7.3 %collective-permute-start.5 = (bf16[32,2048]{1,0:T(8,128)(2,1)S(1)}, bf16[32,2048]{1,0:T(8,128)(2,1)S(1)}, u32[]{:S(2)}, u32[]{:S(2)}) collective-permute-start(bf16[32,2048]{1,0:T(8,128)(2,1)S(1)} %collective-permute-done.4), channel_id=1, source_target_pairs={{0,2},{2,4},{4,6},{6,8},{8,10},{10,12},{12,14},{14,16},{16,18},{18... | collective-permute-start | bytes 393224 | tf_op jit(solution)/shard_map/ppermute | solution.py:45
  53.9 7.3 %collective-permute-start.12 = (bf16[32,2048]{1,0:T(8,128)(2,1)S(1)}, bf16[32,2048]{1,0:T(8,128)(2,1)S(1)}, u32[]{:S(2)}, u32[]{:S(2)}) collective-permute-start(bf16[32,2048]{1,0:T(8,128)(2,1)S(1)} %collective-permute-done.11), channel_id=1, source_target_pairs={{0,30},{2,0},{4,2},{6,4},{8,6},{10,8},{12,10},{14,12},{16,14},{18,... | collective-permute-start | bytes 393224 | tf_op jit(solution)/shard_map/ppermute | solution.py:46
  59.3 7.3 %collective-permute-start.6 = (bf16[32,2048]{1,0:T(8,128)(2,1)S(1)}, bf16[32,2048]{1,0:T(8,128)(2,1)S(1)}, u32[]{:S(2)}, u32[]{:S(2)}) collective-permute-start(bf16[32,2048]{1,0:T(8,128)(2,1)S(1)} %collective-permute-done.5), channel_id=1, source_target_pairs={{0,2},{2,4},{4,6},{6,8},{8,10},{10,12},{12,14},{14,16},{16,18},{18... | collective-permute-start | bytes 393224 | tf_op jit(solution)/shard_map/ppermute | solution.py:45
  61.2 7.3 %collective-permute-start.13 = (bf16[32,2048]{1,0:T(8,128)(2,1)S(1)}, bf16[32,2048]{1,0:T(8,128)(2,1)S(1)}, u32[]{:S(2)}, u32[]{:S(2)}) collective-permute-start(bf16[32,2048]{1,0:T(8,128)(2,1)S(1)} %collective-permute-done.12), channel_id=1, source_target_pairs={{0,30},{2,0},{4,2},{6,4},{8,6},{10,8},{12,10},{14,12},{16,14},{18,... | collective-permute-start | bytes 393224 | tf_op jit(solution)/shard_map/ppermute | solution.py:46
  66.6 7.3 %collective-permute-start.7 = (bf16[32,2048]{1,0:T(8,128)(2,1)S(1)}, bf16[32,2048]{1,0:T(8,128)(2,1)S(1)}, u32[]{:S(2)}, u32[]{:S(2)}) collective-permute-start(bf16[32,2048]{1,0:T(8,128)(2,1)S(1)} %collective-permute-done.6), channel_id=1, source_target_pairs={{0,2},{2,4},{4,6},{6,8},{8,10},{10,12},{12,14},{14,16},{16,18},{18... | collective-permute-start | bytes 393224 | tf_op jit(solution)/shard_map/ppermute | solution.py:45
  68.5 7.3 %collective-permute-start.14 = (bf16[32,2048]{1,0:T(8,128)(2,1)S(1)}, bf16[32,2048]{1,0:T(8,128)(2,1)S(1)}, u32[]{:S(2)}, u32[]{:S(2)}) collective-permute-start(bf16[32,2048]{1,0:T(8,128)(2,1)S(1)} %collective-permute-done.13), channel_id=1, source_target_pairs={{0,30},{2,0},{4,2},{6,4},{8,6},{10,8},{12,10},{14,12},{16,14},{18,... | collective-permute-start | bytes 393224 | tf_op jit(solution)/shard_map/ppermute | solution.py:46
  73.9 11.3 %collective-permute-start.16 = (bf16[16,2048]{1,0:T(8,128)(2,1)S(1)}, bf16[16,2048]{1,0:T(8,128)(2,1)S(1)}, u32[]{:S(2)}, u32[]{:S(2)}) collective-permute-start(bf16[16,2048]{1,0:T(8,128)(2,1)S(1)} %slice.27), channel_id=1, source_target_pairs={{0,2},{2,4},{4,6},{6,8},{8,10},{10,12},{12,14},{14,16},{16,18},{18... | collective-permute-start | bytes 196616 | tf_op jit(solution)/shard_map/ppermute | solution.py:45
  75.8 9.3 %collective-permute-start.15 = (bf16[16,2048]{1,0:T(8,128)(2,1)S(1)}, bf16[16,2048]{1,0:T(8,128)(2,1)S(1)}, u32[]{:S(2)}, u32[]{:S(2)}) collective-permute-start(bf16[16,2048]{1,0:T(8,128)(2,1)S(1)} %slice.26), channel_id=1, source_target_pairs={{0,30},{2,0},{4,2},{6,4},{8,6},{10,8},{12,10},{14,12},{16,14},{18,... | collective-permute-start | bytes 196616 | tf_op jit(solution)/shard_map/ppermute | solution.py:46
  115.0 55.0 %copy-start.2 = (f32[32,256]{1,0:T(8,128)}, f32[32,256]{1,0:T(8,128)S(1)}, u32[]{:S(2)}) copy-start(f32[32,256]{1,0:T(8,128)S(1)} %convert_reduce_fusion.images_ref) | copy-start | bytes 98308
